TPU v7x, 32 devices: a whole 2x2x4 slice. The times are simulated.
32 devices in a mesh: blk: 8 (over z, y), sub: 4 (over x, core).
Axes of the slice: x: 2, y: 2, z: 4, core: 2. Of those that a mesh axis runs over, the one named last changes fastest.
Arguments:
- pressure: float32 [2, 8, 8, 8, 16384], P(None, None, None, None, ('blk', 'sub')), may hold values from -6 to 6
- right_side: float32 [2, 8, 8, 8, 16384], P(None, None, None, None, ('blk', 'sub')), may hold values from -6 to 6
- geometry: float32 [6, 8, 8, 8, 16384], P(None, None, None, None, ('blk', 'sub')), may hold values from -0.03 to 0.08, as said below
- face_weight: float32 [64, 6, 16384], P(None, None, ('blk', 'sub')), may hold values from 0.004 to 0.02
- face_metric: float32 [64, 6, 16384], P(None, None, ('blk', 'sub')), may hold values from 0.5 to 2
- cross_slots: int32 [5, 32, 576], P(None, ('blk', 'sub')), may hold values from 0 to 511, as said below
- local_pairs: int32 [5, 16384], P(None, ('blk', 'sub')), may hold values from 0 to 511, as said below
- coarse_map: int32 [16384], P(('blk', 'sub')), may hold values from 0 to 255, as said below
- coarse_inverse: float32 [8, 8, 2048], P(None, None, 'blk'), may hold values from -0.12 to 0.48, as said below
Outputs:
- residual: float32 [2, 8, 8, 8, 16384], P(None, None, None, None, ('blk', 'sub'))
- corrected: float32 [2, 8, 8, 8, 16384], P(None, None, None, None, ('blk', 'sub'))
Inputs may be any that keep to these rules, and one draw needn't show every extreme that they name: `cross_slots`: Rows: local element index, face 0 to 5 (low or high end of node axis 1, 2, 3), live flag, owner flag, orientation code 0 to 7. Columns come in 9 blocks of 64, block k for neighbour k of the device grid; block 4 (the device itself) has no live slot. The slot of device d at neighbour k, place c and the slot of neighbour k at column (8 - k) * 64 + c describe the same pair: equal live flags and codes, opposite owner flags. Within a block the live slots come first; every device shares exactly 64 pairs with some neighbour. Every (element, face) of a device appears at most once among its slots, live or not, and its local pairs. `local_pairs`: the columns of device d hold 512 pairs of its own elements; see cross_slots for the faces used. `coarse_map`: each coarse cell of a Morton block holds exactly 8 elements of that block. `geometry`: at each node the 3 x 3 matrix of the six rows is symmetric positive definite. `coarse_inverse`: each block is symmetric.
All inputs are finite; a program needn't handle non-finite values.
Results may differ from a plain program's by a relative error of at most 0.00016.
Values sent between devices are 32-bit elements; how exact they have to be, the bound alone decides.
No kernel may reach another device: no remote copies, remote signals or barrier semaphores. Data moves between devices by JAX's collectives and lax.ppermute only.
A program may use at most 128 MiB of HBM per device.

v0:
```python
import jax
import jax.numpy as jnp
import numpy as np
from jax import lax
from jax.sharding import PartitionSpec as P

precise = lax.Precision.HIGHEST


def extended(cells, sides, width):
    for axis, dim in sides:
        count = lax.axis_size(axis)
        head = lax.slice_in_dim(cells, 0, width, axis=dim)
        tail = lax.slice_in_dim(cells, cells.shape[dim] - width, cells.shape[dim], axis=dim)
        cells = jnp.concatenate(
            [
                lax.ppermute(tail, axis, [(i, (i + 1) % count) for i in range(count)]),
                cells,
                lax.ppermute(head, axis, [((i + 1) % count, i) for i in range(count)]),
            ],
            axis=dim,
        )
    return cells


def node_points():
    positive = [0.2092992179024789, 0.5917001814331423, 0.8717401485096066, 1.0]
    return np.array(sorted([-entry_value for entry_value in positive] + positive))


def derivative_matrix(node_count):
    points = node_points()
    weights = np.array(
        [
            1.0
            / np.prod(
                [
                    points[row_index] - points[col_index]
                    for col_index in range(node_count)
                    if col_index != row_index
                ]
            )
            for row_index in range(node_count)
        ]
    )
    matrix = np.zeros((node_count, node_count))
    for row_index in range(node_count):
        for col_index in range(node_count):
            if row_index != col_index:
                matrix[row_index, col_index] = (
                    weights[col_index]
                    / weights[row_index]
                    / (points[row_index] - points[col_index])
                )
        matrix[row_index, row_index] = -np.sum(matrix[row_index])
    return matrix


def edge_matrix(node_count):
    derivative = derivative_matrix(node_count)
    edge_rows = np.zeros((4, node_count))
    edge_rows[0, 0] = 1.0
    edge_rows[1] = -derivative[0]
    edge_rows[2, node_count - 1] = 1.0
    edge_rows[3] = derivative[node_count - 1]
    return edge_rows


def prolong_matrix():
    points = node_points()
    return np.stack([(1.0 - points) / 2.0, (1.0 + points) / 2.0], axis=1)


def orient_tables(node_count):
    forward = np.zeros((8, node_count * node_count), np.int32)
    for orient_code in range(8):
        for first_axis in range(node_count):
            for second_axis in range(node_count):
                if orient_code & 4:
                    source_one, source_two = (second_axis, first_axis)
                else:
                    source_one, source_two = (first_axis, second_axis)
                if orient_code & 1:
                    source_one = node_count - 1 - source_one
                if orient_code & 2:
                    source_two = node_count - 1 - source_two
                forward[orient_code, first_axis * node_count + second_axis] = (
                    source_one * node_count + source_two
                )
    inverse = np.argsort(forward, axis=1).astype(np.int32)
    return (forward, inverse)


def perm_matrices(table):
    face_size = table.shape[1]
    identity = np.eye(face_size, dtype=np.float32)
    return jnp.asarray(identity[table].reshape(8 * face_size, face_size), jnp.float32)


def reorient(traces, orient_codes, perm_tables):
    shape_all = traces.shape
    face_size = shape_all[-2]
    slot_total = shape_all[-1]
    flattened = traces.reshape(-1, face_size, slot_total)
    groups = flattened.shape[0]
    tiled = jnp.broadcast_to(perm_tables, (groups,) + perm_tables.shape)
    product = lax.dot_general(tiled, flattened, (((2,), (1,)), ((0,), (0,))), precision=precise)
    product = product.reshape(groups, 8, face_size, slot_total)
    code_mask = (orient_codes[None, :] == jnp.arange(8, dtype=jnp.int32)[:, None]).astype(
        jnp.float32
    )
    return jnp.sum(product * code_mask[None, :, None, :], axis=1).reshape(shape_all)


def face_flux(first_side, second_side, orient_codes, node_count):
    forward, inverse = orient_tables(node_count)
    forward_perm = perm_matrices(forward)
    inverse_perm = perm_matrices(inverse)
    first_value, first_slope, first_weight, first_metric = first_side
    second_value = reorient(second_side[0], orient_codes, forward_perm)
    second_slope = reorient(second_side[1], orient_codes, forward_perm)
    second_weight = reorient(second_side[2], orient_codes, forward_perm)
    second_metric = reorient(second_side[3], orient_codes, forward_perm)
    penalty = node_count * (node_count + 1) / 2.0
    jump_value = first_value - second_value
    weight = 0.5 * (first_weight + second_weight)
    penalty_term = penalty * 0.5 * (first_metric + second_metric)
    normal_term = weight * (penalty_term * jump_value - 0.5 * (first_slope - second_slope))
    symmetric_term = -0.5 * weight * jump_value
    return (
        normal_term,
        symmetric_term * first_metric,
        -reorient(normal_term, orient_codes, inverse_perm),
        -reorient(symmetric_term, orient_codes, inverse_perm) * second_side[3],
    )


def apply_along(small_table, operand, axis):
    shape_all = operand.shape
    before = int(np.prod(shape_all[:axis]))
    shaped = operand.reshape(before, shape_all[axis], -1)
    tiled = jnp.broadcast_to(small_table, (before,) + small_table.shape)
    product = lax.dot_general(tiled, shaped, (((2,), (1,)), ((0,), (0,))), precision=precise)
    return product.reshape(shape_all[:axis] + (small_table.shape[0],) + shape_all[axis + 1 :])


def volume_term(fields, geometry, derivative):
    slope_first = apply_along(derivative, fields, 1)
    slope_second = apply_along(derivative, fields, 2)
    slope_third = apply_along(derivative, fields, 3)
    flux_first = geometry[0] * slope_first + geometry[3] * slope_second + geometry[4] * slope_third
    flux_second = geometry[3] * slope_first + geometry[1] * slope_second + geometry[5] * slope_third
    flux_third = geometry[4] * slope_first + geometry[5] * slope_second + geometry[2] * slope_third
    transposed = derivative.T
    result = apply_along(transposed, flux_first, 1)
    result = result + apply_along(transposed, flux_second, 2)
    return result + apply_along(transposed, flux_third, 3)


def edge_values(fields, edge_np, axis):
    slices = [
        lax.index_in_dim(fields, node_index, axis, keepdims=False)
        for node_index in range(fields.shape[axis])
    ]
    collected = []
    for row_index in range(4):
        running = 0.0
        for node_index, layer_slice in enumerate(slices):
            factor = float(edge_np[row_index, node_index])
            if factor != 0.0:
                running = running + factor * layer_slice
        collected.append(running)
    return collected


def face_tables(fields, face_metric, edge_np):
    field_count = fields.shape[0]
    elem_count = fields.shape[-1]
    face_size = fields.shape[1] * fields.shape[1]
    values = []
    slopes = []
    for axis_number in range(3):
        collected = edge_values(fields, edge_np, 1 + axis_number)
        shaped = [entry.reshape(field_count, face_size, elem_count) for entry in collected]
        values += [shaped[0], shaped[2]]
        slopes += [shaped[1], shaped[3]]
    value_all = jnp.stack(values, axis=2)
    slope_all = jnp.stack(slopes, axis=2) * face_metric
    return (
        value_all.reshape(field_count * face_size, 6 * elem_count),
        slope_all.reshape(field_count * face_size, 6 * elem_count),
    )


def lift_faces(value_grid, lift_grid, edge_np, node_count):
    field_count = value_grid.shape[0]
    elem_count = value_grid.shape[-1]
    result = 0.0
    for axis_number in range(3):
        face_rows = [
            value_grid[:, :, 2 * axis_number],
            lift_grid[:, :, 2 * axis_number],
            value_grid[:, :, 2 * axis_number + 1],
            lift_grid[:, :, 2 * axis_number + 1],
        ]
        face_rows = [
            entry.reshape(field_count, node_count, node_count, elem_count) for entry in face_rows
        ]
        node_terms = []
        for node_index in range(node_count):
            running = 0.0
            for row_index in range(4):
                factor = float(edge_np[row_index, node_index])
                if factor != 0.0:
                    running = running + factor * face_rows[row_index]
            node_terms.append(running)
        result = result + jnp.stack(node_terms, axis=1 + axis_number)
    return result


def on_device(
    pressure,
    right_side,
    geometry,
    face_weight,
    face_metric,
    cross_slots,
    local_pairs,
    coarse_map,
    coarse_inverse,
):
    node_count = pressure.shape[1]
    elem_count = pressure.shape[-1]
    face_size = node_count * node_count
    derivative = jnp.asarray(derivative_matrix(node_count), jnp.float32)
    edge_np = edge_matrix(node_count)
    slot_table = cross_slots[:, 0, :]
    slot_total = slot_table.shape[1]
    cross_index = slot_table[1] * elem_count + slot_table[0]
    live_mask = slot_table[2].astype(jnp.float32)
    owned_mask = slot_table[3].astype(jnp.float32)
    orient_codes = slot_table[4]
    local_first = local_pairs[1] * elem_count + local_pairs[0]
    local_second = local_pairs[3] * elem_count + local_pairs[2]
    all_index = jnp.concatenate([cross_index, local_first, local_second])
    selector = (jnp.arange(6 * elem_count, dtype=jnp.int32)[:, None] == all_index[None, :]).astype(
        jnp.float32
    )
    weight_flat = face_weight.reshape(face_size, 6 * elem_count)
    metric_flat = face_metric.reshape(face_size, 6 * elem_count)

    def split_rows(matrix, field_count):
        field_rows = field_count * face_size
        columns = matrix.shape[1]
        return (
            matrix[0:field_rows].reshape(field_count, face_size, columns),
            matrix[field_rows : 2 * field_rows].reshape(field_count, face_size, columns),
            matrix[2 * field_rows : 2 * field_rows + face_size],
            matrix[2 * field_rows + face_size : 2 * field_rows + 2 * face_size],
        )

    def apply_operator(fields):
        field_count = fields.shape[0]
        field_rows = field_count * face_size
        volume = volume_term(fields, geometry, derivative)
        value_rows, slope_rows = face_tables(fields, face_metric, edge_np)
        table_all = jnp.concatenate([value_rows, slope_rows, weight_flat, metric_flat], axis=0)
        picked = jnp.dot(table_all, selector, precision=precise)
        own_block = picked[:, 0:slot_total]
        row_total = own_block.shape[0]
        padded = extended(
            own_block.reshape(row_total, 3, 3, slot_total // 9), (("blk", 1), ("sub", 2)), 1
        )
        received = padded[:, 0::2, 0::2].reshape(row_total, slot_total)
        own_traces = split_rows(own_block, field_count)
        peer_traces = split_rows(received, field_count)
        chosen = owned_mask > 0.5
        first_side = tuple(
            (
                jnp.where(chosen, own_piece, peer_piece)
                for own_piece, peer_piece in zip(own_traces, peer_traces)
            )
        )
        second_side = tuple(
            (
                jnp.where(chosen, peer_piece, own_piece)
                for own_piece, peer_piece in zip(own_traces, peer_traces)
            )
        )
        first_value, first_lift, second_value, second_lift = face_flux(
            first_side, second_side, orient_codes, node_count
        )
        cross_value = jnp.where(chosen, first_value, second_value) * live_mask
        cross_lift = jnp.where(chosen, first_lift, second_lift) * live_mask
        first_local = split_rows(picked[:, slot_total : slot_total + elem_count], field_count)
        second_local = split_rows(picked[:, slot_total + elem_count :], field_count)
        local_value_one, local_lift_one, local_value_two, local_lift_two = face_flux(
            first_local, second_local, local_pairs[4], node_count
        )
        value_cols = jnp.concatenate([cross_value, local_value_one, local_value_two], axis=2)
        lift_cols = jnp.concatenate([cross_lift, local_lift_one, local_lift_two], axis=2)
        column_total = value_cols.shape[2]
        contrib = jnp.concatenate(
            [
                value_cols.reshape(field_rows, column_total),
                lift_cols.reshape(field_rows, column_total),
            ],
            axis=0,
        )
        deposited = lax.dot_general(contrib, selector, (((1,), (1,)), ((), ())), precision=precise)
        value_grid = deposited[0:field_rows].reshape(field_count, face_size, 6, elem_count)
        lift_grid = deposited[field_rows : 2 * field_rows].reshape(
            field_count, face_size, 6, elem_count
        )
        return volume + lift_faces(value_grid, lift_grid, edge_np, node_count)

    operated = jnp.concatenate(
        [apply_operator(pressure[0:1]), apply_operator(pressure[1:2])], axis=0
    )
    residual = right_side - operated
    prolong = jnp.asarray(prolong_matrix(), jnp.float32)
    prolong_rows = prolong.T
    field_total = residual.shape[0]
    restricted = apply_along(prolong_rows, residual, 1)
    restricted = apply_along(prolong_rows, restricted, 2)
    restricted = apply_along(prolong_rows, restricted, 3).reshape(field_total, 8, elem_count)
    row_cells = coarse_inverse.shape[-1]
    one_hot = (coarse_map[:, None] == jnp.arange(row_cells, dtype=jnp.int32)[None, :]).astype(
        jnp.float32
    )
    cell_sums = jnp.einsum("fae,ec->fac", restricted, one_hot, precision=precise)
    totals = lax.psum(cell_sums, "sub")
    correction = jnp.einsum("ijc,fjc->fic", coarse_inverse, totals, precision=precise)
    spread = lax.dot_general(correction, one_hot, (((2,), (1,)), ((), ())), precision=precise)
    spread = spread.reshape(field_total, 2, 2, 2, elem_count)
    grown = apply_along(prolong, spread, 1)
    grown = apply_along(prolong, grown, 2)
    grown = apply_along(prolong, grown, 3)
    corrected = pressure + grown
    return (residual, corrected)


def solution(mesh):
    return jax.shard_map(
        on_device,
        mesh=mesh,
        in_specs=(
            P(None, None, None, None, ("blk", "sub")),
            P(None, None, None, None, ("blk", "sub")),
            P(None, None, None, None, ("blk", "sub")),
            P(None, None, ("blk", "sub")),
            P(None, None, ("blk", "sub")),
            P(None, ("blk", "sub"), None),
            P(None, ("blk", "sub")),
            P(("blk", "sub")),
            P(None, None, "blk"),
        ),
        out_specs=(
            P(None, None, None, None, ("blk", "sub")),
            P(None, None, None, None, ("blk", "sub")),
        ),
        check_vma=False,
    )
```

profile of v0, /device:TPU:0, one launch (start us, length us, event | category | flops | bytes accessed | tf_op | source)
XLA Modules:
  0.0 446.1 jit_solution(12132688431828383891)
XLA Ops:
  2.0 9.3 %fusion.165 = (f32[1,8,8,1,512]{4,3,2,1,0:T(1,128)S(1)}, f32[1,8,8,1,512]{4,3,2,1,0:T(1,128)S(1)}, f32[1,8,8,1,512]{4,3,2,1,0:T(1,128)S(1)}, f32[1,8,8,1,512]{4,...) fusion(f32[2,8,8,8,512]{4,3,2,1,0:T(8,128)} %param.19), kind=kLoop, calls=%fused_computation.399 | loop fusion | bytes 4194304 | tf_op jit(solution)/shard_map/slice | solution.py:162
  27.8 18.2 %fusion.3 = f32[256,1600]{0,1:T(8,128)S(1)} fusion(s32[1600]{0:T(1024)S(1)} %concatenate.51, f32[64,3072]{1,0:T(8,128)} %bitcast.505, f32[64,3072]{1,0:T(8,128)} %bitcast.507, f32[64,3072]{1,0:T(8,128)} %bitcast.509, f32[64,3072]{1,0:T(8,128)} %bitcast.502), kind=kOutput, calls=%fused_computation.4 | convolution fusion | flops 15106768896 | bytes 4790528 | tf_op jit(solution)/shard_map/dot_general | solution.py:268
  46.8 6.0 %collective-permute-start.1 = (f32[256,1,3,64]{0,3,2,1:T(8,128)}, f32[256,1,3,64]{0,3,2,1:T(8,128)}, u32[]{:S(2)}, u32[]{:S(2)}) collective-permute-start(f32[256,1,3,64]{0,3,2,1:T(8,128)} %get-tuple-element.149), channel_id=1, source_target_pairs={{4,0},{8,4},{12,8},{16,12},{20,16},{24,20},{28,24},{0,28},{5,1},{9... | collective-permute-start | bytes 589832 | tf_op jit(solution)/shard_map/ppermute | solution.py:19
  61.0 17.9 %fusion.1 = f32[256,1600]{0,1:T(8,128)S(1)} fusion(s32[1600]{0:T(1024)S(1)} %concatenate.51, f32[64,3072]{1,0:T(8,128)S(1)} %bitcast.506, f32[64,3072]{1,0:T(8,128)S(1)} %bitcast.508, f32[64,3072]{1,0:T(8,128)} %bitcast.510, f32[64,3072]{1,0:T(8,128)S(1)} %bitcast.503), kind=kOutput, calls=%fused_computation.2 | convolution fusion | flops 15106768896 | bytes 4790528 | tf_op jit(solution)/shard_map/dot_general | solution.py:268
  79.9 4.7 %collective-permute-start.5 = (f32[256,1,3,64]{0,3,2,1:T(8,128)}, f32[256,1,3,64]{0,3,2,1:T(8,128)}, u32[]{:S(2)}, u32[]{:S(2)}) collective-permute-start(f32[256,1,3,64]{0,3,2,1:T(8,128)} %get-tuple-element.155), channel_id=1, source_target_pairs={{4,0},{8,4},{12,8},{16,12},{20,16},{24,20},{28,24},{0,28},{5,1},{9... | collective-permute-start | bytes 589832 | tf_op jit(solution)/shard_map/ppermute | solution.py:19
  112.2 4.7 %fusion.164 = (f32[1,8,8,8,512]{4,3,2,1,0:T(8,128)}, f32[1,8,8,8,512]{4,3,2,1,0:T(8,128)S(1)}, f32[1,8,8,8,512]{4,3,2,1,0:T(8,128)S(1)}, f32[1,8,8,8,512]{4,3,2,...) fusion(f32[6,8,8,8,512]{4,3,2,1,0:T(8,128)} %param.21), kind=kLoop, calls=%fused_computation.398 | loop fusion | bytes 12582912 | tf_op jit(solution)/shard_map/slice | solution.py:151
  125.6 10.1 %multiply_add_fusion.1 = (f32[1,8,8,8,512]{4,1,3,2,0:T(8,128)S(1)}, f32[1,8,8,8,512]{4,1,3,2,0:T(8,128)S(1)}, f32[1,8,8,8,512]{4,1,3,2,0:T(8,128)}, f32[1,8,8,8,512]{4,1,3,2,0:T(8,128)}, f32[1,8,8,8,512]{4,1,3,2,0:T(8,128)}) fusion(f32[1,8,8,8,512]{4,3,2,1,0:T(8,128)S(1)} %get-tuple-element.26, f32[1,8,8,8,512]{4,3,2,1,0:T(8,128)S(1)} %bitcast.476, ...), kind=kOutput, calls=%fused_computation.88 | convolution fusion | flops 30408704 | bytes 16777472 | tf_op jit(solution)/shard_map/dot_general | solution.py:143
  141.5 3.3 fusion.124
  213.3 4.4 collective-permute-done.3
  250.2 3.1 fusion.95
  267.1 3.0 fusion.27
  281.1 3.1 fusion.83
  293.3 3.4 multiply_bitcast_fusion.5
  297.9 11.2 %fusion = f32[128,3072]{1,0:T(8,128)S(1)} fusion(s32[1600]{0:T(1024)S(1)} %copy-done.119, f32[64,1600]{0,1:T(8,128)S(1)} %maximum_bitcast_fusion.3, f32[64,1600]{0,1:T(8,128)S(1)} %maximum_bitcast_fusion.2), kind=kOutput, calls=%fused_computation.1 | convolution fusion | flops 7554867200 | bytes 2398464 | tf_op jit(solution)/shard_map/dot_general | solution.py:310
  312.8 6.7 %multiply_add_fusion.11 = (f32[1,64,1,512]{3,2,1,0:T(1,128)}, f32[1,64,1,512]{3,2,1,0:T(1,128)}, f32[1,64,1,512]{3,2,1,0:T(1,128)}, f32[1,64,1,512]{3,2,1,0:T(1,...) fusion(f32[1,64,6,512]{3,2,1,0:T(8,128)} %reshape.4678), kind=kLoop, calls=%fused_computation.307 | loop fusion | flops 884736 | bytes 1966080 | tf_op jit(solution)/shard_map/add | solution.py:215
  322.3 11.4 %fusion.2 = f32[128,3072]{1,0:T(8,128)S(1)} fusion(s32[1600]{0:T(1024)S(1)} %copy-done.119, f32[64,1600]{0,1:T(8,128)S(1)} %maximum_bitcast_fusion.1, f32[64,1600]{0,1:T(8,128)S(1)} %maximum_bitcast_fusion), kind=kOutput, calls=%fused_computation.3 | convolution fusion | flops 7554867200 | bytes 2398464 | tf_op jit(solution)/shard_map/dot_general | solution.py:310
  337.5 6.7 %multiply_add_fusion.29 = (f32[1,64,1,512]{3,2,1,0:T(1,128)}, f32[1,64,1,512]{3,2,1,0:T(1,128)}, f32[1,64,1,512]{3,2,1,0:T(1,128)}, f32[1,64,1,512]{3,2,1,0:T(1,...) fusion(f32[1,64,6,512]{3,2,1,0:T(8,128)} %reshape.4659), kind=kLoop, calls=%fused_computation.328 | loop fusion | flops 884736 | bytes 1966080 | tf_op jit(solution)/shard_map/add | solution.py:215
  349.3 7.4 %fusion.110 = (f32[1,64,1,512]{3,2,1,0:T(1,128)S(1)}, f32[1,64,1,512]{3,2,1,0:T(1,128)S(1)}, f32[1,64,1,512]{3,2,1,0:T(1,128)S(1)}, f32[1,64,1,512]{3,2,1,0:T(1,...) fusion(f32[1,64,6,512]{3,2,1,0:T(8,128)} %reshape.4677, f32[1,64,6,512]{3,2,1,0:T(8,128)} %reshape.4678), kind=kLoop, calls=%fused_computation.201 | loop fusion | flops 786432 | bytes 2359296 | tf_op jit(solution)/shard_map/add | solution.py:215
  370.1 8.0 %fusion.116 = (f32[1,64,1,512]{3,2,1,0:T(1,128)S(1)}, f32[1,64,1,512]{3,2,1,0:T(1,128)S(1)}, f32[1,64,1,512]{3,2,1,0:T(1,128)S(1)}, f32[1,64,1,512]{3,2,1,0:T(1,...) fusion(f32[1,64,6,512]{3,2,1,0:T(8,128)} %reshape.4658, f32[1,64,6,512]{3,2,1,0:T(8,128)} %reshape.4659), kind=kLoop, calls=%fused_computation.213 | loop fusion | flops 786432 | bytes 2359296 | tf_op jit(solution)/shard_map/add | solution.py:215
  387.2 4.0 stack.22
  391.3 10.0 %fusion.19 = f32[1,8,8,8,512]{4,1,3,2,0:T(8,128)} fusion(f32[8,8,1,1]{1,0,3,2:T(8,128)S(1)} %copy-done.108, f32[8,8,8,512]{3,2,1,0:T(8,128)} %bitcast.488, f32[8,8,8,512]{3,2,1,0:T(8,128)} %copy.895, f32[8,8,8,512]{3,0,2,1:T(8,128)} %copy-done.51, f32[8,8,8,512]{3,0,2,1:T(8,128)} %stack.22, f32[8,8,8,512]{3,0,2,1:T(8,128)} %copy_dynamic-update-slice_fusion.24, ...), kind=kOutput, calls=%fused_computation.42 | convolution fusion | flops 27787264 | bytes 12583168 | tf_op jit(solution)/shard_map/dot_general | solution.py:143
  401.2 3.8 stack.27
  405.0 9.6 %fusion.16 = f32[1,8,8,8,512]{4,1,3,2,0:T(8,128)S(1)} fusion(f32[8,8,1,1]{1,0,3,2:T(8,128)S(1)} %copy-done.108, f32[8,8,8,512]{3,2,1,0:T(8,128)} %bitcast.487, f32[8,8,8,512]{3,2,1,0:T(8,128)} %copy.894, f32[8,8,8,512]{3,0,2,1:T(8,128)} %copy-done.50, f32[8,8,8,512]{3,0,2,1:T(8,128)} %stack.27, f32[8,8,8,512]{3,0,2,1:T(8,128)} %copy-done.48, ...), kind=kOutput, calls=%fused_computation.37 | convolution fusion | flops 27787264 | bytes 12583168 | tf_op jit(solution)/shard_map/dot_general | solution.py:143
  426.6 10.7 %psum.7 = f32[2,8,256]{2,1,0:T(8,128)S(1)} all-reduce(f32[2,8,256]{2,1,0:T(8,128)S(1)} %fusion.75), channel_id=1, replica_groups=mesh['blk'=8,'sub'=4] {'sub'}, use_global_device_ids=true, to_apply=%region_24.25 | all-reduce | flops 4096 | bytes 32768 | tf_op jit(solution)/shard_map/psum | solution.py:332
  (491 shorter events, 262.6 us)
Async XLA Ops:
  2.0 9.4 %copy-start = (f32[2,8,8,8,512]{4,3,2,1,0:T(8,128)S(1)}, f32[2,8,8,8,512]{4,3,2,1,0:T(8,128)}, u32[]{:S(2)}) copy-start(f32[2,8,8,8,512]{4,3,2,1,0:T(8,128)} %param.19) | copy-start | bytes 6291460
  27.8 32.4 %copy-start.118 = (s32[1600]{0:T(1024)}, s32[1600]{0:T(1024)S(1)}, u32[]{:S(2)}) copy-start(s32[1600]{0:T(1024)S(1)} %concatenate.51) | copy-start | bytes 19204
  46.8 162.2 %collective-permute-start.1 = (f32[256,1,3,64]{0,3,2,1:T(8,128)}, f32[256,1,3,64]{0,3,2,1:T(8,128)}, u32[]{:S(2)}, u32[]{:S(2)}) collective-permute-start(f32[256,1,3,64]{0,3,2,1:T(8,128)} %get-tuple-element.149), channel_id=1, source_target_pairs={{4,0},{8,4},{12,8},{16,12},{20,16},{24,20},{28,24},{0,28},{5,1},{9... | collective-permute-start | bytes 589832 | tf_op jit(solution)/shard_map/ppermute | solution.py:19
  52.9 156.2 %collective-permute-start = (f32[256,1,3,64]{0,3,2,1:T(8,128)}, f32[256,1,3,64]{0,3,2,1:T(8,128)}, u32[]{:S(2)}, u32[]{:S(2)}) collective-permute-start(f32[256,1,3,64]{0,3,2,1:T(8,128)} %get-tuple-element.148), channel_id=1, source_target_pairs={{0,4},{4,8},{8,12},{12,16},{16,20},{20,24},{24,28},{28,0},{1,5},{5... | collective-permute-start | bytes 589832 | tf_op jit(solution)/shard_map/ppermute | solution.py:17
  79.9 130.9 %collective-permute-start.5 = (f32[256,1,3,64]{0,3,2,1:T(8,128)}, f32[256,1,3,64]{0,3,2,1:T(8,128)}, u32[]{:S(2)}, u32[]{:S(2)}) collective-permute-start(f32[256,1,3,64]{0,3,2,1:T(8,128)} %get-tuple-element.155), channel_id=1, source_target_pairs={{4,0},{8,4},{12,8},{16,12},{20,16},{24,20},{28,24},{0,28},{5,1},{9... | collective-permute-start | bytes 589832 | tf_op jit(solution)/shard_map/ppermute | solution.py:19
  84.7 126.2 %collective-permute-start.4 = (f32[256,1,3,64]{0,3,2,1:T(8,128)}, f32[256,1,3,64]{0,3,2,1:T(8,128)}, u32[]{:S(2)}, u32[]{:S(2)}) collective-permute-start(f32[256,1,3,64]{0,3,2,1:T(8,128)} %get-tuple-element.154), channel_id=1, source_target_pairs={{0,4},{4,8},{8,12},{12,16},{16,20},{20,24},{24,28},{28,0},{1,5},{5... | collective-permute-start | bytes 589832 | tf_op jit(solution)/shard_map/ppermute | solution.py:17
  94.7 9.5 %copy-start.3 = (f32[256,1600]{0,1:T(8,128)S(1)}, f32[256,1600]{0,1:T(8,128)}, u32[]{:S(2)}) copy-start(f32[256,1600]{0,1:T(8,128)} %copy-done.2) | copy-start | bytes 4915204
  123.5 12.2 %copy-start.18 = (f32[1,8,8,8,512]{4,3,2,1,0:T(8,128)}, f32[1,8,8,8,512]{4,3,2,1,0:T(8,128)S(1)}, u32[]{:S(2)}) copy-start(f32[1,8,8,8,512]{4,3,2,1,0:T(8,128)S(1)} %get-tuple-element.168) | copy-start | bytes 3145732
  123.5 12.2 %copy-start.19 = (f32[1,8,8,8,512]{4,3,2,1,0:T(8,128)}, f32[1,8,8,8,512]{4,3,2,1,0:T(8,128)S(1)}, u32[]{:S(2)}) copy-start(f32[1,8,8,8,512]{4,3,2,1,0:T(8,128)S(1)} %get-tuple-element.169) | copy-start | bytes 3145732
  124.6 11.1 %copy-start.17 = (f32[1,8,8,8,512]{4,1,3,2,0:T(8,128)}, f32[1,8,8,8,512]{4,1,3,2,0:T(8,128)S(1)}, u32[]{:S(2)}) copy-start(f32[1,8,8,8,512]{4,1,3,2,0:T(8,128)S(1)} %convolution_bitcast_fusion.1) | copy-start | bytes 3145732
  209.0 11.4 %copy-start.23 = (f32[256,576]{0,1:T(8,128)S(1)}, f32[256,576]{0,1:T(8,128)}, u32[]{:S(2)}) copy-start(f32[256,576]{0,1:T(8,128)} %copy-done.22) | copy-start | bytes 1769476
  210.3 7.4 %collective-permute-start.3 = (f32[256,5,1,64]{0,3,2,1:T(8,128)S(1)}, f32[256,5,1,64]{0,3,2,1:T(8,128)S(1)}, u32[]{:S(2)}, u32[]{:S(2)}) collective-permute-start(f32[256,5,1,64]{0,3,2,1:T(8,128)S(1)} %get-tuple-element.137), channel_id=1, source_target_pairs={{1,0},{2,1},{3,2},{0,3},{5,4},{6,5},{7,6},{4,7},{9,8},{10,9},{11,1... | collective-permute-start | bytes 983048 | tf_op jit(solution)/shard_map/ppermute | solution.py:19
  210.4 10.0 %collective-permute-start.2 = (f32[256,5,1,64]{0,3,2,1:T(8,128)S(1)}, f32[256,5,1,64]{0,3,2,1:T(8,128)S(1)}, u32[]{:S(2)}, u32[]{:S(2)}) collective-permute-start(f32[256,5,1,64]{0,3,2,1:T(8,128)S(1)} %get-tuple-element.136), channel_id=1, source_target_pairs={{0,1},{1,2},{2,3},{3,0},{4,5},{5,6},{6,7},{7,4},{8,9},{9,10},{10,1... | collective-permute-start | bytes 983048 | tf_op jit(solution)/shard_map/ppermute | solution.py:17
  211.9 12.8 %collective-permute-start.7 = (f32[256,5,1,64]{0,3,2,1:T(8,128)S(1)}, f32[256,5,1,64]{0,3,2,1:T(8,128)S(1)}, u32[]{:S(2)}, u32[]{:S(2)}) collective-permute-start(f32[256,5,1,64]{0,3,2,1:T(8,128)S(1)} %get-tuple-element.139), channel_id=1, source_target_pairs={{1,0},{2,1},{3,2},{0,3},{5,4},{6,5},{7,6},{4,7},{9,8},{10,9},{11,1... | collective-permute-start | bytes 983048 | tf_op jit(solution)/shard_map/ppermute | solution.py:19
  213.3 14.2 %collective-permute-start.6 = (f32[256,5,1,64]{0,3,2,1:T(8,128)S(1)}, f32[256,5,1,64]{0,3,2,1:T(8,128)S(1)}, u32[]{:S(2)}, u32[]{:S(2)}) collective-permute-start(f32[256,5,1,64]{0,3,2,1:T(8,128)S(1)} %get-tuple-element.138), channel_id=1, source_target_pairs={{0,1},{1,2},{2,3},{3,0},{4,5},{5,6},{6,7},{7,4},{8,9},{9,10},{10,1... | collective-permute-start | bytes 983048 | tf_op jit(solution)/shard_map/ppermute | solution.py:17
  349.3 9.6 %copy-start.104 = (f32[1,64,1,512]{3,2,1,0:T(1,128)S(1)}, f32[1,64,1,512]{3,2,1,0:T(1,128)}, u32[]{:S(2)}) copy-start(f32[1,64,1,512]{3,2,1,0:T(1,128)} %get-tuple-element.129) | copy-start | bytes 393220
  349.3 10.2 %copy-start.103 = (f32[1,64,1,512]{3,2,1,0:T(1,128)S(1)}, f32[1,64,1,512]{3,2,1,0:T(1,128)}, u32[]{:S(2)}) copy-start(f32[1,64,1,512]{3,2,1,0:T(1,128)} %get-tuple-element.130) | copy-start | bytes 393220
  349.3 10.9 %copy-start.102 = (f32[1,64,1,512]{3,2,1,0:T(1,128)S(1)}, f32[1,64,1,512]{3,2,1,0:T(1,128)}, u32[]{:S(2)}) copy-start(f32[1,64,1,512]{3,2,1,0:T(1,128)} %get-tuple-element.131) | copy-start | bytes 393220
  349.3 11.6 %copy-start.101 = (f32[1,64,1,512]{3,2,1,0:T(1,128)S(1)}, f32[1,64,1,512]{3,2,1,0:T(1,128)}, u32[]{:S(2)}) copy-start(f32[1,64,1,512]{3,2,1,0:T(1,128)} %get-tuple-element.132) | copy-start | bytes 393220
  391.3 10.0 %copy-start.78 = (f32[1,64,1,512]{3,2,1,0:T(1,128)S(1)}, f32[1,64,1,512]{3,2,1,0:T(1,128)}, u32[]{:S(2)}) copy-start(f32[1,64,1,512]{3,2,1,0:T(1,128)} %get-tuple-element.119) | copy-start | bytes 393220
  405.0 9.6 %copy-start.33 = (f32[1,8,8,8,512]{4,1,3,2,0:T(8,128)S(1)}, f32[1,8,8,8,512]{4,1,3,2,0:T(8,128)}, u32[]{:S(2)}) copy-start(f32[1,8,8,8,512]{4,1,3,2,0:T(8,128)} %fusion.19) | copy-start | bytes 3145732
  405.0 9.6 %copy-start.46 = (f32[2,8,8,8,512]{4,3,2,1,0:T(8,128)S(1)}, f32[2,8,8,8,512]{4,3,2,1,0:T(8,128)}, u32[]{:S(2)}) copy-start(f32[2,8,8,8,512]{4,3,2,1,0:T(8,128)} %param.20) | copy-start | bytes 6291460
  421.8 15.7 %copy-start.30 = (f32[8,8,256]{1,0,2:T(8,128)S(1)}, f32[8,8,256]{1,0,2:T(8,128)}, u32[]{:S(2)}) copy-start(f32[8,8,256]{1,0,2:T(8,128)} %copy.603) | copy-start | bytes 196612
  424.2 15.8 %copy-start.116 = (f32[8,2]{0,1:T(2,128)S(1)}, f32[8,2]{0,1:T(2,128)}, u32[]{:S(2)}) copy-start(f32[8,2]{0,1:T(2,128)} %constant.48.clone) | copy-start | bytes 196
  (108 other events, 442.9 us)
where the time goes:
time: 454 us; the launch traced here: 446 us
  matrix products  169 us (37%)
  local copies, waits for them, and re-layouts  166 us (37%)
  other arithmetic  72.7 us (16%)
  starting transfers between devices  12.7 us (3%)
  waiting for transfers between devices  12.7 us (3%)
  blocking collectives  10.7 us (2%)
    dot_general x24, matrix products, reorient(): lax.dot_general(tiled, flattened, (((2,), (1,)), ((0,), (0,))), precision...  56 us
    dot_general x18, matrix products, apply_along(): lax.dot_general(tiled, shaped, (((2,), (1,)), ((0,), (0,))), precision=pr...  51.2 us
    unnamed x322, local copies, waits for them, and re-layouts  48.8 us
    dot_general x2, matrix products, apply_operator(): picked = jnp.dot(table_all, selector, precision=precise)  36 us
    add x6, other arithmetic, lift_faces(): running = running + factor * face_rows[row_index]  34 us
    reduce_sum x16, local copies, waits for them, and re-layouts, reorient(): jnp.sum(product * code_mask[None, :, None, :], axis=1).reshape(shape_all)  28.4 us
    dot_general x2, matrix products, apply_operator(): lax.dot_general(contrib, selector, (((1,), (1,)), ((), ())), precision=pr...  22.5 us
    another operation x18, local copies, waits for them, and re-layouts, face_tables(): value_all = jnp.stack(values, axis=2)  14 us
  transfers between devices with their start and end apart: 8, of which 4 were waited for; matrix products, arithmetic and copies ran while one was open for 34% of the time, Pallas kernels for 0%

commit v1 on v0

v1 whole, which is shorter than its diff:
```python
import functools

import jax
import jax.numpy as jnp
import numpy as np
from jax import lax
from jax.experimental import pallas as pl
from jax.experimental.pallas import tpu as pltpu
from jax.sharding import PartitionSpec as P


LANES = 128
MIB = 1024 * 1024


def node_points():
    positive = [0.2092992179024789, 0.5917001814331423, 0.8717401485096066, 1.0]
    return np.array(sorted([-entry for entry in positive] + positive))


def derivative_matrix(node_count):
    points = node_points()
    weights = np.array(
        [
            1.0 / np.prod([points[row] - points[col] for col in range(node_count) if col != row])
            for row in range(node_count)
        ]
    )
    matrix = np.zeros((node_count, node_count))
    for row in range(node_count):
        for col in range(node_count):
            if row != col:
                matrix[row, col] = weights[col] / weights[row] / (points[row] - points[col])
        matrix[row, row] = -np.sum(matrix[row])
    return matrix


def inverse_code(code):
    swapped = 4 + 2 * jnp.bitwise_and(code, 1) + jnp.bitwise_and(jnp.right_shift(code, 1), 1)
    return jnp.where(code >= 4, swapped, code)


def spread_down(row):
    return jnp.broadcast_to(row, (LANES, LANES)).T


def lane_order(code, nodes):
    lane = lax.broadcasted_iota(jnp.int32, code.shape, 1)
    half = nodes * nodes
    place = jnp.bitwise_and(lane, half - 1)
    one, two = place // nodes, jnp.bitwise_and(place, nodes - 1)
    other = lane - place + two * nodes + one
    first = jnp.bitwise_and(code, 1) * ((nodes - 1) * nodes)
    second = jnp.bitwise_and(jnp.right_shift(code, 1), 1) * (nodes - 1)
    return jnp.bitwise_xor(jnp.where(jnp.bitwise_and(code, 4) > 0, other, lane), first + second)


def column(values):
    place = lax.broadcasted_iota(jnp.int32, (len(values), LANES), 0)
    result = jnp.full((len(values), LANES), float(values[0]), jnp.float32)
    for at, value in enumerate(values[1:], 1):
        result = jnp.where(place == at, float(value), result)
    return result


def weighted(factors, terms):
    running = None
    for factor, term in zip(factors, terms):
        if float(factor) == 0.0:
            continue
        product = term if float(factor) == 1.0 else float(factor) * term
        running = product if running is None else running + product
    return running


def derive(matrix, terms):
    count = len(terms)
    half = count // 2
    even = [terms[k] + terms[count - 1 - k] for k in range(half)]
    odd = [terms[k] - terms[count - 1 - k] for k in range(half)]
    low, high = [], []
    for i in range(half):
        plus = weighted([0.5 * (matrix[i, k] + matrix[i, count - 1 - k]) for k in range(half)], even)
        minus = weighted([0.5 * (matrix[i, k] - matrix[i, count - 1 - k]) for k in range(half)], odd)
        low.append(minus + plus)
        high.append(minus - plus)
    return low + high[::-1]


def split(value):
    head = value.astype(jnp.bfloat16)
    return head, (value - head.astype(jnp.float32)).astype(jnp.bfloat16)


def mxu(left, right, dims=(((1,), (0,)), ((), ()))):
    return lax.dot_general(left, right, dims, preferred_element_type=jnp.float32)


def trace_kernel(rows_ref, p_ref, fw_ref, fm_ref, table, send_ref, nat, *, derivative, elems):
    step = pl.program_id(0)
    steps = pl.num_programs(0)
    fields, nodes = p_ref.shape[0], p_ref.shape[1]
    pieces_total = fields + 1
    face_size = nodes * nodes
    last = nodes - 1
    flat = p_ref.reshape(fields * nodes * nodes * nodes, LANES)
    base = step * LANES
    low = [-derivative[0, k] for k in range(nodes)]
    high = [derivative[last, k] for k in range(nodes)]

    def put(face, piece, part):
        table[pl.ds((face * elems + base) * pieces_total + piece, LANES, stride=pieces_total), :] = part.T

    for face in range(6):
        put(face, fields, jnp.concatenate([fw_ref[face], fm_ref[face]], axis=0))

    for f in range(fields):
        for axis in range(3):
            for at in range(nodes):
                if axis == 0:
                    terms = [p_ref[f, k, at] for k in range(nodes)]
                elif axis == 1:
                    terms = [p_ref[f, at, k] for k in range(nodes)]
                else:
                    first = (f * nodes + at) * nodes * nodes
                    terms = [flat[pl.ds(first + k, nodes, stride=nodes), :] for k in range(nodes)]
                rows = slice(at * nodes, (at + 1) * nodes)
                more = slice(face_size + at * nodes, face_size + (at + 1) * nodes)
                nat[f, 2 * axis, rows] = terms[0]
                nat[f, 2 * axis, more] = weighted(low, terms)
                nat[f, 2 * axis + 1, rows] = terms[last]
                nat[f, 2 * axis + 1, more] = weighted(high, terms)
            put(2 * axis, f, nat[f, 2 * axis])
            put(2 * axis + 1, f, nat[f, 2 * axis + 1])

    @pl.when(step == steps - 1)
    def _():
        group_size = 16
        slot_total = send_ref.shape[0] // pieces_total

        def pick(group, carry):
            for u in range(group_size):
                k = group * group_size + u
                send_ref[pl.ds(k * pieces_total, pieces_total), :] = table[pl.ds(rows_ref[k], pieces_total), :]
            return carry

        lax.fori_loop(0, slot_total // group_size, pick, 0)


def traces(rows, pressure, face_weight, face_metric, derivative):
    fields, nodes, elems = pressure.shape[0], pressure.shape[1], pressure.shape[-1]
    face_size = nodes * nodes
    slot_total = rows.shape[0]
    face_spec = pl.BlockSpec((6, face_size, LANES), lambda s: (0, 0, s))
    whole = pl.BlockSpec(memory_space=pltpu.VMEM)
    return pl.pallas_call(
        functools.partial(trace_kernel, derivative=derivative, elems=elems),
        out_shape=(
            jax.ShapeDtypeStruct((6 * elems * (fields + 1), LANES), jnp.float32),
            jax.ShapeDtypeStruct((slot_total * (fields + 1), LANES), jnp.float32),
        ),
        grid=(elems // LANES,),
        in_specs=[
            pl.BlockSpec(memory_space=pltpu.SMEM),
            pl.BlockSpec((fields, nodes, nodes, nodes, LANES), lambda s: (0, 0, 0, 0, s)),
            face_spec,
            face_spec,
        ],
        out_specs=(whole, whole),
        scratch_shapes=[pltpu.VMEM((fields, 6, 2 * face_size, LANES), jnp.float32)],
        compiler_params=pltpu.CompilerParams(vmem_limit_bytes=16 * MIB),
        cost_estimate=pl.CostEstimate(flops=10**7, bytes_accessed=9 * 10**6, transcendentals=0),
        name="traces",
    )(rows, pressure, face_weight, face_metric)


def flux_rows(own, other, order, fields, nodes):
    half = nodes * nodes
    penalty = nodes * (nodes + 1) / 2.0
    lane = lax.broadcasted_iota(jnp.int32, order.shape, 1)
    head = lane < half
    turned = [jnp.take_along_axis(piece, order, axis=1) for piece in other]
    own_wm, other_wm = own[fields], turned[fields]
    mean = 0.5 * (own_wm + other_wm)
    swapped = pltpu.roll(mean, half, 1)
    weight = jnp.where(head, mean, swapped)
    own_scale = jnp.where(head, 1.0, own_wm)
    other_scale = jnp.where(head, 1.0, other_wm)
    direct = jnp.where(head, penalty * weight * swapped, 0.0)
    crossed = -0.5 * weight * own_scale
    results = []
    for f in range(fields):
        gap = own[f] * own_scale - turned[f] * other_scale
        results.append(direct * gap + crossed * pltpu.roll(gap, half, 1))
    return results


def pieces(ref, start, rows, fields):
    return [ref[pl.ds(start * (fields + 1) + f, rows, stride=fields + 1), :] for f in range(fields + 1)]


def local_kernel(from_ref, to_ref, code_ref, table_ref, out_ref, picked, order, result, *, fields, nodes):
    total = from_ref.shape[0]
    count = total // 2
    width = fields + 1
    group_size = 16
    out_ref[...] = jnp.zeros_like(out_ref)

    def pick(group, carry):
        for u in range(group_size):
            k = group * group_size + u
            picked[pl.ds(k * width, width), :] = table_ref[pl.ds(from_ref[k], width), :]
        return carry

    lax.fori_loop(0, total // group_size, pick, 0)
    for at in range(count // LANES):
        code = code_ref[4:5, at * LANES : (at + 1) * LANES]
        column_code = spread_down(code.astype(jnp.float32)).astype(jnp.int32)
        order[at * LANES : (at + 1) * LANES, :] = lane_order(column_code, nodes)
        order[count + at * LANES : count + (at + 1) * LANES, :] = lane_order(inverse_code(column_code), nodes)
    rows = 32

    def flux(at, carry):
        start = at * rows
        other = lax.rem(start + count, total)
        values = flux_rows(
            pieces(picked, start, rows, fields),
            pieces(picked, other, rows, fields),
            order[pl.ds(pl.multiple_of(start, rows), rows), :],
            fields,
            nodes,
        )
        for f in range(fields):
            result[pl.ds(start * fields + f, rows, stride=fields), :] = values[f]
        return carry

    lax.fori_loop(0, total // rows, flux, 0)

    def place(group, carry):
        for u in range(group_size):
            k = group * group_size + u
            out_ref[pl.ds(to_ref[k], fields), :] = result[pl.ds(k * fields, fields), :]
        return carry

    lax.fori_loop(0, total // group_size, place, 0)


def local_fluxes(rows_from, rows_to, local_pairs, table, fields, nodes, elems):
    total = rows_from.shape[0]
    vmem = pl.BlockSpec(memory_space=pltpu.VMEM)
    smem = pl.BlockSpec(memory_space=pltpu.SMEM)
    return pl.pallas_call(
        functools.partial(local_kernel, fields=fields, nodes=nodes),
        out_shape=jax.ShapeDtypeStruct((6 * elems * fields, LANES), jnp.float32),
        in_specs=[smem, smem, vmem, vmem],
        out_specs=vmem,
        scratch_shapes=[
            pltpu.VMEM((total * (fields + 1), LANES), jnp.float32),
            pltpu.VMEM((total, LANES), jnp.int32),
            pltpu.VMEM((total * fields, LANES), jnp.float32),
        ],
        compiler_params=pltpu.CompilerParams(vmem_limit_bytes=16 * MIB),
        cost_estimate=pl.CostEstimate(flops=10**7, bytes_accessed=12 * 10**6, transcendentals=0),
        name="local_fluxes",
    )(rows_from, rows_to, local_pairs, table)


def volume_kernel(p_ref, rs_ref, g_ref, dh_ref, dl_ref, th_ref, tl_ref, out_ref, one, two, three, *, derivative):
    fields, nodes = p_ref.shape[0], p_ref.shape[1]
    rows = nodes**3
    block = dh_ref.shape[0]
    back = derivative.T

    def along_last(read, write, head_ref, tail_ref):
        for at in range(rows // block):
            value = jnp.concatenate([read(f)[at * block : (at + 1) * block] for f in range(fields)], axis=1)
            head, tail = split(value)
            result = mxu(head_ref[...], head) + mxu(head_ref[...], tail) + mxu(tail_ref[...], head)
            for f in range(fields):
                write(f, at, result[:, f * LANES : (f + 1) * LANES])

    def put_three(f, at, value):
        three[f, at * (block // 64) : (at + 1) * (block // 64)] = value.reshape(block // 64, nodes, nodes, LANES)

    along_last(lambda f: p_ref[f].reshape(rows, LANES), put_three, dh_ref, dl_ref)
    for f in range(fields):
        for j in range(nodes):
            slopes = derive(derivative, [p_ref[f, k, j] for k in range(nodes)])
            for i in range(nodes):
                one[f, i, j] = slopes[i]
    for i in range(nodes):
        for f in range(fields):
            slopes = derive(derivative, [p_ref[f, i, k] for k in range(nodes)])
            flux = []
            for j in range(nodes):
                s1, s2, s3 = one[f, i, j], slopes[j], three[f, i, j]
                xx, yy, zz, xy, xz, yz = [g_ref[c, i, j] for c in range(6)]
                one[f, i, j] = xx * s1 + xy * s2 + xz * s3
                flux.append(xy * s1 + yy * s2 + yz * s3)
                three[f, i, j] = xz * s1 + yz * s2 + zz * s3
            for j, value in enumerate(derive(back, flux)):
                two[f, i, j] = rs_ref[f, i, j] - value

    def put_two(f, at, value):
        part = value.reshape(block // 64, nodes, nodes, LANES)
        rng = slice(at * (block // 64), (at + 1) * (block // 64))
        two[f, rng] = two[f, rng] - part

    along_last(lambda f: three[f].reshape(rows, LANES), put_two, th_ref, tl_ref)
    for f in range(fields):
        for j in range(nodes):
            sums = derive(back, [one[f, k, j] for k in range(nodes)])
            for i in range(nodes):
                out_ref[f, i, j] = two[f, i, j] - sums[i]


def volume(pressure, right_side, geometry, derivative):
    fields, nodes, elems = pressure.shape[0], pressure.shape[1], pressure.shape[-1]
    block = 256
    spread = np.kron(np.eye(block // nodes), derivative)

    def parts(matrix):
        head = jnp.asarray(matrix, jnp.float32).astype(jnp.bfloat16)
        tail = (jnp.asarray(matrix, jnp.float32) - head.astype(jnp.float32)).astype(jnp.bfloat16)
        return head, tail

    whole = (fields, nodes, nodes, nodes, LANES)
    field_spec = pl.BlockSpec(whole, lambda s: (0, 0, 0, 0, s))
    table_spec = pl.BlockSpec((block, block), lambda s: (0, 0))
    return pl.pallas_call(
        functools.partial(volume_kernel, derivative=derivative),
        out_shape=jax.ShapeDtypeStruct(pressure.shape, jnp.float32),
        grid=(elems // LANES,),
        in_specs=[
            field_spec,
            field_spec,
            pl.BlockSpec((6, nodes, nodes, nodes, LANES), lambda s: (0, 0, 0, 0, s)),
            table_spec,
            table_spec,
            table_spec,
            table_spec,
        ],
        out_specs=field_spec,
        scratch_shapes=[pltpu.VMEM(whole, jnp.float32)] * 3,
        compiler_params=pltpu.CompilerParams(vmem_limit_bytes=16 * MIB),
        cost_estimate=pl.CostEstimate(flops=10**9, bytes_accessed=13 * 10**6, transcendentals=0),
        name="volume",
    )(pressure, right_side, geometry, *parts(spread), *parts(spread.T))


def residual_kernel(
    to_ref, slots_ref, own_ref, got0, got1, got2, got3, got4, got5, got6, got7, start_ref, rows_in, map_ref,
    res_ref, sums_ref, rows_ref, order, result, nat, restricted,
    *, derivative, prolong, elems, fields, nodes,
):
    step = pl.program_id(0)
    slot_total = to_ref.shape[0]
    cap = slot_total // 9
    half = nodes * nodes
    last = nodes - 1
    del rows_in

    @pl.when(step == 0)
    def _():
        source = dict(zip((0, 1, 2, 3, 5, 6, 7, 8), (got0, got1, got2, got3, got4, got5, got6, got7)))
        code = jnp.where(slots_ref[3] > 0, slots_ref[4], inverse_code(slots_ref[4]))
        flags = (code + 8 * slots_ref[2]).astype(jnp.float32)
        flags = jnp.concatenate([flags, jnp.zeros((1, order.shape[0] - slot_total), jnp.float32)], axis=1)
        for at in range(order.shape[0] // LANES):
            order[at * LANES : (at + 1) * LANES, :] = spread_down(flags[:, at * LANES : (at + 1) * LANES]).astype(
                jnp.int32
            )
        result[4 * cap * fields : 5 * cap * fields, :] = jnp.zeros((cap * fields, LANES), jnp.float32)
        rows = min(cap, 32)
        for k, ref in source.items():
            for part in range(cap // rows):
                first = k * cap + part * rows
                flag = order[first : first + rows, :]
                values = flux_rows(
                    pieces(own_ref, first, rows, fields),
                    pieces(ref, part * rows, rows, fields),
                    lane_order(flag, nodes),
                    fields,
                    nodes,
                )
                for f in range(fields):
                    result[pl.ds(first * fields + f, rows, stride=fields), :] = jnp.where(flag >= 8, values[f], 0.0)
        group_size = 16

        def put(group, carry):
            for u in range(group_size):
                k = group * group_size + u
                rows_ref[pl.ds(to_ref[k], fields), :] = result[pl.ds(k * fields, fields), :]
            return carry

        lax.fori_loop(0, slot_total // group_size, put, 0)

    base = step * LANES
    for f in range(fields):
        for face in range(6):
            nat[f, face] = rows_ref[pl.ds((face * elems + base) * fields + f, LANES, stride=fields), :].T
    value_low = column([1.0] + [0.0] * last)
    value_high = column([0.0] * last + [1.0])
    lift_low = column(list(-derivative[0]))
    lift_high = column(list(derivative[last]))
    ramp = prolong[:, 1]
    ramp_rows = column(list(ramp))
    for f in range(fields):
        spots = [[None, None], [None, None]]
        for i in range(nodes):
            pencil = []
            for j in range(nodes):
                value = start_ref[f, i, j]
                at_j = slice(j * nodes, (j + 1) * nodes)
                at_i = slice(i * nodes, (i + 1) * nodes)
                low_j = slice(half + j * nodes, half + (j + 1) * nodes)
                low_i = slice(half + i * nodes, half + (i + 1) * nodes)
                if i == 0:
                    value = value - nat[f, 0, at_j]
                if i == last:
                    value = value - nat[f, 1, at_j]
                value = value + float(derivative[0, i]) * nat[f, 0, low_j]
                value = value - float(derivative[last, i]) * nat[f, 1, low_j]
                if j == 0:
                    value = value - nat[f, 2, at_i]
                if j == last:
                    value = value - nat[f, 3, at_i]
                value = value + float(derivative[0, j]) * nat[f, 2, low_i]
                value = value - float(derivative[last, j]) * nat[f, 3, low_i]
                node = i * nodes + j
                value = value - value_low * nat[f, 4, node : node + 1]
                value = value - lift_low * nat[f, 4, half + node : half + node + 1]
                value = value - value_high * nat[f, 5, node : node + 1]
                value = value - lift_high * nat[f, 5, half + node : half + node + 1]
                res_ref[f, i, j] = value
                pencil.append(value)
            total = weighted([1.0] * nodes, pencil)
            sloped = weighted(list(ramp), pencil)
            for b, part in enumerate((total, sloped)):
                spots[0][b] = part if i == 0 else spots[0][b] + part
                extra = float(ramp[i]) * part
                if float(ramp[i]) != 0.0:
                    spots[1][b] = extra if spots[1][b] is None else spots[1][b] + extra
        for a in range(2):
            for b in range(2):
                if a == 0:
                    part = spots[0][b] - spots[1][b]
                    other = spots[0][1] - spots[1][1]
                else:
                    part = spots[1][b]
                    other = spots[1][1]
                if b == 0:
                    part = part - other
                whole = jnp.sum(part, axis=0, keepdims=True)
                up = jnp.sum(part * ramp_rows, axis=0, keepdims=True)
                at = f * 8 + 4 * a + 2 * b
                restricted[at : at + 1, :] = whole - up
                restricted[at + 1 : at + 2, :] = up

    cells = sums_ref.shape[1]
    hot = (lax.broadcasted_iota(jnp.int32, (cells, LANES), 0) == map_ref[...]).astype(jnp.bfloat16)
    value = restricted[...]
    head, rest = split(value)
    tail = (value - head.astype(jnp.float32) - rest.astype(jnp.float32)).astype(jnp.bfloat16)
    across = (((1,), (1,)), ((), ()))
    sums = mxu(head, hot, across) + mxu(rest, hot, across) + mxu(tail, hot, across)

    @pl.when(step == 0)
    def _():
        sums_ref[...] = sums

    @pl.when(step > 0)
    def _():
        sums_ref[...] += sums


def residuals(rows_to, slots, own, received, start, local_rows, cell_row, cells, derivative, prolong):
    fields, nodes, elems = start.shape[0], start.shape[1], start.shape[-1]
    slot_total = rows_to.shape[0]
    padded = -(-slot_total // LANES) * LANES
    field_spec = pl.BlockSpec((fields, nodes, nodes, nodes, LANES), lambda s: (0, 0, 0, 0, s))
    vmem = pl.BlockSpec(memory_space=pltpu.VMEM)
    residual, sums, _ = pl.pallas_call(
        functools.partial(
            residual_kernel, derivative=derivative, prolong=prolong, elems=elems, fields=fields, nodes=nodes
        ),
        out_shape=(
            jax.ShapeDtypeStruct(start.shape, jnp.float32),
            jax.ShapeDtypeStruct((fields * 8, cells), jnp.float32),
            jax.ShapeDtypeStruct(local_rows.shape, jnp.float32),
        ),
        grid=(elems // LANES,),
        in_specs=[pl.BlockSpec(memory_space=pltpu.SMEM)] + [vmem] * 10
        + [field_spec, vmem, pl.BlockSpec((1, LANES), lambda s: (0, s))],
        out_specs=(field_spec, pl.BlockSpec((fields * 8, cells), lambda s: (0, 0)), vmem),
        scratch_shapes=[
            pltpu.VMEM((padded, LANES), jnp.int32),
            pltpu.VMEM((slot_total * fields, LANES), jnp.float32),
            pltpu.VMEM((fields, 6, LANES, LANES), jnp.float32),
            pltpu.VMEM((fields * 8, LANES), jnp.float32),
        ],
        input_output_aliases={12: 2},
        compiler_params=pltpu.CompilerParams(vmem_limit_bytes=16 * MIB),
        cost_estimate=pl.CostEstimate(flops=10**8, bytes_accessed=9 * 10**6, transcendentals=0),
        name="residuals",
    )(rows_to, slots, own, *received, start, local_rows, cell_row)
    return residual, sums


def correct_kernel(p_ref, inverse_ref, map_ref, *refs, prolong, parts):
    sum_refs = refs[:parts]
    out_ref, heads, rests, tails = refs[parts:]
    step = pl.program_id(0)
    fields, nodes = p_ref.shape[0], p_ref.shape[1]
    cells = inverse_ref.shape[-1]

    @pl.when(step == 0)
    def _():
        total = sum_refs[0][...]
        for ref in sum_refs[1:]:
            total = total + ref[...]
        for f in range(fields):
            running = None
            for j in range(8):
                term = inverse_ref[j] * total[f * 8 + j : f * 8 + j + 1, :]
                running = term if running is None else running + term
            head, rest = split(running)
            tail = (running - head.astype(jnp.float32) - rest.astype(jnp.float32)).astype(jnp.bfloat16)
            heads[f * 8 : f * 8 + 8] = head.astype(jnp.float32)
            rests[f * 8 : f * 8 + 8] = rest.astype(jnp.float32)
            tails[f * 8 : f * 8 + 8] = tail.astype(jnp.float32)

    hot = (lax.broadcasted_iota(jnp.int32, (cells, LANES), 0) == map_ref[...]).astype(jnp.bfloat16)
    spread = (
        mxu(heads[...].astype(jnp.bfloat16), hot)
        + mxu(rests[...].astype(jnp.bfloat16), hot)
        + mxu(tails[...].astype(jnp.bfloat16), hot)
    )
    ramp = prolong[:, 1]
    ramp_rows = column(list(ramp))
    for f in range(fields):
        quad = []
        for ab in range(4):
            at = f * 8 + 2 * ab
            down, up = spread[at : at + 1, :], spread[at + 1 : at + 2, :]
            quad.append(down + ramp_rows * (up - down))
        for j in range(nodes):
            down = quad[0] + float(ramp[j]) * (quad[1] - quad[0])
            slope = quad[2] + float(ramp[j]) * (quad[3] - quad[2]) - down
            for i in range(nodes):
                out_ref[f, i, j] = p_ref[f, i, j] + (down + float(ramp[i]) * slope)


def corrected_field(pressure, coarse_inverse, cell_row, sums, prolong):
    fields, nodes, elems = pressure.shape[0], pressure.shape[1], pressure.shape[-1]
    cells = coarse_inverse.shape[-1]
    field_spec = pl.BlockSpec((fields, nodes, nodes, nodes, LANES), lambda s: (0, 0, 0, 0, s))
    sum_spec = pl.BlockSpec((fields * 8, cells), lambda s: (0, 0))
    return pl.pallas_call(
        functools.partial(correct_kernel, prolong=prolong, parts=len(sums)),
        out_shape=jax.ShapeDtypeStruct(pressure.shape, jnp.float32),
        grid=(elems // LANES,),
        in_specs=[
            field_spec,
            pl.BlockSpec(coarse_inverse.shape, lambda s: (0, 0, 0)),
            pl.BlockSpec((1, LANES), lambda s: (0, s)),
        ]
        + [sum_spec] * len(sums),
        out_specs=field_spec,
        scratch_shapes=[pltpu.VMEM((fields * 8, cells), jnp.float32)] * 3,
        compiler_params=pltpu.CompilerParams(vmem_limit_bytes=16 * MIB),
        cost_estimate=pl.CostEstimate(flops=10**8, bytes_accessed=5 * 10**6, transcendentals=0),
        name="correct",
    )(pressure, coarse_inverse, cell_row, *sums)


def solution(mesh):
    blk_count, sub_count = mesh.shape["blk"], mesh.shape["sub"]

    def shifted(block, k):
        da, db = k // 3 - 1, k % 3 - 1
        pairs = []
        for b in range(blk_count):
            for u in range(sub_count):
                source = ((b + da) % blk_count) * sub_count + (u + db) % sub_count
                pairs.append((source, b * sub_count + u))
        size = block.shape[0] // 9
        return lax.ppermute(block[(8 - k) * size : (9 - k) * size], ("blk", "sub"), pairs)

    def on_device(
        pressure,
        right_side,
        geometry,
        face_weight,
        face_metric,
        cross_slots,
        local_pairs,
        coarse_map,
        coarse_inverse,
    ):
        fields, nodes, elems = pressure.shape[0], pressure.shape[1], pressure.shape[-1]
        derivative = derivative_matrix(nodes)
        points = node_points()
        prolong = np.stack([(1.0 - points) / 2.0, (1.0 + points) / 2.0], axis=1)
        cells = coarse_inverse.shape[-1]
        cell_row = coarse_map.reshape(1, elems)
        cross = cross_slots[1, 0] * elems + cross_slots[0, 0]
        pairs = jnp.concatenate(
            [local_pairs[1] * elems + local_pairs[0], local_pairs[3] * elems + local_pairs[2]]
        )
        width = fields + 1
        table, send = traces(
            cross * width,
            pltpu.with_memory_space_constraint(pressure, pltpu.HBM),
            pltpu.with_memory_space_constraint(jnp.transpose(face_weight, (1, 0, 2)), pltpu.HBM),
            pltpu.with_memory_space_constraint(jnp.transpose(face_metric, (1, 0, 2)), pltpu.HBM),
            derivative,
        )
        received = {k: shifted(send, k) for k in (3, 5, 1, 7)}
        local_rows = local_fluxes(pairs * width, pairs * fields, local_pairs, table, fields, nodes, elems)
        later, local_rows, right_later = lax.optimization_barrier((send, local_rows, right_side))
        received.update({k: shifted(later, k) for k in (0, 2, 6, 8)})
        start = volume(pressure, right_later, geometry, derivative)
        received = [received[k] for k in sorted(received)]
        residual, sums = residuals(
            cross * fields, cross_slots, send, received, start, local_rows, cell_row, cells, derivative, prolong
        )
        all_sums = [sums]
        for shift in range(1, sub_count):
            ring = [(at, (at + shift) % sub_count) for at in range(sub_count)]
            all_sums.append(lax.ppermute(sums, "sub", ring))
        return residual, corrected_field(pressure, coarse_inverse, cell_row, all_sums, prolong)

    split_elems = ("blk", "sub")
    field_spec = P(None, None, None, None, split_elems)

    return jax.shard_map(
        on_device,
        mesh=mesh,
        in_specs=(
            field_spec,
            field_spec,
            field_spec,
            P(None, None, split_elems),
            P(None, None, split_elems),
            P(None, split_elems, None),
            P(None, split_elems),
            P(split_elems),
            P(None, None, "blk"),
        ),
        out_specs=(field_spec, field_spec),
        check_vma=False,
    )
```

time: 454 us -> 55 us (0.12); the launches traced: 446 us -> 54.7 us
  matrix products: 169 us -> 0 us
  local copies, waits for them, and re-layouts: 166 us -> 0.12 us
  other arithmetic: 72.7 us -> 1.63 us
  Pallas kernels: 0 us -> 29.7 us
  blocking collectives: 10.7 us -> 0 us
  waiting for transfers between devices: 12.7 us -> 2.96 us
  starting transfers between devices: 12.7 us -> 19.5 us
    dot_general x49 -> x0, matrix products: 169 us -> none  [the longest x24 56 us: reorient(): lax.dot_general(tiled, flattened, (((2,), (1,)), ((0,), (0,))), precision...]
    unnamed x322 -> x22, local copies, waits for them, and re-layouts: 48.8 us -> 0.07 us
    add x7 -> x1, other arithmetic: 35.8 us -> 0.9 us  [on_device(): local_pairs[1] * elems + local_pairs[0]]
    pallas_call x0 -> x5, Pallas kernels: none -> 29.7 us  [the longest x1 8.83 us: local_fluxes(): pl.pallas_call(functools.partial(local_kernel, fields=fields, nodes=nodes...]
    reduce_sum x16 -> x0, local copies, waits for them, and re-layouts: 28.4 us -> none  [reorient(): jnp.sum(product * code_mask[None, :, None, :], axis=1).reshape(shape_all)]
    another operation x32 -> x0, local copies, waits for them, and re-layouts: 28.3 us -> none  [the longest x18 14 us: face_tables(): value_all = jnp.stack(values, axis=2)]
    reshape x13 -> x0, local copies, waits for them, and re-layouts: 24.2 us -> none  [the longest x4 8.71 us: apply_along(): shaped = operand.reshape(before, shape_all[axis], -1)]
    slice x15 -> x2, local copies, waits for them, and re-layouts: 23.7 us -> 0.05 us  [shifted(): block[(8 - k) * size:(9 - k) * size]]
  transfers between devices with their start and end apart: 8 -> 11, of which waited for: 4 -> 3; matrix products, arithmetic and copies ran while one was open for 34% -> 0% of each run, Pallas kernels for 0% -> 13%
where the time goes in v1:
time: 55 us; the launch traced here: 54.7 us
  Pallas kernels  29.7 us (54%)
  starting transfers between devices  19.5 us (35%)
  waiting for transfers between devices  2.96 us (5%)
  other arithmetic  1.63 us (3%)
  between operations  0.87 us (2%)
    ppermute x8, starting transfers between devices, shifted(): lax.ppermute(block[(8 - k) * size:(9 - k) * size], ('blk', 'sub'), pairs)  18.2 us
    pallas_call x1, Pallas kernels, local_fluxes(): pl.pallas_call(functools.partial(local_kernel, fields=fields, nodes=nodes...  8.83 us
    pallas_call x1, Pallas kernels, volume(): pl.pallas_call(functools.partial(volume_kernel, derivative=derivative), o...  7.02 us
    pallas_call x1, Pallas kernels, residuals(): pl.pallas_call(functools.partial(residual_kernel, derivative=derivative,...  6.73 us
    pallas_call x1, Pallas kernels, traces(): pl.pallas_call(functools.partial(trace_kernel, derivative=derivative, ele...  4.53 us
    ppermute x3, waiting for transfers between devices, on_device(): all_sums.append(lax.ppermute(sums, 'sub', ring))  2.94 us
    pallas_call x1, Pallas kernels, corrected_field(): pl.pallas_call(functools.partial(correct_kernel, prolong=prolong, parts=l...  2.54 us
    ppermute x3, starting transfers between devices, on_device(): all_sums.append(lax.ppermute(sums, 'sub', ring))  1.22 us
  transfers between devices with their start and end apart: 11, of which 3 were waited for; matrix products, arithmetic and copies ran while one was open for 0% of the time, Pallas kernels for 13%

profile of v1, /device:TPU:0, one launch (start us, length us, event | category | flops | bytes accessed | tf_op | source)
XLA Modules:
  0.0 54.7 jit_solution(4146631341177209686)
XLA Ops:
  0.6 0.9 %slice_add_fusion.2 = (s32[1,512]{1,0:T(1,128)S(1)}, s32[1,512]{1,0:T(1,128)S(1)}) fusion(s32[5,512]{1,0:T(8,128)} %code_ref.1), kind=kLoop, calls=%fused_computation.7 | loop fusion | flops 2048 | bytes 12288 | tf_op jit(solution)/shard_map/add | solution.py:609
  1.5 0.7 %multiply_reduce_fusion = (s32[576]{0:T(1024)S(1)}, s32[576]{0:T(1024)S(1)}) fusion(s32[5,1,576]{2,1,0:T(1,128)} %slots_ref.1), kind=kLoop, calls=%fused_computation.3 | loop fusion | flops 2304 | bytes 9216 | tf_op jit(solution)/shard_map/mul | solution.py:613
  2.3 0.0 copy-start.2
  2.3 4.5 %traces.1 = (f32[9216,128]{1,0:T(8,128)S(1)}, f32[1728,128]{1,0:T(8,128)S(1)}) custom-call(s32[576]{0:T(1024)S(1)} %get-tuple-element.16.rows_ref, f32[2,8,8,8,512]{4,3,2,1,0:T(8,128)} %p_ref.5, f32[6,64,512]{2,1,0:T(8,128)} %bitcast.7, f32[6,64,512]{2,1,0:T(8,128)} %bitcast.8), custom_call_target="tpu_custom_call" | custom-call | flops 10000000 | bytes 9000000 | tf_op jit(solution)/shard_map/traces/pallas_call | solution.py:156
  6.8 0.0 copy-start
  6.9 0.0 copy-start.3
  6.9 0.0 copy-start.4
  6.9 0.0 copy-start.5
  6.9 0.0 copy-start.6
  6.9 8.8 %local_fluxes.1.rows_in = f32[6144,128]{1,0:T(8,128)S(1)} custom-call(s32[1024]{0:T(1024)S(1)} %get-tuple-element.29.from_ref, s32[1024]{0:T(1024)S(1)} %get-tuple-element.28.to_ref, s32[5,512]{1,0:T(8,128)S(1)} %copy-done.8, f32[9216,128]{1,0:T(8,128)S(1)} %get-tuple-element.10.table_ref), custom_call_target="tpu_custom_call" | custom-call | flops 10000000 | bytes 12000000 | tf_op jit(solution)/shard_map/local_fluxes/pallas_call | solution.py:252
  15.8 6.5 %collective-permute-start.7 = (f32[192,128]{1,0:T(8,128)S(1)}, f32[192,128]{1,0:T(8,128)S(1)}, u32[]{:S(2)}, u32[]{:S(2)}) collective-permute-start(f32[192,128]{1,0:T(8,128)S(1)} %get-tuple-element.18), channel_id=1, source_target_pairs={{5,0},{6,1},{7,2},{4,3},{9,4},{10,5},{11,6},{8,7},{13,8},{14,9},{1... | collective-permute-start | bytes 294920 | tf_op jit(solution)/shard_map/ppermute | solution.py:588
  22.3 2.6 %collective-permute-start.2 = (f32[192,128]{1,0:T(8,128)S(1)}, f32[192,128]{1,0:T(8,128)S(1)}, u32[]{:S(2)}, u32[]{:S(2)}) collective-permute-start(f32[192,128]{1,0:T(8,128)S(1)} %get-tuple-element.20), channel_id=1, source_target_pairs={{29,0},{30,1},{31,2},{28,3},{1,4},{2,5},{3,6},{0,7},{5,8},{6,9},{7... | collective-permute-start | bytes 294920 | tf_op jit(solution)/shard_map/ppermute | solution.py:588
  24.9 3.3 %collective-permute-start.6 = (f32[192,128]{1,0:T(8,128)S(1)}, f32[192,128]{1,0:T(8,128)S(1)}, u32[]{:S(2)}, u32[]{:S(2)}) collective-permute-start(f32[192,128]{1,0:T(8,128)S(1)} %get-tuple-element.22), channel_id=1, source_target_pairs={{4,0},{5,1},{6,2},{7,3},{8,4},{9,5},{10,6},{11,7},{12,8},{13,9},{1... | collective-permute-start | bytes 294920 | tf_op jit(solution)/shard_map/ppermute | solution.py:588
  28.2 2.4 %collective-permute-start.4 = (f32[192,128]{1,0:T(8,128)S(1)}, f32[192,128]{1,0:T(8,128)S(1)}, u32[]{:S(2)}, u32[]{:S(2)}) collective-permute-start(f32[192,128]{1,0:T(8,128)S(1)} %get-tuple-element.23), channel_id=1, source_target_pairs={{1,0},{2,1},{3,2},{0,3},{5,4},{6,5},{7,6},{4,7},{9,8},{10,9},{11,1... | collective-permute-start | bytes 294920 | tf_op jit(solution)/shard_map/ppermute | solution.py:588
  30.6 0.0 copy-start.9
  30.6 3.5 %collective-permute-start.1 = (f32[192,128]{1,0:T(8,128)S(1)}, f32[192,128]{1,0:T(8,128)S(1)}, u32[]{:S(2)}, u32[]{:S(2)}) collective-permute-start(f32[192,128]{1,0:T(8,128)S(1)} %get-tuple-element.25), channel_id=1, source_target_pairs={{28,0},{29,1},{30,2},{31,3},{0,4},{1,5},{2,6},{3,7},{4,8},{5,9},{6... | collective-permute-start | bytes 294920 | tf_op jit(solution)/shard_map/ppermute | solution.py:588
  34.2 7.0 %volume.1.start_ref = f32[2,8,8,8,512]{4,3,2,1,0:T(8,128)S(1)} custom-call(f32[2,8,8,8,512]{4,3,2,1,0:T(8,128)S(1)} %copy-done, f32[2,8,8,8,512]{4,3,2,1,0:T(8,128)S(1)} %copy-done.2, f32[6,8,8,8,512]{4,3,2,1,0:T(8,128)S(1)} %copy-done.1, bf16[256,256]{1,0:T(8,128)(2,1)S(1)} %copy-done.6, bf16[256,256]{1,0:T(8,128)(2,1)S(1)} %copy-done.5, ...), custom_call_target="tpu_custom_call" | custom-call | flops 1000000000 | bytes 13000000 | tf_op jit(solution)/shard_map/volume/pallas_call | solution.py:330
  41.3 6.7 %residuals.1 = (f32[2,8,8,8,512]{4,3,2,1,0:T(8,128)}, f32[16,256]{1,0:T(8,128)S(1)}, f32[6144,128]{1,0:T(8,128)S(1)}) custom-call(s32[576]{0:T(1024)S(1)} %get-tuple-element.17.to_ref, s32[5,1,576]{2,1,0:T(1,128)S(1)} %copy-done.9, f32[1728,128]{1,0:T(8,128)S(1)} %get-tuple-element.11.own_ref, ...), custom_call_target="tpu_custom_call", output_to_operand_aliasing={{2}: (12, {})} | custom-call | flops 100000000 | bytes 9000000 | tf_op jit(solution)/shard_map/residuals/pallas_call | solution.py:483
  48.0 1.0 %collective-permute-start.9 = (f32[16,256]{1,0:T(8,128)S(1)}, f32[16,256]{1,0:T(8,128)S(1)}, u32[]{:S(2)}, u32[]{:S(2)}) collective-permute-start(f32[16,256]{1,0:T(8,128)S(1)} %get-tuple-element.15.refs_0_), channel_id=1, source_target_pairs={{0,2},{1,3},{2,0},{3,1},{4,6},{5,7},{6,4},{7,5},{8,10},{9,11},{10,... | collective-permute-start | bytes 49160 | tf_op jit(solution)/shard_map/ppermute | solution.py:631
  49.0 0.2 collective-permute-start.8
  49.2 0.2 collective-permute-done.10.refs_3_
  49.4 2.3 %collective-permute-done.9.refs_2_ = f32[16,256]{1,0:T(8,128)S(1)} collective-permute-done((f32[16,256]{1,0:T(8,128)S(1)}, f32[16,256]{1,0:T(8,128)S(1)}, u32[]{:S(2)}, u32[]{:S(2)}) %collective-permute-start.9) | collective-permute-done | bytes 16416 | tf_op jit(solution)/shard_map/ppermute | solution.py:631
  51.7 0.4 collective-permute-done.8.refs_1_
  52.2 2.5 %correct.1 = f32[2,8,8,8,512]{4,3,2,1,0:T(8,128)} custom-call(f32[2,8,8,8,512]{4,3,2,1,0:T(8,128)S(1)} %copy-done, f32[8,8,256]{2,1,0:T(8,128)S(1)} %copy-done.7, s32[1,512]{1,0:T(1,128)S(1)} %bitcast.6, f32[16,256]{1,0:T(8,128)S(1)} %get-tuple-element.15.refs_0_, f32[16,256]{1,0:T(8,128)S(1)} %collective-permute-done.8.refs_1_, ...), custom_call_target="tpu_custom_call" | custom-call | flops 100000000 | bytes 5000000 | tf_op jit(solution)/shard_map/correct/pallas_call | solution.py:559
  (30 shorter events, 0.1 us)
Async XLA Ops:
  0.6 6.2 %copy-start.8 = (s32[5,512]{1,0:T(8,128)S(1)}, s32[5,512]{1,0:T(8,128)}, u32[]{:S(2)}) copy-start(s32[5,512]{1,0:T(8,128)} %code_ref.1) | copy-start | bytes 30724
  2.3 31.8 %copy-start.2 = (f32[2,8,8,8,512]{4,3,2,1,0:T(8,128)S(1)}, f32[2,8,8,8,512]{4,3,2,1,0:T(8,128)}, u32[]{:S(2)}) copy-start(f32[2,8,8,8,512]{4,3,2,1,0:T(8,128)} %rs_ref) | copy-start | bytes 6291460
  6.8 27.3 %copy-start = (f32[2,8,8,8,512]{4,3,2,1,0:T(8,128)S(1)}, f32[2,8,8,8,512]{4,3,2,1,0:T(8,128)}, u32[]{:S(2)}) copy-start(f32[2,8,8,8,512]{4,3,2,1,0:T(8,128)} %p_ref.5) | copy-start | bytes 6291460
  6.9 27.3 %copy-start.1 = (f32[6,8,8,8,512]{4,3,2,1,0:T(8,128)S(1)}, f32[6,8,8,8,512]{4,3,2,1,0:T(8,128)}, u32[]{:S(2)}) copy-start(f32[6,8,8,8,512]{4,3,2,1,0:T(8,128)} %g_ref.1) | copy-start | bytes 18874372
  6.9 27.2 %copy-start.3 = (bf16[256,256]{1,0:T(8,128)(2,1)S(1)}, bf16[256,256]{1,0:T(8,128)(2,1)}, u32[]{:S(2)}) copy-start(bf16[256,256]{1,0:T(8,128)(2,1)} %constant.23.tl_ref) | copy-start | bytes 393220
  6.9 27.2 %copy-start.4 = (bf16[256,256]{1,0:T(8,128)(2,1)S(1)}, bf16[256,256]{1,0:T(8,128)(2,1)}, u32[]{:S(2)}) copy-start(bf16[256,256]{1,0:T(8,128)(2,1)} %constant.20.th_ref) | copy-start | bytes 393220
  6.9 27.2 %copy-start.5 = (bf16[256,256]{1,0:T(8,128)(2,1)S(1)}, bf16[256,256]{1,0:T(8,128)(2,1)}, u32[]{:S(2)}) copy-start(bf16[256,256]{1,0:T(8,128)(2,1)} %constant.19.dl_ref) | copy-start | bytes 393220
  6.9 27.2 %copy-start.6 = (bf16[256,256]{1,0:T(8,128)(2,1)S(1)}, bf16[256,256]{1,0:T(8,128)(2,1)}, u32[]{:S(2)}) copy-start(bf16[256,256]{1,0:T(8,128)(2,1)} %constant.16.dh_ref) | copy-start | bytes 393220
  15.8 12.4 %collective-permute-start.7 = (f32[192,128]{1,0:T(8,128)S(1)}, f32[192,128]{1,0:T(8,128)S(1)}, u32[]{:S(2)}, u32[]{:S(2)}) collective-permute-start(f32[192,128]{1,0:T(8,128)S(1)} %get-tuple-element.18), channel_id=1, source_target_pairs={{5,0},{6,1},{7,2},{4,3},{9,4},{10,5},{11,6},{8,7},{13,8},{14,9},{1... | collective-permute-start | bytes 294920 | tf_op jit(solution)/shard_map/ppermute | solution.py:588
  22.3 8.4 %collective-permute-start.5 = (f32[192,128]{1,0:T(8,128)S(1)}, f32[192,128]{1,0:T(8,128)S(1)}, u32[]{:S(2)}, u32[]{:S(2)}) collective-permute-start(f32[192,128]{1,0:T(8,128)S(1)} %get-tuple-element.19), channel_id=1, source_target_pairs={{7,0},{4,1},{5,2},{6,3},{11,4},{8,5},{9,6},{10,7},{15,8},{12,9},{1... | collective-permute-start | bytes 294920 | tf_op jit(solution)/shard_map/ppermute | solution.py:588
  22.3 8.4 %collective-permute-start.2 = (f32[192,128]{1,0:T(8,128)S(1)}, f32[192,128]{1,0:T(8,128)S(1)}, u32[]{:S(2)}, u32[]{:S(2)}) collective-permute-start(f32[192,128]{1,0:T(8,128)S(1)} %get-tuple-element.20), channel_id=1, source_target_pairs={{29,0},{30,1},{31,2},{28,3},{1,4},{2,5},{3,6},{0,7},{5,8},{6,9},{7... | collective-permute-start | bytes 294920 | tf_op jit(solution)/shard_map/ppermute | solution.py:588
  24.9 16.3 %collective-permute-start = (f32[192,128]{1,0:T(8,128)S(1)}, f32[192,128]{1,0:T(8,128)S(1)}, u32[]{:S(2)}, u32[]{:S(2)}) collective-permute-start(f32[192,128]{1,0:T(8,128)S(1)} %get-tuple-element.21), channel_id=1, source_target_pairs={{31,0},{28,1},{29,2},{30,3},{3,4},{0,5},{1,6},{2,7},{7,8},{4,9},{5... | collective-permute-start | bytes 294920 | tf_op jit(solution)/shard_map/ppermute | solution.py:588
  24.9 16.3 %collective-permute-start.6 = (f32[192,128]{1,0:T(8,128)S(1)}, f32[192,128]{1,0:T(8,128)S(1)}, u32[]{:S(2)}, u32[]{:S(2)}) collective-permute-start(f32[192,128]{1,0:T(8,128)S(1)} %get-tuple-element.22), channel_id=1, source_target_pairs={{4,0},{5,1},{6,2},{7,3},{8,4},{9,5},{10,6},{11,7},{12,8},{13,9},{1... | collective-permute-start | bytes 294920 | tf_op jit(solution)/shard_map/ppermute | solution.py:588
  28.2 13.0 %collective-permute-start.4 = (f32[192,128]{1,0:T(8,128)S(1)}, f32[192,128]{1,0:T(8,128)S(1)}, u32[]{:S(2)}, u32[]{:S(2)}) collective-permute-start(f32[192,128]{1,0:T(8,128)S(1)} %get-tuple-element.23), channel_id=1, source_target_pairs={{1,0},{2,1},{3,2},{0,3},{5,4},{6,5},{7,6},{4,7},{9,8},{10,9},{11,1... | collective-permute-start | bytes 294920 | tf_op jit(solution)/shard_map/ppermute | solution.py:588
  30.6 10.6 %collective-permute-start.3 = (f32[192,128]{1,0:T(8,128)S(1)}, f32[192,128]{1,0:T(8,128)S(1)}, u32[]{:S(2)}, u32[]{:S(2)}) collective-permute-start(f32[192,128]{1,0:T(8,128)S(1)} %get-tuple-element.24), channel_id=1, source_target_pairs={{3,0},{0,1},{1,2},{2,3},{7,4},{4,5},{5,6},{6,7},{11,8},{8,9},{9,10... | collective-permute-start | bytes 294920 | tf_op jit(solution)/shard_map/ppermute | solution.py:588
  30.6 10.6 %copy-start.9 = (s32[5,1,576]{2,1,0:T(1,128)S(1)}, s32[5,1,576]{2,1,0:T(1,128)}, u32[]{:S(2)}) copy-start(s32[5,1,576]{2,1,0:T(1,128)} %slots_ref.1) | copy-start | bytes 34564
  30.6 10.6 %copy-start.10 = (s32[512]{0:T(512)S(1)}, s32[512]{0:T(512)}, u32[]{:S(2)}) copy-start(s32[512]{0:T(512)} %param.20) | copy-start | bytes 6148
  30.6 10.6 %collective-permute-start.1 = (f32[192,128]{1,0:T(8,128)S(1)}, f32[192,128]{1,0:T(8,128)S(1)}, u32[]{:S(2)}, u32[]{:S(2)}) collective-permute-start(f32[192,128]{1,0:T(8,128)S(1)} %get-tuple-element.25), channel_id=1, source_target_pairs={{28,0},{29,1},{30,2},{31,3},{0,4},{1,5},{2,6},{3,7},{4,8},{5,9},{6... | collective-permute-start | bytes 294920 | tf_op jit(solution)/shard_map/ppermute | solution.py:588
  41.3 10.9 %copy-start.7 = (f32[8,8,256]{2,1,0:T(8,128)S(1)}, f32[8,8,256]{2,1,0:T(8,128)}, u32[]{:S(2)}) copy-start(f32[8,8,256]{2,1,0:T(8,128)} %inverse_ref.1) | copy-start | bytes 196612
  48.0 1.4 %collective-permute-start.10 = (f32[16,256]{1,0:T(8,128)S(1)}, f32[16,256]{1,0:T(8,128)S(1)}, u32[]{:S(2)}, u32[]{:S(2)}) collective-permute-start(f32[16,256]{1,0:T(8,128)S(1)} %get-tuple-element.15.refs_0_), channel_id=1, source_target_pairs={{0,3},{1,0},{2,1},{3,2},{4,7},{5,4},{6,5},{7,6},{8,11},{9,8},{10,9... | collective-permute-start | bytes 49160 | tf_op jit(solution)/shard_map/ppermute | solution.py:631
  48.0 3.7 %collective-permute-start.9 = (f32[16,256]{1,0:T(8,128)S(1)}, f32[16,256]{1,0:T(8,128)S(1)}, u32[]{:S(2)}, u32[]{:S(2)}) collective-permute-start(f32[16,256]{1,0:T(8,128)S(1)} %get-tuple-element.15.refs_0_), channel_id=1, source_target_pairs={{0,2},{1,3},{2,0},{3,1},{4,6},{5,7},{6,4},{7,5},{8,10},{9,11},{10,... | collective-permute-start | bytes 49160 | tf_op jit(solution)/shard_map/ppermute | solution.py:631
  49.0 3.2 %collective-permute-start.8 = (f32[16,256]{1,0:T(8,128)S(1)}, f32[16,256]{1,0:T(8,128)S(1)}, u32[]{:S(2)}, u32[]{:S(2)}) collective-permute-start(f32[16,256]{1,0:T(8,128)S(1)} %get-tuple-element.15.refs_0_), channel_id=1, source_target_pairs={{0,1},{1,2},{2,3},{3,0},{4,5},{5,6},{6,7},{7,4},{8,9},{9,10},{10,1... | collective-permute-start | bytes 49160 | tf_op jit(solution)/shard_map/ppermute | solution.py:631

commit v2 on v1

--- a/solution.py
+++ b/solution.py
@@ -168,7 +168,7 @@
         ],
         out_specs=(whole, whole),
         scratch_shapes=[pltpu.VMEM((fields, 6, 2 * face_size, LANES), jnp.float32)],
-        compiler_params=pltpu.CompilerParams(vmem_limit_bytes=16 * MIB),
+        compiler_params=pltpu.CompilerParams(vmem_limit_bytes=6 * MIB),
         cost_estimate=pl.CostEstimate(flops=10**7, bytes_accessed=9 * 10**6, transcendentals=0),
         name="traces",
     )(rows, pressure, face_weight, face_metric)
@@ -199,6 +199,88 @@
     return [ref[pl.ds(start * (fields + 1) + f, rows, stride=fields + 1), :] for f in range(fields + 1)]
 
 
+def cross_flags(slots_ref, flags):
+    slot_total = slots_ref.shape[-1]
+    code = jnp.where(slots_ref[3] > 0, slots_ref[4], inverse_code(slots_ref[4]))
+    row = (code + 8 * slots_ref[2]).astype(jnp.float32)
+    row = jnp.concatenate([row, jnp.zeros((1, flags.shape[0] - slot_total), jnp.float32)], axis=1)
+    for at in range(flags.shape[0] // LANES):
+        lanes = slice(at * LANES, (at + 1) * LANES)
+        flags[lanes, :] = spread_down(row[:, lanes]).astype(jnp.int32)
+
+
+def cross_rows(sources, own_ref, flags, result, cap, fields, nodes):
+    rows = min(cap, 64)
+    for k, (ref, place) in sources.items():
+        for part in range(cap // rows):
+            first = k * cap + part * rows
+            flag = flags[first : first + rows, :]
+            values = flux_rows(
+                pieces(own_ref, first, rows, fields),
+                pieces(ref, place * cap + part * rows, rows, fields),
+                lane_order(flag, nodes),
+                fields,
+                nodes,
+            )
+            for f in range(fields):
+                result[pl.ds(first * fields + f, rows, stride=fields), :] = jnp.where(flag >= 8, values[f], 0.0)
+
+
+def put_blocks(blocks, to_ref, result, rows_ref, cap, fields):
+    group_size = 16
+    for k in blocks:
+
+        def put(group, carry, k=k):
+            for u in range(group_size):
+                at = k * cap + group * group_size + u
+                rows_ref[pl.ds(to_ref[at], fields), :] = result[pl.ds(at * fields, fields), :]
+            return carry
+
+        lax.fori_loop(0, cap // group_size, put, 0)
+
+
+def three_parts(value):
+    head, rest = split(value)
+    return head, rest, (value - head.astype(jnp.float32) - rest.astype(jnp.float32)).astype(jnp.bfloat16)
+
+
+def cell_mask(map_row, cells):
+    place = lax.broadcasted_iota(jnp.int32, (cells, map_row.shape[1]), 0)
+    return (place == map_row).astype(jnp.bfloat16)
+
+
+def restrict_nodes(read, modes, at, ramp, nodes):
+    ramp_rows = column(list(ramp))
+    spots = [[None, None], [None, None]]
+    for i in range(nodes):
+        pencil = [read(i, j) for j in range(nodes)]
+        for b, part in enumerate((weighted([1.0] * nodes, pencil), weighted(list(ramp), pencil))):
+            spots[0][b] = part if i == 0 else spots[0][b] + part
+            if float(ramp[i]) != 0.0:
+                extra = float(ramp[i]) * part
+                spots[1][b] = extra if spots[1][b] is None else spots[1][b] + extra
+    for a in range(2):
+        sides = [spots[1][b] if a == 1 else spots[0][b] - spots[1][b] for b in range(2)]
+        for b, part in enumerate((sides[0] - sides[1], sides[1])):
+            whole = jnp.sum(part, axis=0, keepdims=True)
+            up = jnp.sum(part * ramp_rows, axis=0, keepdims=True)
+            modes[at + 4 * a + 2 * b : at + 4 * a + 2 * b + 1, :] = whole - up
+            modes[at + 4 * a + 2 * b + 1 : at + 4 * a + 2 * b + 2, :] = up
+
+
+def face_modes(derivative, prolong):
+    nodes = derivative.shape[0]
+    ends = (0, nodes - 1)
+    table = np.zeros((6, 2, nodes, nodes, 2, 2, 2))
+    for axis in range(3):
+        for side, end in enumerate(ends):
+            slope = (-derivative[0] if side == 0 else derivative[end]) @ prolong
+            for which, weights in enumerate((prolong[end], slope)):
+                grid = np.einsum("x,py,qz->pqxyz", weights, prolong, prolong)
+                table[2 * axis + side, which] = np.moveaxis(grid, 2, 2 + axis)
+    return table.reshape(6, 2 * nodes * nodes, 8)
+
+
 def local_kernel(from_ref, to_ref, code_ref, table_ref, out_ref, picked, order, result, *, fields, nodes):
     total = from_ref.shape[0]
     count = total // 2
@@ -218,7 +300,7 @@
         column_code = spread_down(code.astype(jnp.float32)).astype(jnp.int32)
         order[at * LANES : (at + 1) * LANES, :] = lane_order(column_code, nodes)
         order[count + at * LANES : count + (at + 1) * LANES, :] = lane_order(inverse_code(column_code), nodes)
-    rows = 32
+    rows = min(count, 256)
 
     def flux(at, carry):
         start = at * rows
@@ -259,143 +341,192 @@
             pltpu.VMEM((total, LANES), jnp.int32),
             pltpu.VMEM((total * fields, LANES), jnp.float32),
         ],
-        compiler_params=pltpu.CompilerParams(vmem_limit_bytes=16 * MIB),
+        compiler_params=pltpu.CompilerParams(vmem_limit_bytes=8 * MIB),
         cost_estimate=pl.CostEstimate(flops=10**7, bytes_accessed=12 * 10**6, transcendentals=0),
         name="local_fluxes",
     )(rows_from, rows_to, local_pairs, table)
 
 
-def volume_kernel(p_ref, rs_ref, g_ref, dh_ref, dl_ref, th_ref, tl_ref, out_ref, one, two, three, *, derivative):
+def volume_kernel(
+    p_ref, rs_ref, g_ref, fwd_ref, back_ref, map_ref, *refs, derivative, ramp, earlier
+):
+    base_ref = refs[1] if earlier else None
+    out_ref, sums_ref, one, two, three, four, modes = refs[2:] if earlier else refs
     fields, nodes = p_ref.shape[0], p_ref.shape[1]
     rows = nodes**3
-    block = dh_ref.shape[0]
+    block = back_ref.shape[0]
+    planes = block // (nodes * nodes)
     back = derivative.T
 
-    def along_last(read, write, head_ref, tail_ref):
-        for at in range(rows // block):
-            value = jnp.concatenate([read(f)[at * block : (at + 1) * block] for f in range(fields)], axis=1)
-            head, tail = split(value)
-            result = mxu(head_ref[...], head) + mxu(head_ref[...], tail) + mxu(tail_ref[...], head)
-            for f in range(fields):
-                write(f, at, result[:, f * LANES : (f + 1) * LANES])
-
-    def put_three(f, at, value):
-        three[f, at * (block // 64) : (at + 1) * (block // 64)] = value.reshape(block // 64, nodes, nodes, LANES)
-
-    along_last(lambda f: p_ref[f].reshape(rows, LANES), put_three, dh_ref, dl_ref)
+    def both(at, read):
+        return jnp.concatenate([read(f).reshape(rows, LANES)[at * block : (at + 1) * block] for f in range(fields)], axis=1)
+
+    for at in range(rows // block):
+        head, tail = split(both(at, lambda f: p_ref[f]))
+        slopes = mxu(fwd_ref[...], jnp.concatenate([head, tail, head], axis=0))
+        for f in range(fields):
+            lanes = slice(f * LANES, (f + 1) * LANES)
+            here = slice(at * planes, (at + 1) * planes)
+            two[f, here] = slopes[:block, lanes].reshape(planes, nodes, nodes, LANES)
+            three[f, here] = slopes[block:, lanes].reshape(planes, nodes, nodes, LANES)
     for f in range(fields):
         for j in range(nodes):
             slopes = derive(derivative, [p_ref[f, k, j] for k in range(nodes)])
             for i in range(nodes):
                 one[f, i, j] = slopes[i]
     for i in range(nodes):
+        for j in range(nodes):
+            xx, yy, zz, xy, xz, yz = [g_ref[c, i, j] for c in range(6)]
+            for f in range(fields):
+                s1, s2, s3 = one[f, i, j], two[f, i, j], three[f, i, j]
+                one[f, i, j] = xx * s1 + xy * s2 + xz * s3
+                two[f, i, j] = xy * s1 + yy * s2 + yz * s3
+                three[f, i, j] = xz * s1 + yz * s2 + zz * s3
+    for at in range(rows // block):
+        head2, tail2 = split(both(at, lambda f: two[f]))
+        head3, tail3 = split(both(at, lambda f: three[f]))
+        sums = mxu(back_ref[...], jnp.concatenate([head2, tail2, head2, head3, tail3, head3], axis=0))
         for f in range(fields):
-            slopes = derive(derivative, [p_ref[f, i, k] for k in range(nodes)])
-            flux = []
-            for j in range(nodes):
-                s1, s2, s3 = one[f, i, j], slopes[j], three[f, i, j]
-                xx, yy, zz, xy, xz, yz = [g_ref[c, i, j] for c in range(6)]
-                one[f, i, j] = xx * s1 + xy * s2 + xz * s3
-                flux.append(xy * s1 + yy * s2 + yz * s3)
-                three[f, i, j] = xz * s1 + yz * s2 + zz * s3
-            for j, value in enumerate(derive(back, flux)):
-                two[f, i, j] = rs_ref[f, i, j] - value
-
-    def put_two(f, at, value):
-        part = value.reshape(block // 64, nodes, nodes, LANES)
-        rng = slice(at * (block // 64), (at + 1) * (block // 64))
-        two[f, rng] = two[f, rng] - part
-
-    along_last(lambda f: three[f].reshape(rows, LANES), put_two, th_ref, tl_ref)
+            lanes = slice(f * LANES, (f + 1) * LANES)
+            here = slice(at * planes, (at + 1) * planes)
+            four[f, here] = rs_ref[f, here] - sums[:, lanes].reshape(planes, nodes, nodes, LANES)
     for f in range(fields):
         for j in range(nodes):
             sums = derive(back, [one[f, k, j] for k in range(nodes)])
             for i in range(nodes):
-                out_ref[f, i, j] = two[f, i, j] - sums[i]
-
-
-def volume(pressure, right_side, geometry, derivative):
-    fields, nodes, elems = pressure.shape[0], pressure.shape[1], pressure.shape[-1]
+                out_ref[f, i, j] = four[f, i, j] - sums[i]
+        restrict_nodes(lambda i, j, f=f: out_ref[f, i, j], modes, f * 8, ramp, nodes)
+    hot = cell_mask(map_ref[...], sums_ref.shape[1])
+    across = (((1,), (1,)), ((), ()))
+    head, rest, tail = three_parts(modes[...])
+    total = mxu(head, hot, across) + mxu(rest, hot, across) + mxu(tail, hot, across)
+
+    @pl.when(pl.program_id(0) == 0)
+    def _():
+        sums_ref[...] = base_ref[...] + total if earlier else total
+
+    @pl.when(pl.program_id(0) > 0)
+    def _():
+        sums_ref[...] += total
+
+
+def volume(pressure, right_side, geometry, cell_row, cells, derivative, ramp, first, steps, earlier=()):
+    fields, nodes = pressure.shape[0], pressure.shape[1]
     block = 256
-    spread = np.kron(np.eye(block // nodes), derivative)
+    planes = block // (nodes * nodes)
+    eye = np.eye(nodes)
+    middle = np.kron(np.eye(planes), np.kron(derivative, eye))
+    minor = np.kron(np.eye(planes), np.kron(eye, derivative))
 
     def parts(matrix):
-        head = jnp.asarray(matrix, jnp.float32).astype(jnp.bfloat16)
-        tail = (jnp.asarray(matrix, jnp.float32) - head.astype(jnp.float32)).astype(jnp.bfloat16)
-        return head, tail
-
+        whole = jnp.asarray(matrix, jnp.float32)
+        head = whole.astype(jnp.bfloat16)
+        return head, (whole - head.astype(jnp.float32)).astype(jnp.bfloat16)
+
+    head, tail = parts(np.concatenate([middle, minor], axis=0))
+    forward = jnp.concatenate([head, head, tail], axis=1)
+    (head2, tail2), (head3, tail3) = parts(middle.T), parts(minor.T)
+    backward = jnp.concatenate([head2, head2, tail2, head3, head3, tail3], axis=1)
     whole = (fields, nodes, nodes, nodes, LANES)
-    field_spec = pl.BlockSpec(whole, lambda s: (0, 0, 0, 0, s))
-    table_spec = pl.BlockSpec((block, block), lambda s: (0, 0))
+    field_spec = pl.BlockSpec(whole, lambda s: (0, 0, 0, 0, s + first))
+    vmem = pl.BlockSpec(memory_space=pltpu.VMEM)
     return pl.pallas_call(
-        functools.partial(volume_kernel, derivative=derivative),
-        out_shape=jax.ShapeDtypeStruct(pressure.shape, jnp.float32),
-        grid=(elems // LANES,),
+        functools.partial(volume_kernel, derivative=derivative, ramp=ramp, earlier=bool(earlier)),
+        out_shape=(
+            jax.ShapeDtypeStruct(pressure.shape, jnp.float32),
+            jax.ShapeDtypeStruct((fields * 8, cells), jnp.float32),
+        ),
+        grid=(steps,),
         in_specs=[
             field_spec,
             field_spec,
-            pl.BlockSpec((6, nodes, nodes, nodes, LANES), lambda s: (0, 0, 0, 0, s)),
-            table_spec,
-            table_spec,
-            table_spec,
-            table_spec,
-        ],
-        out_specs=field_spec,
-        scratch_shapes=[pltpu.VMEM(whole, jnp.float32)] * 3,
-        compiler_params=pltpu.CompilerParams(vmem_limit_bytes=16 * MIB),
+            pl.BlockSpec((6, nodes, nodes, nodes, LANES), lambda s: (0, 0, 0, 0, s + first)),
+            vmem,
+            vmem,
+            pl.BlockSpec((1, LANES), lambda s: (0, s + first)),
+        ]
+        + [pl.BlockSpec(memory_space=pl.ANY), vmem][: len(earlier)],
+        out_specs=(field_spec, vmem),
+        scratch_shapes=[pltpu.VMEM(whole, jnp.float32)] * 4 + [pltpu.VMEM((fields * 8, LANES), jnp.float32)],
+        input_output_aliases={6: 0} if earlier else {},
+        compiler_params=pltpu.CompilerParams(vmem_limit_bytes=14 * MIB),
         cost_estimate=pl.CostEstimate(flops=10**9, bytes_accessed=13 * 10**6, transcendentals=0),
-        name="volume",
-    )(pressure, right_side, geometry, *parts(spread), *parts(spread.T))
-
-
-def residual_kernel(
-    to_ref, slots_ref, own_ref, got0, got1, got2, got3, got4, got5, got6, got7, start_ref, rows_in, map_ref,
-    res_ref, sums_ref, rows_ref, order, result, nat, restricted,
-    *, derivative, prolong, elems, fields, nodes,
+    )(pressure, right_side, geometry, forward, backward, cell_row, *earlier)
+
+
+def cross_kernel(
+    to_ref, slots_ref, own_ref, far_up, far_down, up_ref, down_ref, right_ref, left_ref, rows_in, map_ref, base_ref,
+    table_ref,
+    rows_ref, sums_ref, order, result, packed, *, elems, fields, nodes,
 ):
-    step = pl.program_id(0)
     slot_total = to_ref.shape[0]
     cap = slot_total // 9
+    del rows_in
+    sources = {8: (far_up, 0), 6: (far_up, 1), 2: (far_down, 0), 0: (far_down, 1)}
+    sources.update({1: (down_ref, 0), 3: (left_ref, 0), 5: (right_ref, 0), 7: (up_ref, 0)})
+    cross_flags(slots_ref, order)
+    cross_rows(sources, own_ref, order, result, cap, fields, nodes)
+    put_blocks(sources, to_ref, result, rows_ref, cap, fields)
+    cells = base_ref.shape[1]
+    size = table_ref.shape[0] // 2
+    block = min(elems, 256)
+    for at in range(elems // block):
+        parts = [
+            split(rows_ref[pl.ds((face * elems + at * block) * fields + f, block, stride=fields), :])
+            for f in range(fields)
+            for face in range(6)
+        ]
+        heads = jnp.concatenate([head for head, _ in parts], axis=1)
+        tails = jnp.concatenate([tail for _, tail in parts], axis=1)
+        packed[at * block : (at + 1) * block, :] = (
+            mxu(heads, table_ref[:size]) + mxu(tails, table_ref[:size]) + mxu(heads, table_ref[size:])
+        )
+    hot = cell_mask(map_ref[...], cells)
+    head, rest, tail = three_parts(packed[...])
+    total = mxu(hot, head) + mxu(hot, rest) + mxu(hot, tail)
+    sums_ref[...] = base_ref[...] - total.T[: base_ref.shape[0]]
+
+
+def cross_sums(rows_to, slots, own, far, local_rows, cell_row, base, derivative, prolong, nodes):
+    elems = cell_row.shape[1]
+    fields = base.shape[0] // 8
+    slot_total = rows_to.shape[0]
+    padded = -(-slot_total // LANES) * LANES
+    table = face_modes(derivative, prolong).reshape(-1, 8)
+    wide = np.zeros((fields, table.shape[0], LANES))
+    for f in range(fields):
+        wide[f, :, f * 8 : f * 8 + 8] = table
+    wide = jnp.asarray(wide.reshape(-1, LANES), jnp.float32)
+    head = wide.astype(jnp.bfloat16)
+    both = jnp.concatenate([head, (wide - head.astype(jnp.float32)).astype(jnp.bfloat16)], axis=0)
+    vmem = pl.BlockSpec(memory_space=pltpu.VMEM)
+    return pl.pallas_call(
+        functools.partial(cross_kernel, elems=elems, fields=fields, nodes=nodes),
+        out_shape=(
+            jax.ShapeDtypeStruct(local_rows.shape, jnp.float32),
+            jax.ShapeDtypeStruct(base.shape, jnp.float32),
+        ),
+        in_specs=[pl.BlockSpec(memory_space=pltpu.SMEM)] + [vmem] * 12,
+        out_specs=(vmem, vmem),
+        scratch_shapes=[
+            pltpu.VMEM((padded, LANES), jnp.int32),
+            pltpu.VMEM((slot_total * fields, LANES), jnp.float32),
+            pltpu.VMEM((elems, LANES), jnp.float32),
+        ],
+        input_output_aliases={9: 0},
+        compiler_params=pltpu.CompilerParams(vmem_limit_bytes=8 * MIB),
+        cost_estimate=pl.CostEstimate(flops=10**8, bytes_accessed=4 * 10**6, transcendentals=0),
+        name="cross_sums",
+    )(rows_to, slots, own, *far, local_rows, cell_row, base, both)
+
+
+def lift_kernel(start_ref, rows_ref, *refs, derivative, elems, first):
+    res_ref, nat = refs[-2:]
+    fields, nodes = res_ref.shape[0], res_ref.shape[1]
     half = nodes * nodes
     last = nodes - 1
-    del rows_in
-
-    @pl.when(step == 0)
-    def _():
-        source = dict(zip((0, 1, 2, 3, 5, 6, 7, 8), (got0, got1, got2, got3, got4, got5, got6, got7)))
-        code = jnp.where(slots_ref[3] > 0, slots_ref[4], inverse_code(slots_ref[4]))
-        flags = (code + 8 * slots_ref[2]).astype(jnp.float32)
-        flags = jnp.concatenate([flags, jnp.zeros((1, order.shape[0] - slot_total), jnp.float32)], axis=1)
-        for at in range(order.shape[0] // LANES):
-            order[at * LANES : (at + 1) * LANES, :] = spread_down(flags[:, at * LANES : (at + 1) * LANES]).astype(
-                jnp.int32
-            )
-        result[4 * cap * fields : 5 * cap * fields, :] = jnp.zeros((cap * fields, LANES), jnp.float32)
-        rows = min(cap, 32)
-        for k, ref in source.items():
-            for part in range(cap // rows):
-                first = k * cap + part * rows
-                flag = order[first : first + rows, :]
-                values = flux_rows(
-                    pieces(own_ref, first, rows, fields),
-                    pieces(ref, part * rows, rows, fields),
-                    lane_order(flag, nodes),
-                    fields,
-                    nodes,
-                )
-                for f in range(fields):
-                    result[pl.ds(first * fields + f, rows, stride=fields), :] = jnp.where(flag >= 8, values[f], 0.0)
-        group_size = 16
-
-        def put(group, carry):
-            for u in range(group_size):
-                k = group * group_size + u
-                rows_ref[pl.ds(to_ref[k], fields), :] = result[pl.ds(k * fields, fields), :]
-            return carry
-
-        lax.fori_loop(0, slot_total // group_size, put, 0)
-
-    base = step * LANES
+    base = (pl.program_id(0) + first) * LANES
+    here = pl.ds(pl.multiple_of(base, LANES), LANES)
     for f in range(fields):
         for face in range(6):
             nat[f, face] = rows_ref[pl.ds((face * elems + base) * fields + f, LANES, stride=fields), :].T
@@ -403,14 +534,10 @@
     value_high = column([0.0] * last + [1.0])
     lift_low = column(list(-derivative[0]))
     lift_high = column(list(derivative[last]))
-    ramp = prolong[:, 1]
-    ramp_rows = column(list(ramp))
     for f in range(fields):
-        spots = [[None, None], [None, None]]
         for i in range(nodes):
-            pencil = []
             for j in range(nodes):
-                value = start_ref[f, i, j]
+                value = start_ref[f, i, j, :, here]
                 at_j = slice(j * nodes, (j + 1) * nodes)
                 at_i = slice(i * nodes, (i + 1) * nodes)
                 low_j = slice(half + j * nodes, half + (j + 1) * nodes)
@@ -433,78 +560,22 @@
                 value = value - value_high * nat[f, 5, node : node + 1]
                 value = value - lift_high * nat[f, 5, half + node : half + node + 1]
                 res_ref[f, i, j] = value
-                pencil.append(value)
-            total = weighted([1.0] * nodes, pencil)
-            sloped = weighted(list(ramp), pencil)
-            for b, part in enumerate((total, sloped)):
-                spots[0][b] = part if i == 0 else spots[0][b] + part
-                extra = float(ramp[i]) * part
-                if float(ramp[i]) != 0.0:
-                    spots[1][b] = extra if spots[1][b] is None else spots[1][b] + extra
-        for a in range(2):
-            for b in range(2):
-                if a == 0:
-                    part = spots[0][b] - spots[1][b]
-                    other = spots[0][1] - spots[1][1]
-                else:
-                    part = spots[1][b]
-                    other = spots[1][1]
-                if b == 0:
-                    part = part - other
-                whole = jnp.sum(part, axis=0, keepdims=True)
-                up = jnp.sum(part * ramp_rows, axis=0, keepdims=True)
-                at = f * 8 + 4 * a + 2 * b
-                restricted[at : at + 1, :] = whole - up
-                restricted[at + 1 : at + 2, :] = up
-
-    cells = sums_ref.shape[1]
-    hot = (lax.broadcasted_iota(jnp.int32, (cells, LANES), 0) == map_ref[...]).astype(jnp.bfloat16)
-    value = restricted[...]
-    head, rest = split(value)
-    tail = (value - head.astype(jnp.float32) - rest.astype(jnp.float32)).astype(jnp.bfloat16)
-    across = (((1,), (1,)), ((), ()))
-    sums = mxu(head, hot, across) + mxu(rest, hot, across) + mxu(tail, hot, across)
-
-    @pl.when(step == 0)
-    def _():
-        sums_ref[...] = sums
-
-    @pl.when(step > 0)
-    def _():
-        sums_ref[...] += sums
-
-
-def residuals(rows_to, slots, own, received, start, local_rows, cell_row, cells, derivative, prolong):
+
+
+def lift(start, rows, derivative, first, steps, earlier=()):
     fields, nodes, elems = start.shape[0], start.shape[1], start.shape[-1]
-    slot_total = rows_to.shape[0]
-    padded = -(-slot_total // LANES) * LANES
-    field_spec = pl.BlockSpec((fields, nodes, nodes, nodes, LANES), lambda s: (0, 0, 0, 0, s))
     vmem = pl.BlockSpec(memory_space=pltpu.VMEM)
-    residual, sums, _ = pl.pallas_call(
-        functools.partial(
-            residual_kernel, derivative=derivative, prolong=prolong, elems=elems, fields=fields, nodes=nodes
-        ),
-        out_shape=(
-            jax.ShapeDtypeStruct(start.shape, jnp.float32),
-            jax.ShapeDtypeStruct((fields * 8, cells), jnp.float32),
-            jax.ShapeDtypeStruct(local_rows.shape, jnp.float32),
-        ),
-        grid=(elems // LANES,),
-        in_specs=[pl.BlockSpec(memory_space=pltpu.SMEM)] + [vmem] * 10
-        + [field_spec, vmem, pl.BlockSpec((1, LANES), lambda s: (0, s))],
-        out_specs=(field_spec, pl.BlockSpec((fields * 8, cells), lambda s: (0, 0)), vmem),
-        scratch_shapes=[
-            pltpu.VMEM((padded, LANES), jnp.int32),
-            pltpu.VMEM((slot_total * fields, LANES), jnp.float32),
-            pltpu.VMEM((fields, 6, LANES, LANES), jnp.float32),
-            pltpu.VMEM((fields * 8, LANES), jnp.float32),
-        ],
-        input_output_aliases={12: 2},
-        compiler_params=pltpu.CompilerParams(vmem_limit_bytes=16 * MIB),
+    return pl.pallas_call(
+        functools.partial(lift_kernel, derivative=derivative, elems=elems, first=first),
+        out_shape=jax.ShapeDtypeStruct(start.shape, jnp.float32),
+        grid=(steps,),
+        in_specs=[vmem, vmem] + [pl.BlockSpec(memory_space=pl.ANY)] * len(earlier),
+        out_specs=pl.BlockSpec((fields, nodes, nodes, nodes, LANES), lambda s: (0, 0, 0, 0, s + first)),
+        scratch_shapes=[pltpu.VMEM((fields, 6, LANES, LANES), jnp.float32)],
+        input_output_aliases={2: 0} if earlier else {},
+        compiler_params=pltpu.CompilerParams(vmem_limit_bytes=6 * MIB),
         cost_estimate=pl.CostEstimate(flops=10**8, bytes_accessed=9 * 10**6, transcendentals=0),
-        name="residuals",
-    )(rows_to, slots, own, *received, start, local_rows, cell_row)
-    return residual, sums
+    )(start, rows, *earlier)
 
 
 def correct_kernel(p_ref, inverse_ref, map_ref, *refs, prolong, parts):
@@ -512,6 +583,7 @@
     out_ref, heads, rests, tails = refs[parts:]
     step = pl.program_id(0)
     fields, nodes = p_ref.shape[0], p_ref.shape[1]
+    here = pl.ds(pl.multiple_of(step * LANES, LANES), LANES)
     cells = inverse_ref.shape[-1]
 
     @pl.when(step == 0)
@@ -548,7 +620,7 @@
             down = quad[0] + float(ramp[j]) * (quad[1] - quad[0])
             slope = quad[2] + float(ramp[j]) * (quad[3] - quad[2]) - down
             for i in range(nodes):
-                out_ref[f, i, j] = p_ref[f, i, j] + (down + float(ramp[i]) * slope)
+                out_ref[f, i, j] = p_ref[f, i, j, :, here] + (down + float(ramp[i]) * slope)
 
 
 def corrected_field(pressure, coarse_inverse, cell_row, sums, prolong):
@@ -561,31 +633,38 @@
         out_shape=jax.ShapeDtypeStruct(pressure.shape, jnp.float32),
         grid=(elems // LANES,),
         in_specs=[
-            field_spec,
+            pl.BlockSpec(memory_space=pltpu.VMEM),
             pl.BlockSpec(coarse_inverse.shape, lambda s: (0, 0, 0)),
             pl.BlockSpec((1, LANES), lambda s: (0, s)),
         ]
         + [sum_spec] * len(sums),
         out_specs=field_spec,
         scratch_shapes=[pltpu.VMEM((fields * 8, cells), jnp.float32)] * 3,
-        compiler_params=pltpu.CompilerParams(vmem_limit_bytes=16 * MIB),
+        compiler_params=pltpu.CompilerParams(vmem_limit_bytes=6 * MIB),
         cost_estimate=pl.CostEstimate(flops=10**8, bytes_accessed=5 * 10**6, transcendentals=0),
         name="correct",
     )(pressure, coarse_inverse, cell_row, *sums)
 
 
 def solution(mesh):
-    blk_count, sub_count = mesh.shape["blk"], mesh.shape["sub"]
-
-    def shifted(block, k):
-        da, db = k // 3 - 1, k % 3 - 1
-        pairs = []
-        for b in range(blk_count):
-            for u in range(sub_count):
-                source = ((b + da) % blk_count) * sub_count + (u + db) % sub_count
-                pairs.append((source, b * sub_count + u))
-        size = block.shape[0] // 9
-        return lax.ppermute(block[(8 - k) * size : (9 - k) * size], ("blk", "sub"), pairs)
+    sub_count = mesh.shape["sub"]
+
+    def ring(axis, step):
+        count = mesh.shape[axis]
+        return axis, [((at + step) % count, at) for at in range(count)]
+
+    def swap(value, axis, step):
+        return lax.ppermute(value, *ring(axis, step))
+
+    def both_ways(to_next, to_last, axis, paired):
+        count = mesh.shape[axis]
+        if count % 2 or not paired:
+            return swap(to_last, axis, 1), swap(to_next, axis, -1)
+        even = lax.axis_index(axis) % 2 == 0
+        one = lax.ppermute(jnp.where(even, to_next, to_last), axis, [(at, at ^ 1) for at in range(count)])
+        pairs = [(at, (at + (1 if at % 2 else -1)) % count) for at in range(count)]
+        two = lax.ppermute(jnp.where(even, to_last, to_next), axis, pairs)
+        return jnp.where(even, one, two), jnp.where(even, two, one)
 
     def on_device(
         pressure,
@@ -616,19 +695,42 @@
             pltpu.with_memory_space_constraint(jnp.transpose(face_metric, (1, 0, 2)), pltpu.HBM),
             derivative,
         )
-        received = {k: shifted(send, k) for k in (3, 5, 1, 7)}
+        size = send.shape[0] // 9
+        block = [send[k * size : (k + 1) * size] for k in range(9)]
+        right, left = both_ways(
+            jnp.concatenate([block[2], block[8]]), jnp.concatenate([block[0], block[6]]), "sub", False
+        )
+        up, down = both_ways(block[7], block[1], "blk", True)
+        hbm = [pltpu.with_memory_space_constraint(value, pltpu.HBM) for value in (pressure, right_side, geometry)]
+        steps = elems // LANES
+        far_up, far_down = both_ways(
+            jnp.concatenate([right[size:], left[size:]]), jnp.concatenate([right[:size], left[:size]]), "blk", True
+        )
+        right, left = both_ways(block[5], block[3], "sub", False)
         local_rows = local_fluxes(pairs * width, pairs * fields, local_pairs, table, fields, nodes, elems)
-        later, local_rows, right_later = lax.optimization_barrier((send, local_rows, right_side))
-        received.update({k: shifted(later, k) for k in (0, 2, 6, 8)})
-        start = volume(pressure, right_later, geometry, derivative)
-        received = [received[k] for k in sorted(received)]
-        residual, sums = residuals(
-            cross * fields, cross_slots, send, received, start, local_rows, cell_row, cells, derivative, prolong
+        start, sums = volume(*hbm, cell_row, cells, derivative, prolong[:, 1], 0, steps)
+        rows, sums = cross_sums(
+            cross * fields,
+            cross_slots,
+            send,
+            (far_up, far_down, up, down, right, left),
+            local_rows,
+            cell_row,
+            sums,
+            derivative,
+            prolong,
+            nodes,
         )
-        all_sums = [sums]
-        for shift in range(1, sub_count):
-            ring = [(at, (at + shift) % sub_count) for at in range(sub_count)]
-            all_sums.append(lax.ppermute(sums, "sub", ring))
+        if sub_count == 4 and steps > 1:
+            other = lax.ppermute(sums, "sub", [(at, at ^ 1) for at in range(sub_count)])
+            residual = lift(start, rows, derivative, 0, steps // 2)
+            sums = sums + other
+            other = lax.ppermute(sums, "sub", [(at, at ^ 2) for at in range(sub_count)])
+            residual = lift(start, rows, derivative, steps // 2, steps - steps // 2, (residual,))
+            all_sums = [sums, other]
+        else:
+            all_sums = [sums] + [swap(sums, "sub", step) for step in range(1, sub_count)]
+            residual = lift(start, rows, derivative, 0, steps)
         return residual, corrected_field(pressure, coarse_inverse, cell_row, all_sums, prolong)
 
     split_elems = ("blk", "sub")

time: 55 us -> 57.7 us (1.049)
  waiting for transfers between devices: 2.96 us -> 15.6 us
  starting transfers between devices: 19.5 us -> 10.7 us
  other arithmetic: 1.63 us -> 0.91 us
    ppermute x11 -> x10, waiting for transfers between devices: 2.96 us -> 15.6 us  [the longest x2 7.52 us: both_ways(): two = lax.ppermute(jnp.where(even, to_last, to_next), axis, pairs)]
    ppermute x11 -> x10, starting transfers between devices: 19.5 us -> 10.7 us  [the longest x2 4.78 us: both_ways(): two = lax.ppermute(jnp.where(even, to_last, to_next), axis, pairs)]
    pallas_call x1, Pallas kernels: 8.83 us -> 5.29 us  [local_fluxes(): pl.pallas_call(functools.partial(local_kernel, fields=fields, nodes=nodes...]
    pallas_call x2 -> x4, Pallas kernels: 13.8 us -> 17.3 us  [the longest x1 9.35 us: volume(): pl.pallas_call(functools.partial(volume_kernel, derivative=derivative, ra...]
    add x1, other arithmetic: 0.9 us -> 0.01 us  [on_device(): local_pairs[1] * elems + local_pairs[0]]
  transfers between devices with their start and end apart: 11 -> 10, of which waited for: 3 -> 4; matrix products, arithmetic and copies ran while one was open for 0% -> 0% of each run, Pallas kernels for 13% -> 32%
where the time goes in v2:
time: 57.7 us; the launch traced here: 57.5 us
  Pallas kernels  29.3 us (51%)
  waiting for transfers between devices  15.6 us (27%)
  starting transfers between devices  10.7 us (19%)
  other arithmetic  0.91 us (2%)
  between operations  0.88 us (2%)
    pallas_call x1, Pallas kernels, volume(): pl.pallas_call(functools.partial(volume_kernel, derivative=derivative, ra...  9.35 us
    ppermute x2, waiting for transfers between devices, both_ways(): two = lax.ppermute(jnp.where(even, to_last, to_next), axis, pairs)  7.52 us
    pallas_call x1, Pallas kernels, local_fluxes(): pl.pallas_call(functools.partial(local_kernel, fields=fields, nodes=nodes...  5.29 us
    ppermute x2, starting transfers between devices, both_ways(): two = lax.ppermute(jnp.where(even, to_last, to_next), axis, pairs)  4.78 us
    ppermute x4, waiting for transfers between devices, swap(): return lax.ppermute(value, *ring(axis, step))  4.6 us
    pallas_call x1, Pallas kernels, traces(): pl.pallas_call(functools.partial(trace_kernel, derivative=derivative, ele...  4.39 us
    pallas_call x1, Pallas kernels, cross_sums(): pl.pallas_call(functools.partial(cross_kernel, elems=elems, fields=fields...  4.35 us
    pallas_call x2, Pallas kernels, lift(): pl.pallas_call(functools.partial(lift_kernel, derivative=derivative, elem...  3.55 us
  transfers between devices with their start and end apart: 10, of which 4 were waited for; matrix products, arithmetic and copies ran while one was open for 0% of the time, Pallas kernels for 32%

profile of v2, /device:TPU:0, one launch (start us, length us, event | category | flops | bytes accessed | tf_op | source)
XLA Modules:
  0.0 57.5 jit_solution(10784775428258755184)
XLA Ops:
  0.6 0.7 %multiply_reduce_fusion = (s32[576]{0:T(1024)S(1)}, s32[576]{0:T(1024)S(1)}) fusion(s32[5,1,576]{2,1,0:T(1,128)} %slots_ref.1), kind=kLoop, calls=%fused_computation.15 | loop fusion | flops 2304 | bytes 9216 | tf_op jit(solution)/shard_map/mul | solution.py:692
  1.4 4.4 %traces.1 = (f32[9216,128]{1,0:T(8,128)S(1)}, f32[1728,128]{1,0:T(8,128)S(1)}) custom-call(s32[576]{0:T(1024)S(1)} %get-tuple-element.14.rows_ref, f32[2,8,8,8,512]{4,3,2,1,0:T(8,128)} %p_ref.5, f32[6,64,512]{2,1,0:T(8,128)} %bitcast.8, f32[6,64,512]{2,1,0:T(8,128)} %bitcast.9), custom_call_target="tpu_custom_call" | custom-call | flops 10000000 | bytes 9000000 | tf_op jit(solution)/shard_map/traces/pallas_call | solution.py:156
  5.8 0.1 fusion.4
  5.8 0.5 collective-permute-start.7
  6.4 2.0 %collective-permute-start.6 = (f32[192,128]{1,0:T(8,128)S(1)}, f32[192,128]{1,0:T(8,128)S(1)}, u32[]{:S(2)}, u32[]{:S(2)}) collective-permute-start(f32[192,128]{1,0:T(8,128)S(1)} %get-tuple-element.17), channel_id=1, source_target_pairs={{1,0},{2,1},{3,2},{0,3},{5,4},{6,5},{7,6},{4,7},{9,8},{10,9},{11,1... | collective-permute-start | bytes 294920 | tf_op jit(solution)/shard_map/ppermute | solution.py:657
  8.4 2.3 %collective-permute-start.4 = (f32[192,128]{1,0:T(8,128)S(1)}, f32[192,128]{1,0:T(8,128)S(1)}, u32[]{:S(2)}, u32[]{:S(2)}) collective-permute-start(f32[192,128]{1,0:T(8,128)S(1)} %get-tuple-element.18), channel_id=1, source_target_pairs={{0,4},{4,0},{8,12},{12,8},{16,20},{20,16},{24,28},{28,24},{1,5},{5... | collective-permute-start | bytes 294920 | tf_op jit(solution)/shard_map/ppermute | solution.py:664
  10.6 3.5 %collective-permute-start.5 = (f32[192,128]{1,0:T(8,128)S(1)}, f32[192,128]{1,0:T(8,128)S(1)}, u32[]{:S(2)}, u32[]{:S(2)}) collective-permute-start(f32[192,128]{1,0:T(8,128)S(1)} %get-tuple-element.19), channel_id=1, source_target_pairs={{0,28},{4,8},{8,4},{12,16},{16,12},{20,24},{24,20},{28,0},{1,29},{... | collective-permute-start | bytes 294920 | tf_op jit(solution)/shard_map/ppermute | solution.py:666
  14.2 0.1 collective-permute-start
  14.3 0.0 copy-start.1
  14.3 0.0 copy-start.2
  14.3 5.3 %local_fluxes.1.rows_in = f32[6144,128]{1,0:T(8,128)S(1)} custom-call(s32[1024]{0:T(1024)S(1)} %get-tuple-element.37.from_ref, s32[1024]{0:T(1024)S(1)} %get-tuple-element.36.to_ref, s32[5,512]{1,0:T(8,128)S(1)} %copy-done.5, f32[9216,128]{1,0:T(8,128)S(1)} %get-tuple-element.10.table_ref), custom_call_target="tpu_custom_call" | custom-call | flops 10000000 | bytes 12000000 | tf_op jit(solution)/shard_map/local_fluxes/pallas_call | solution.py:334
  19.7 9.4 %shard_map.140 = (f32[2,8,8,8,512]{4,3,2,1,0:T(8,128)S(1)}, f32[16,256]{1,0:T(8,128)S(1)}) custom-call(f32[2,8,8,8,512]{4,3,2,1,0:T(8,128)} %p_ref.5, f32[2,8,8,8,512]{4,3,2,1,0:T(8,128)} %rs_ref.1, f32[6,8,8,8,512]{4,3,2,1,0:T(8,128)} %g_ref.1, bf16[512,768]{1,0:T(8,128)(2,1)S(1)} %copy-done.2, bf16[256,1536]{1,0:T(8,128)(2,1)S(1)} %copy-done.1, ...), custom_call_target="tpu_custom_call" | custom-call | flops 1000000000 | bytes 13000000 | tf_op jit(solution)/shard_map/pallas_call | solution.py:433
  29.1 0.5 collective-permute-start.1
  29.6 4.6 %collective-permute-done.1 = f32[384,128]{1,0:T(8,128)S(1)} collective-permute-done((f32[384,128]{1,0:T(8,128)S(1)}, f32[384,128]{1,0:T(8,128)S(1)}, u32[]{:S(2)}, u32[]{:S(2)}) %collective-permute-start.1) | collective-permute-done | bytes 196640 | tf_op jit(solution)/shard_map/ppermute | solution.py:657
  34.3 1.2 %collective-permute-start.3 = (f32[384,128]{1,0:T(8,128)S(1)}, f32[384,128]{1,0:T(8,128)S(1)}, u32[]{:S(2)}, u32[]{:S(2)}) collective-permute-start(f32[384,128]{1,0:T(8,128)S(1)} %get-tuple-element.26), channel_id=1, source_target_pairs={{0,28},{4,8},{8,4},{12,16},{16,12},{20,24},{24,20},{28,0},{1,29},{... | collective-permute-start | bytes 589832 | tf_op jit(solution)/shard_map/ppermute | solution.py:666
  35.6 7.5 %collective-permute-done.3 = f32[384,128]{1,0:T(8,128)S(1)} collective-permute-done((f32[384,128]{1,0:T(8,128)S(1)}, f32[384,128]{1,0:T(8,128)S(1)}, u32[]{:S(2)}, u32[]{:S(2)}) %collective-permute-start.3) | collective-permute-done | bytes 196640 | tf_op jit(solution)/shard_map/ppermute | solution.py:666
  43.1 2.3 %collective-permute-done.2 = f32[384,128]{1,0:T(8,128)S(1)} collective-permute-done((f32[384,128]{1,0:T(8,128)S(1)}, f32[384,128]{1,0:T(8,128)S(1)}, u32[]{:S(2)}, u32[]{:S(2)}) %collective-permute-start.2) | collective-permute-done | bytes 196640 | tf_op jit(solution)/shard_map/ppermute | solution.py:664
  45.5 4.4 %cross_sums.1 = (f32[6144,128]{1,0:T(8,128)S(1)}, f32[16,256]{1,0:T(8,128)S(1)}) custom-call(s32[576]{0:T(1024)S(1)} %get-tuple-element.15.to_ref, s32[5,1,576]{2,1,0:T(1,128)S(1)} %copy-done.6, f32[1728,128]{1,0:T(8,128)S(1)} %get-tuple-element.9.own_ref, f32[384,128]{1,0:T(8,128)S(1)} %get-tuple-element.25.far_up, ...), custom_call_target="tpu_custom_call", output_to_operand_aliasing={{0}: (9, {})} | custom-call | flops 100000000 | bytes 4000000 | tf_op jit(solution)/shard_map/cross_sums/pallas_call | solution.py:503
  49.8 0.0 collective-permute-start.8
  49.9 1.2 %collective-permute-done.8 = f32[16,256]{1,0:T(8,128)S(1)} collective-permute-done((f32[16,256]{1,0:T(8,128)S(1)}, f32[16,256]{1,0:T(8,128)S(1)}, u32[]{:S(2)}, u32[]{:S(2)}) %collective-permute-start.8) | collective-permute-done | bytes 16416 | tf_op jit(solution)/shard_map/ppermute | solution.py:725
  51.0 0.5 collective-permute-start.9
  51.6 1.8 %shard_map.141.refs_0_ = f32[2,8,8,8,512]{4,3,2,1,0:T(8,128)} custom-call(f32[2,8,8,8,512]{4,3,2,1,0:T(8,128)S(1)} %get-tuple-element.8.start_ref, f32[6144,128]{1,0:T(8,128)S(1)} %get-tuple-element.12.rows_ref), custom_call_target="tpu_custom_call" | custom-call | flops 100000000 | bytes 9000000 | tf_op jit(solution)/shard_map/pallas_call | solution.py:568
  53.4 1.8 %shard_map.142 = f32[2,8,8,8,512]{4,3,2,1,0:T(8,128)} custom-call(f32[2,8,8,8,512]{4,3,2,1,0:T(8,128)S(1)} %get-tuple-element.8.start_ref, f32[6144,128]{1,0:T(8,128)S(1)} %get-tuple-element.12.rows_ref, f32[2,8,8,8,512]{4,3,2,1,0:T(8,128)} %shard_map.141.refs_0_), custom_call_target="tpu_custom_call", output_to_operand_aliasing={{}: (2, {})} | custom-call | flops 100000000 | bytes 9000000 | tf_op jit(solution)/shard_map/pallas_call | solution.py:568
  55.2 2.4 %correct.1 = f32[2,8,8,8,512]{4,3,2,1,0:T(8,128)} custom-call(f32[2,8,8,8,512]{4,3,2,1,0:T(8,128)S(1)} %copy-done, f32[8,8,256]{2,1,0:T(8,128)S(1)} %copy-done.4, s32[1,512]{1,0:T(1,128)S(1)} %bitcast.7, f32[16,256]{1,0:T(8,128)S(1)} %add.30.refs_0_, f32[16,256]{1,0:T(8,128)S(1)} %collective-permute-done.9.refs_1_), custom_call_target="tpu_custom_call" | custom-call | flops 100000000 | bytes 5000000 | tf_op jit(solution)/shard_map/correct/pallas_call | solution.py:631
  (31 shorter events, 0.2 us)
Async XLA Ops:
  1.4 12.9 %copy-start.5 = (s32[5,512]{1,0:T(8,128)S(1)}, s32[5,512]{1,0:T(8,128)}, u32[]{:S(2)}) copy-start(s32[5,512]{1,0:T(8,128)} %code_ref.1) | copy-start | bytes 30724
  5.8 39.6 %collective-permute-start.7 = (f32[192,128]{1,0:T(8,128)S(1)}, f32[192,128]{1,0:T(8,128)S(1)}, u32[]{:S(2)}, u32[]{:S(2)}) collective-permute-start(f32[192,128]{1,0:T(8,128)S(1)} %get-tuple-element.16), channel_id=1, source_target_pairs={{3,0},{0,1},{1,2},{2,3},{7,4},{4,5},{5,6},{6,7},{11,8},{8,9},{9,10... | collective-permute-start | bytes 294920 | tf_op jit(solution)/shard_map/ppermute | solution.py:657
  6.4 39.0 %collective-permute-start.6 = (f32[192,128]{1,0:T(8,128)S(1)}, f32[192,128]{1,0:T(8,128)S(1)}, u32[]{:S(2)}, u32[]{:S(2)}) collective-permute-start(f32[192,128]{1,0:T(8,128)S(1)} %get-tuple-element.17), channel_id=1, source_target_pairs={{1,0},{2,1},{3,2},{0,3},{5,4},{6,5},{7,6},{4,7},{9,8},{10,9},{11,1... | collective-permute-start | bytes 294920 | tf_op jit(solution)/shard_map/ppermute | solution.py:657
  8.4 27.2 %collective-permute-start.4 = (f32[192,128]{1,0:T(8,128)S(1)}, f32[192,128]{1,0:T(8,128)S(1)}, u32[]{:S(2)}, u32[]{:S(2)}) collective-permute-start(f32[192,128]{1,0:T(8,128)S(1)} %get-tuple-element.18), channel_id=1, source_target_pairs={{0,4},{4,0},{8,12},{12,8},{16,20},{20,16},{24,28},{28,24},{1,5},{5... | collective-permute-start | bytes 294920 | tf_op jit(solution)/shard_map/ppermute | solution.py:664
  10.6 24.9 %collective-permute-start.5 = (f32[192,128]{1,0:T(8,128)S(1)}, f32[192,128]{1,0:T(8,128)S(1)}, u32[]{:S(2)}, u32[]{:S(2)}) collective-permute-start(f32[192,128]{1,0:T(8,128)S(1)} %get-tuple-element.19), channel_id=1, source_target_pairs={{0,28},{4,8},{8,4},{12,16},{16,12},{20,24},{24,20},{28,0},{1,29},{... | collective-permute-start | bytes 294920 | tf_op jit(solution)/shard_map/ppermute | solution.py:666
  14.2 14.9 %collective-permute-start = (f32[384,128]{1,0:T(8,128)S(1)}, f32[384,128]{1,0:T(8,128)S(1)}, u32[]{:S(2)}, u32[]{:S(2)}) collective-permute-start(f32[384,128]{1,0:T(8,128)S(1)} %pad_maximum_fusion), channel_id=1, source_target_pairs={{1,0},{2,1},{3,2},{0,3},{5,4},{6,5},{7,6},{4,7},{9,8},{10,9},{11,1... | collective-permute-start | bytes 589832 | tf_op jit(solution)/shard_map/ppermute | solution.py:657
  14.3 5.3 %copy-start.1 = (bf16[256,1536]{1,0:T(8,128)(2,1)S(1)}, bf16[256,1536]{1,0:T(8,128)(2,1)}, u32[]{:S(2)}) copy-start(bf16[256,1536]{1,0:T(8,128)(2,1)} %constant.56.back_ref) | copy-start | bytes 2359300
  14.3 5.3 %copy-start.2 = (bf16[512,768]{1,0:T(8,128)(2,1)S(1)}, bf16[512,768]{1,0:T(8,128)(2,1)}, u32[]{:S(2)}) copy-start(bf16[512,768]{1,0:T(8,128)(2,1)} %constant.47.fwd_ref) | copy-start | bytes 2359300
  14.3 5.3 %copy-start.7 = (s32[512]{0:T(512)S(1)}, s32[512]{0:T(512)}, u32[]{:S(2)}) copy-start(s32[512]{0:T(512)} %param.20) | copy-start | bytes 6148
  29.0 16.4 %copy-start.3 = (bf16[3072,128]{1,0:T(8,128)(2,1)S(1)}, bf16[3072,128]{1,0:T(8,128)(2,1)}, u32[]{:S(2)}) copy-start(bf16[3072,128]{1,0:T(8,128)(2,1)} %constant.61.table_ref) | copy-start | bytes 2359300
  29.0 16.4 %copy-start.6 = (s32[5,1,576]{2,1,0:T(1,128)S(1)}, s32[5,1,576]{2,1,0:T(1,128)}, u32[]{:S(2)}) copy-start(s32[5,1,576]{2,1,0:T(1,128)} %slots_ref.1) | copy-start | bytes 34564
  29.1 5.1 %collective-permute-start.1 = (f32[384,128]{1,0:T(8,128)S(1)}, f32[384,128]{1,0:T(8,128)S(1)}, u32[]{:S(2)}, u32[]{:S(2)}) collective-permute-start(f32[384,128]{1,0:T(8,128)S(1)} %pad_maximum_fusion.1), channel_id=1, source_target_pairs={{3,0},{0,1},{1,2},{2,3},{7,4},{4,5},{5,6},{6,7},{11,8},{8,9},{9,10... | collective-permute-start | bytes 589832 | tf_op jit(solution)/shard_map/ppermute | solution.py:657
  34.3 8.8 %collective-permute-start.3 = (f32[384,128]{1,0:T(8,128)S(1)}, f32[384,128]{1,0:T(8,128)S(1)}, u32[]{:S(2)}, u32[]{:S(2)}) collective-permute-start(f32[384,128]{1,0:T(8,128)S(1)} %get-tuple-element.26), channel_id=1, source_target_pairs={{0,28},{4,8},{8,4},{12,16},{16,12},{20,24},{24,20},{28,0},{1,29},{... | collective-permute-start | bytes 589832 | tf_op jit(solution)/shard_map/ppermute | solution.py:666
  35.5 9.9 %collective-permute-start.2 = (f32[384,128]{1,0:T(8,128)S(1)}, f32[384,128]{1,0:T(8,128)S(1)}, u32[]{:S(2)}, u32[]{:S(2)}) collective-permute-start(f32[384,128]{1,0:T(8,128)S(1)} %get-tuple-element.27), channel_id=1, source_target_pairs={{0,4},{4,0},{8,12},{12,8},{16,20},{20,16},{24,28},{28,24},{1,5},{5... | collective-permute-start | bytes 589832 | tf_op jit(solution)/shard_map/ppermute | solution.py:664
  49.8 1.2 %collective-permute-start.8 = (f32[16,256]{1,0:T(8,128)S(1)}, f32[16,256]{1,0:T(8,128)S(1)}, u32[]{:S(2)}, u32[]{:S(2)}) collective-permute-start(f32[16,256]{1,0:T(8,128)S(1)} %get-tuple-element.13), channel_id=1, source_target_pairs={{0,1},{1,0},{2,3},{3,2},{4,5},{5,4},{6,7},{7,6},{8,9},{9,8},{10,11... | collective-permute-start | bytes 49160 | tf_op jit(solution)/shard_map/ppermute | solution.py:725
  51.0 4.1 %collective-permute-start.9 = (f32[16,256]{1,0:T(8,128)S(1)}, f32[16,256]{1,0:T(8,128)S(1)}, u32[]{:S(2)}, u32[]{:S(2)}) collective-permute-start(f32[16,256]{1,0:T(8,128)S(1)} %add.30.refs_0_), channel_id=1, source_target_pairs={{0,2},{1,3},{2,0},{3,1},{4,6},{5,7},{6,4},{7,5},{8,10},{9,11},{10,... | collective-permute-start | bytes 49160 | tf_op jit(solution)/shard_map/ppermute | solution.py:728
  53.4 1.8 %copy-start = (f32[2,8,8,8,512]{4,3,2,1,0:T(8,128)S(1)}, f32[2,8,8,8,512]{4,3,2,1,0:T(8,128)}, u32[]{:S(2)}) copy-start(f32[2,8,8,8,512]{4,3,2,1,0:T(8,128)} %p_ref.5) | copy-start | bytes 6291460
  53.4 1.8 %copy-start.4 = (f32[8,8,256]{2,1,0:T(8,128)S(1)}, f32[8,8,256]{2,1,0:T(8,128)}, u32[]{:S(2)}) copy-start(f32[8,8,256]{2,1,0:T(8,128)} %inverse_ref.1) | copy-start | bytes 196612

commit v3 on v2

--- a/solution.py
+++ b/solution.py
@@ -348,21 +348,20 @@
 
 
 def volume_kernel(
-    p_ref, rs_ref, g_ref, fwd_ref, back_ref, map_ref, *refs, derivative, ramp, earlier
+    p_ref, rs_ref, g_ref, fwd_ref, back_ref, map_ref, out_ref, sums_ref, one, two, three, four, modes, *, derivative, ramp
 ):
-    base_ref = refs[1] if earlier else None
-    out_ref, sums_ref, one, two, three, four, modes = refs[2:] if earlier else refs
     fields, nodes = p_ref.shape[0], p_ref.shape[1]
     rows = nodes**3
     block = back_ref.shape[0]
     planes = block // (nodes * nodes)
     back = derivative.T
+    lanes_here = pl.ds(pl.multiple_of(pl.program_id(0) * LANES, LANES), LANES)
 
     def both(at, read):
         return jnp.concatenate([read(f).reshape(rows, LANES)[at * block : (at + 1) * block] for f in range(fields)], axis=1)
 
     for at in range(rows // block):
-        head, tail = split(both(at, lambda f: p_ref[f]))
+        head, tail = split(both(at, lambda f: p_ref[f, :, :, :, lanes_here]))
         slopes = mxu(fwd_ref[...], jnp.concatenate([head, tail, head], axis=0))
         for f in range(fields):
             lanes = slice(f * LANES, (f + 1) * LANES)
@@ -371,12 +370,12 @@
             three[f, here] = slopes[block:, lanes].reshape(planes, nodes, nodes, LANES)
     for f in range(fields):
         for j in range(nodes):
-            slopes = derive(derivative, [p_ref[f, k, j] for k in range(nodes)])
+            slopes = derive(derivative, [p_ref[f, k, j, :, lanes_here] for k in range(nodes)])
             for i in range(nodes):
                 one[f, i, j] = slopes[i]
     for i in range(nodes):
         for j in range(nodes):
-            xx, yy, zz, xy, xz, yz = [g_ref[c, i, j] for c in range(6)]
+            xx, yy, zz, xy, xz, yz = [g_ref[c, i, j, :, lanes_here] for c in range(6)]
             for f in range(fields):
                 s1, s2, s3 = one[f, i, j], two[f, i, j], three[f, i, j]
                 one[f, i, j] = xx * s1 + xy * s2 + xz * s3
@@ -389,13 +388,13 @@
         for f in range(fields):
             lanes = slice(f * LANES, (f + 1) * LANES)
             here = slice(at * planes, (at + 1) * planes)
-            four[f, here] = rs_ref[f, here] - sums[:, lanes].reshape(planes, nodes, nodes, LANES)
+            four[f, here] = rs_ref[f, here, :, :, lanes_here] - sums[:, lanes].reshape(planes, nodes, nodes, LANES)
     for f in range(fields):
         for j in range(nodes):
             sums = derive(back, [one[f, k, j] for k in range(nodes)])
             for i in range(nodes):
-                out_ref[f, i, j] = four[f, i, j] - sums[i]
-        restrict_nodes(lambda i, j, f=f: out_ref[f, i, j], modes, f * 8, ramp, nodes)
+                out_ref[f, i, j, :, lanes_here] = four[f, i, j] - sums[i]
+        restrict_nodes(lambda i, j, f=f: out_ref[f, i, j, :, lanes_here], modes, f * 8, ramp, nodes)
     hot = cell_mask(map_ref[...], sums_ref.shape[1])
     across = (((1,), (1,)), ((), ()))
     head, rest, tail = three_parts(modes[...])
@@ -403,15 +402,15 @@
 
     @pl.when(pl.program_id(0) == 0)
     def _():
-        sums_ref[...] = base_ref[...] + total if earlier else total
+        sums_ref[...] = total
 
     @pl.when(pl.program_id(0) > 0)
     def _():
         sums_ref[...] += total
 
 
-def volume(pressure, right_side, geometry, cell_row, cells, derivative, ramp, first, steps, earlier=()):
-    fields, nodes = pressure.shape[0], pressure.shape[1]
+def volume(pressure, right_side, geometry, cell_row, cells, derivative, ramp):
+    fields, nodes, elems = pressure.shape[0], pressure.shape[1], pressure.shape[-1]
     block = 256
     planes = block // (nodes * nodes)
     eye = np.eye(nodes)
@@ -428,77 +427,82 @@
     (head2, tail2), (head3, tail3) = parts(middle.T), parts(minor.T)
     backward = jnp.concatenate([head2, head2, tail2, head3, head3, tail3], axis=1)
     whole = (fields, nodes, nodes, nodes, LANES)
-    field_spec = pl.BlockSpec(whole, lambda s: (0, 0, 0, 0, s + first))
     vmem = pl.BlockSpec(memory_space=pltpu.VMEM)
     return pl.pallas_call(
-        functools.partial(volume_kernel, derivative=derivative, ramp=ramp, earlier=bool(earlier)),
+        functools.partial(volume_kernel, derivative=derivative, ramp=ramp),
         out_shape=(
             jax.ShapeDtypeStruct(pressure.shape, jnp.float32),
             jax.ShapeDtypeStruct((fields * 8, cells), jnp.float32),
         ),
-        grid=(steps,),
-        in_specs=[
-            field_spec,
-            field_spec,
-            pl.BlockSpec((6, nodes, nodes, nodes, LANES), lambda s: (0, 0, 0, 0, s + first)),
-            vmem,
-            vmem,
-            pl.BlockSpec((1, LANES), lambda s: (0, s + first)),
-        ]
-        + [pl.BlockSpec(memory_space=pl.ANY), vmem][: len(earlier)],
-        out_specs=(field_spec, vmem),
+        grid=(elems // LANES,),
+        in_specs=[vmem] * 5 + [pl.BlockSpec((1, LANES), lambda s: (0, s))],
+        out_specs=(vmem, vmem),
         scratch_shapes=[pltpu.VMEM(whole, jnp.float32)] * 4 + [pltpu.VMEM((fields * 8, LANES), jnp.float32)],
-        input_output_aliases={6: 0} if earlier else {},
         compiler_params=pltpu.CompilerParams(vmem_limit_bytes=14 * MIB),
         cost_estimate=pl.CostEstimate(flops=10**9, bytes_accessed=13 * 10**6, transcendentals=0),
-    )(pressure, right_side, geometry, forward, backward, cell_row, *earlier)
+    )(pressure, right_side, geometry, forward, backward, cell_row)
+
+
+def center_kernel(
+    to_ref, slots_ref, own_ref, up_ref, down_ref, right_ref, left_ref, rows_in, rows_ref, order, result, *, fields, nodes
+):
+    cap = to_ref.shape[0] // 9
+    del rows_in
+    sources = {1: (down_ref, 0), 3: (left_ref, 1), 5: (right_ref, 1), 7: (up_ref, 0)}
+    cross_flags(slots_ref, order)
+    cross_rows(sources, own_ref, order, result, cap, fields, nodes)
+    put_blocks(sources, to_ref, result, rows_ref, cap, fields)
+
+
+def center_rows(rows_to, slots, own, near, local_rows, fields, nodes):
+    slot_total = rows_to.shape[0]
+    padded = -(-slot_total // LANES) * LANES
+    vmem = pl.BlockSpec(memory_space=pltpu.VMEM)
+    return pl.pallas_call(
+        functools.partial(center_kernel, fields=fields, nodes=nodes),
+        out_shape=(
+            jax.ShapeDtypeStruct(local_rows.shape, jnp.float32),
+            jax.ShapeDtypeStruct((padded, LANES), jnp.int32),
+        ),
+        in_specs=[pl.BlockSpec(memory_space=pltpu.SMEM)] + [vmem] * 7,
+        out_specs=(vmem, vmem),
+        scratch_shapes=[pltpu.VMEM((slot_total * fields, LANES), jnp.float32)],
+        input_output_aliases={7: 0},
+        compiler_params=pltpu.CompilerParams(vmem_limit_bytes=8 * MIB),
+        cost_estimate=pl.CostEstimate(flops=10**7, bytes_accessed=10**6, transcendentals=0),
+        name="center_rows",
+    )(rows_to, slots, own, *near, local_rows)
 
 
 def cross_kernel(
-    to_ref, slots_ref, own_ref, far_up, far_down, up_ref, down_ref, right_ref, left_ref, rows_in, map_ref, base_ref,
-    table_ref,
-    rows_ref, sums_ref, order, result, packed, *, elems, fields, nodes,
+    to_ref, order, own_ref, far_up, far_down, rows_in, map_ref, base_ref, table_ref,
+    rows_ref, sums_ref, result, *, elems, fields, nodes,
 ):
     slot_total = to_ref.shape[0]
     cap = slot_total // 9
     del rows_in
     sources = {8: (far_up, 0), 6: (far_up, 1), 2: (far_down, 0), 0: (far_down, 1)}
-    sources.update({1: (down_ref, 0), 3: (left_ref, 0), 5: (right_ref, 0), 7: (up_ref, 0)})
-    cross_flags(slots_ref, order)
     cross_rows(sources, own_ref, order, result, cap, fields, nodes)
     put_blocks(sources, to_ref, result, rows_ref, cap, fields)
-    cells = base_ref.shape[1]
-    size = table_ref.shape[0] // 2
-    block = min(elems, 256)
-    for at in range(elems // block):
-        parts = [
-            split(rows_ref[pl.ds((face * elems + at * block) * fields + f, block, stride=fields), :])
-            for f in range(fields)
-            for face in range(6)
-        ]
-        heads = jnp.concatenate([head for head, _ in parts], axis=1)
-        tails = jnp.concatenate([tail for _, tail in parts], axis=1)
-        packed[at * block : (at + 1) * block, :] = (
-            mxu(heads, table_ref[:size]) + mxu(tails, table_ref[:size]) + mxu(heads, table_ref[size:])
-        )
-    hot = cell_mask(map_ref[...], cells)
-    head, rest, tail = three_parts(packed[...])
-    total = mxu(hot, head) + mxu(hot, rest) + mxu(hot, tail)
-    sums_ref[...] = base_ref[...] - total.T[: base_ref.shape[0]]
-
-
-def cross_sums(rows_to, slots, own, far, local_rows, cell_row, base, derivative, prolong, nodes):
+    across = (((1,), (1,)), ((), ()))
+    values = []
+    for f in range(fields):
+        parts = [split(rows_ref[pl.ds(face * elems * fields + f, elems, stride=fields), :]) for face in range(6)]
+        by_head = mxu(table_ref[...], jnp.concatenate([head for head, _ in parts], axis=1), across)
+        by_tail = mxu(table_ref[...], jnp.concatenate([tail for _, tail in parts], axis=1), across)
+        values.append(by_head[:8] + by_head[8:] + by_tail[:8])
+    hot = cell_mask(map_ref[...], base_ref.shape[1])
+    head, rest, tail = three_parts(jnp.concatenate(values, axis=0))
+    sums_ref[...] = base_ref[...] - (mxu(head, hot, across) + mxu(rest, hot, across) + mxu(tail, hot, across))
+
+
+def cross_sums(rows_to, flags, own, far, local_rows, cell_row, base, derivative, prolong, nodes):
     elems = cell_row.shape[1]
     fields = base.shape[0] // 8
     slot_total = rows_to.shape[0]
-    padded = -(-slot_total // LANES) * LANES
-    table = face_modes(derivative, prolong).reshape(-1, 8)
-    wide = np.zeros((fields, table.shape[0], LANES))
-    for f in range(fields):
-        wide[f, :, f * 8 : f * 8 + 8] = table
-    wide = jnp.asarray(wide.reshape(-1, LANES), jnp.float32)
-    head = wide.astype(jnp.bfloat16)
-    both = jnp.concatenate([head, (wide - head.astype(jnp.float32)).astype(jnp.bfloat16)], axis=0)
+    table = jnp.asarray(face_modes(derivative, prolong).reshape(-1, 8).T, jnp.float32)
+    head = table.astype(jnp.bfloat16)
+    both = jnp.concatenate([head, (table - head.astype(jnp.float32)).astype(jnp.bfloat16)], axis=0)
     vmem = pl.BlockSpec(memory_space=pltpu.VMEM)
     return pl.pallas_call(
         functools.partial(cross_kernel, elems=elems, fields=fields, nodes=nodes),
@@ -506,18 +510,14 @@
             jax.ShapeDtypeStruct(local_rows.shape, jnp.float32),
             jax.ShapeDtypeStruct(base.shape, jnp.float32),
         ),
-        in_specs=[pl.BlockSpec(memory_space=pltpu.SMEM)] + [vmem] * 12,
+        in_specs=[pl.BlockSpec(memory_space=pltpu.SMEM)] + [vmem] * 8,
         out_specs=(vmem, vmem),
-        scratch_shapes=[
-            pltpu.VMEM((padded, LANES), jnp.int32),
-            pltpu.VMEM((slot_total * fields, LANES), jnp.float32),
-            pltpu.VMEM((elems, LANES), jnp.float32),
-        ],
-        input_output_aliases={9: 0},
-        compiler_params=pltpu.CompilerParams(vmem_limit_bytes=8 * MIB),
+        scratch_shapes=[pltpu.VMEM((slot_total * fields, LANES), jnp.float32)],
+        input_output_aliases={5: 0},
+        compiler_params=pltpu.CompilerParams(vmem_limit_bytes=12 * MIB),
         cost_estimate=pl.CostEstimate(flops=10**8, bytes_accessed=4 * 10**6, transcendentals=0),
         name="cross_sums",
-    )(rows_to, slots, own, *far, local_rows, cell_row, base, both)
+    )(rows_to, flags, own, *far, local_rows, cell_row, base, both)
 
 
 def lift_kernel(start_ref, rows_ref, *refs, derivative, elems, first):
@@ -578,9 +578,23 @@
     )(start, rows, *earlier)
 
 
+def send_out(buffer, out_hbm, sems, step, f):
+    cuts = sems.shape[2]
+    size = buffer.shape[2] // cuts
+    lanes = pl.ds(step * LANES if isinstance(step, int) else pl.multiple_of(step * LANES, LANES), LANES)
+    return [
+        pltpu.make_async_copy(
+            buffer.at[step, f, cut * size : (cut + 1) * size],
+            out_hbm.at[f, cut * size : (cut + 1) * size, :, :, lanes],
+            sems.at[step, f, cut],
+        )
+        for cut in range(cuts)
+    ]
+
+
 def correct_kernel(p_ref, inverse_ref, map_ref, *refs, prolong, parts):
     sum_refs = refs[:parts]
-    out_ref, heads, rests, tails = refs[parts:]
+    out_hbm, heads, rests, tails, buffer, sems = refs[parts:]
     step = pl.program_id(0)
     fields, nodes = p_ref.shape[0], p_ref.shape[1]
     here = pl.ds(pl.multiple_of(step * LANES, LANES), LANES)
@@ -620,13 +634,21 @@
             down = quad[0] + float(ramp[j]) * (quad[1] - quad[0])
             slope = quad[2] + float(ramp[j]) * (quad[3] - quad[2]) - down
             for i in range(nodes):
-                out_ref[f, i, j] = p_ref[f, i, j, :, here] + (down + float(ramp[i]) * slope)
+                buffer[step, f, i, j] = p_ref[f, i, j, :, here] + (down + float(ramp[i]) * slope)
+        for copy in send_out(buffer, out_hbm, sems, step, f):
+            copy.start()
+
+    @pl.when(step == pl.num_programs(0) - 1)
+    def _():
+        for at in range(buffer.shape[0]):
+            for f in range(fields):
+                for copy in send_out(buffer, out_hbm, sems, at, f):
+                    copy.wait()
 
 
 def corrected_field(pressure, coarse_inverse, cell_row, sums, prolong):
     fields, nodes, elems = pressure.shape[0], pressure.shape[1], pressure.shape[-1]
     cells = coarse_inverse.shape[-1]
-    field_spec = pl.BlockSpec((fields, nodes, nodes, nodes, LANES), lambda s: (0, 0, 0, 0, s))
     sum_spec = pl.BlockSpec((fields * 8, cells), lambda s: (0, 0))
     return pl.pallas_call(
         functools.partial(correct_kernel, prolong=prolong, parts=len(sums)),
@@ -638,8 +660,12 @@
             pl.BlockSpec((1, LANES), lambda s: (0, s)),
         ]
         + [sum_spec] * len(sums),
-        out_specs=field_spec,
-        scratch_shapes=[pltpu.VMEM((fields * 8, cells), jnp.float32)] * 3,
+        out_specs=pl.BlockSpec(memory_space=pl.ANY),
+        scratch_shapes=[pltpu.VMEM((fields * 8, cells), jnp.float32)] * 3
+        + [
+            pltpu.VMEM((elems // LANES, fields, nodes, nodes, nodes, LANES), jnp.float32),
+            pltpu.SemaphoreType.DMA((elems // LANES, fields, 4)),
+        ],
         compiler_params=pltpu.CompilerParams(vmem_limit_bytes=6 * MIB),
         cost_estimate=pl.CostEstimate(flops=10**8, bytes_accessed=5 * 10**6, transcendentals=0),
         name="correct",
@@ -698,22 +724,29 @@
         size = send.shape[0] // 9
         block = [send[k * size : (k + 1) * size] for k in range(9)]
         right, left = both_ways(
-            jnp.concatenate([block[2], block[8]]), jnp.concatenate([block[0], block[6]]), "sub", False
+            jnp.concatenate([block[2], block[5], block[8]]),
+            jnp.concatenate([block[0], block[3], block[6]]),
+            "sub",
+            False,
         )
         up, down = both_ways(block[7], block[1], "blk", True)
-        hbm = [pltpu.with_memory_space_constraint(value, pltpu.HBM) for value in (pressure, right_side, geometry)]
         steps = elems // LANES
         far_up, far_down = both_ways(
-            jnp.concatenate([right[size:], left[size:]]), jnp.concatenate([right[:size], left[:size]]), "blk", True
+            jnp.concatenate([right[2 * size :], left[2 * size :]]),
+            jnp.concatenate([right[:size], left[:size]]),
+            "blk",
+            True,
         )
-        right, left = both_ways(block[5], block[3], "sub", False)
         local_rows = local_fluxes(pairs * width, pairs * fields, local_pairs, table, fields, nodes, elems)
-        start, sums = volume(*hbm, cell_row, cells, derivative, prolong[:, 1], 0, steps)
+        start, sums = volume(pressure, right_side, geometry, cell_row, cells, derivative, prolong[:, 1])
+        local_rows, flags = center_rows(
+            cross * fields, cross_slots, send, (up, down, right, left), local_rows, fields, nodes
+        )
         rows, sums = cross_sums(
             cross * fields,
-            cross_slots,
+            flags,
             send,
-            (far_up, far_down, up, down, right, left),
+            (far_up, far_down),
             local_rows,
             cell_row,
             sums,

time: 57.7 us -> 50.4 us (0.87)
  waiting for transfers between devices: 15.6 us -> 11.5 us
  Pallas kernels: 29.3 us -> 27.5 us
  starting transfers between devices: 10.7 us -> 9.34 us
    ppermute x4 -> x2, waiting for transfers between devices: 4.6 us -> 0.01 us  [swap(): return lax.ppermute(value, *ring(axis, step))]
    ppermute x4 -> x2, starting transfers between devices: 3.11 us -> 0.61 us  [swap(): return lax.ppermute(value, *ring(axis, step))]
    pallas_call x1, Pallas kernels: 9.35 us -> 7.48 us  [volume(): pl.pallas_call(functools.partial(volume_kernel, derivative=derivative, ra...]
    pallas_call x0 -> x1, Pallas kernels: none -> 1.55 us  [center_rows(): pl.pallas_call(functools.partial(center_kernel, fields=fields, nodes=node...]
    pallas_call x1, Pallas kernels: 4.35 us -> 2.97 us  [cross_sums(): pl.pallas_call(functools.partial(cross_kernel, elems=elems, fields=fields...]
    ppermute x2, starting transfers between devices: 2.27 us -> 3.06 us  [both_ways(): lax.ppermute(jnp.where(even, to_next, to_last), axis, [(at, at ^ 1) for a...]
  transfers between devices with their start and end apart: 10 -> 8, of which waited for: 4 -> 3; matrix products, arithmetic and copies ran while one was open for 0% -> 0% of each run, Pallas kernels for 32% -> 36%
where the time goes in v3:
time: 50.4 us; the launch traced here: 50.2 us
  Pallas kernels  27.5 us (55%)
  waiting for transfers between devices  11.5 us (23%)
  starting transfers between devices  9.34 us (19%)
  other arithmetic  0.92 us (2%)
  between operations  0.88 us (2%)
    ppermute x2, waiting for transfers between devices, both_ways(): two = lax.ppermute(jnp.where(even, to_last, to_next), axis, pairs)  7.62 us
    pallas_call x1, Pallas kernels, volume(): pl.pallas_call(functools.partial(volume_kernel, derivative=derivative, ra...  7.48 us
    pallas_call x1, Pallas kernels, local_fluxes(): pl.pallas_call(functools.partial(local_kernel, fields=fields, nodes=nodes...  5.29 us
    ppermute x2, starting transfers between devices, both_ways(): two = lax.ppermute(jnp.where(even, to_last, to_next), axis, pairs)  4.79 us
    pallas_call x1, Pallas kernels, traces(): pl.pallas_call(functools.partial(trace_kernel, derivative=derivative, ele...  4.5 us
    pallas_call x2, Pallas kernels, lift(): pl.pallas_call(functools.partial(lift_kernel, derivative=derivative, elem...  3.55 us
    ppermute x2, starting transfers between devices, both_ways(): lax.ppermute(jnp.where(even, to_next, to_last), axis, [(at, at ^ 1) for a...  3.06 us
    pallas_call x1, Pallas kernels, cross_sums(): pl.pallas_call(functools.partial(cross_kernel, elems=elems, fields=fields...  2.97 us
  transfers between devices with their start and end apart: 8, of which 3 were waited for; matrix products, arithmetic and copies ran while one was open for 0% of the time, Pallas kernels for 36%

profile of v3, /device:TPU:0, one launch (start us, length us, event | category | flops | bytes accessed | tf_op | source)
XLA Modules:
  0.0 50.2 jit_solution(5449657382973090188)
XLA Ops:
  0.6 0.7 %multiply_reduce_fusion = (s32[576]{0:T(1024)S(1)}, s32[576]{0:T(1024)S(1)}) fusion(s32[5,1,576]{2,1,0:T(1,128)} %slots_ref.1), kind=kLoop, calls=%fused_computation.15 | loop fusion | flops 2304 | bytes 9216 | tf_op jit(solution)/shard_map/mul | solution.py:718
  1.4 0.0 copy-start.3
  1.4 0.0 copy-start.4
  1.4 4.5 %traces.1 = (f32[9216,128]{1,0:T(8,128)S(1)}, f32[1728,128]{1,0:T(8,128)S(1)}) custom-call(s32[576]{0:T(1024)S(1)} %get-tuple-element.18.rows_ref, f32[2,8,8,8,512]{4,3,2,1,0:T(8,128)} %p_ref.5, f32[6,64,512]{2,1,0:T(8,128)} %bitcast.8, f32[6,64,512]{2,1,0:T(8,128)} %bitcast.9), custom_call_target="tpu_custom_call" | custom-call | flops 10000000 | bytes 9000000 | tf_op jit(solution)/shard_map/traces/pallas_call | solution.py:156
  5.9 0.0 copy-start.6
  5.9 0.0 copy-start.2
  5.9 0.1 fusion.4
  6.0 3.1 %collective-permute-start = (f32[192,128]{1,0:T(8,128)S(1)}, f32[192,128]{1,0:T(8,128)S(1)}, u32[]{:S(2)}, u32[]{:S(2)}) collective-permute-start(f32[192,128]{1,0:T(8,128)S(1)} %get-tuple-element.26), channel_id=1, source_target_pairs={{0,4},{4,0},{8,12},{12,8},{16,20},{20,16},{24,28},{28,24},{1,5},{5... | collective-permute-start | bytes 294920 | tf_op jit(solution)/shard_map/ppermute | solution.py:690
  9.0 3.5 %collective-permute-start.1 = (f32[192,128]{1,0:T(8,128)S(1)}, f32[192,128]{1,0:T(8,128)S(1)}, u32[]{:S(2)}, u32[]{:S(2)}) collective-permute-start(f32[192,128]{1,0:T(8,128)S(1)} %get-tuple-element.27), channel_id=1, source_target_pairs={{0,28},{4,8},{8,4},{12,16},{16,12},{20,24},{24,20},{28,0},{1,29},{... | collective-permute-start | bytes 294920 | tf_op jit(solution)/shard_map/ppermute | solution.py:692
  12.6 0.4 collective-permute-start.2
  13.1 0.2 collective-permute-start.3
  13.3 5.3 %local_fluxes.1.rows_in = f32[6144,128]{1,0:T(8,128)S(1)} custom-call(s32[1024]{0:T(1024)S(1)} %get-tuple-element.41.from_ref, s32[1024]{0:T(1024)S(1)} %get-tuple-element.40.to_ref, s32[5,512]{1,0:T(8,128)S(1)} %copy-done.6, f32[9216,128]{1,0:T(8,128)S(1)} %get-tuple-element.12.table_ref), custom_call_target="tpu_custom_call" | custom-call | flops 10000000 | bytes 12000000 | tf_op jit(solution)/shard_map/local_fluxes/pallas_call | solution.py:334
  18.7 7.5 %shard_map.140 = (f32[2,8,8,8,512]{4,3,2,1,0:T(8,128)S(1)}, f32[16,256]{1,0:T(8,128)S(1)}) custom-call(f32[2,8,8,8,512]{4,3,2,1,0:T(8,128)S(1)} %copy-done, f32[2,8,8,8,512]{4,3,2,1,0:T(8,128)S(1)} %copy-done.2, f32[6,8,8,8,512]{4,3,2,1,0:T(8,128)S(1)} %copy-done.1, bf16[512,768]{1,0:T(8,128)(2,1)S(1)} %copy-done.4, bf16[256,1536]{1,0:T(8,128)(2,1)S(1)} %copy-done.3, ...), custom_call_target="tpu_custom_call" | custom-call | flops 1000000000 | bytes 13000000 | tf_op jit(solution)/shard_map/pallas_call | solution.py:431
  26.3 1.2 %collective-permute-start.5 = (f32[384,128]{1,0:T(8,128)S(1)}, f32[384,128]{1,0:T(8,128)S(1)}, u32[]{:S(2)}, u32[]{:S(2)}) collective-permute-start(f32[384,128]{1,0:T(8,128)S(1)} %get-tuple-element.30), channel_id=1, source_target_pairs={{0,28},{4,8},{8,4},{12,16},{16,12},{20,24},{24,20},{28,0},{1,29},{... | collective-permute-start | bytes 589832 | tf_op jit(solution)/shard_map/ppermute | solution.py:692
  27.6 0.0 copy-start.8
  27.6 1.5 %center_rows.1 = (f32[6144,128]{1,0:T(8,128)S(1)}, s32[640,128]{1,0:T(8,128)S(1)}) custom-call(s32[576]{0:T(1024)S(1)} %get-tuple-element.19.to_ref, s32[5,1,576]{2,1,0:T(1,128)S(1)} %copy-done.7, f32[1728,128]{1,0:T(8,128)S(1)} %get-tuple-element.11.own_ref, f32[192,128]{1,0:T(8,128)S(1)} %get-tuple-element.37.up_ref, ...), custom_call_target="tpu_custom_call", output_to_operand_aliasing={{0}: (7, {})} | custom-call | flops 10000000 | bytes 1000000 | tf_op jit(solution)/shard_map/center_rows/pallas_call | solution.py:461
  29.1 7.6 %collective-permute-done.5 = f32[384,128]{1,0:T(8,128)S(1)} collective-permute-done((f32[384,128]{1,0:T(8,128)S(1)}, f32[384,128]{1,0:T(8,128)S(1)}, u32[]{:S(2)}, u32[]{:S(2)}) %collective-permute-start.5) | collective-permute-done | bytes 196640 | tf_op jit(solution)/shard_map/ppermute | solution.py:692
  36.8 2.6 %collective-permute-done.4 = f32[384,128]{1,0:T(8,128)S(1)} collective-permute-done((f32[384,128]{1,0:T(8,128)S(1)}, f32[384,128]{1,0:T(8,128)S(1)}, u32[]{:S(2)}, u32[]{:S(2)}) %collective-permute-start.4) | collective-permute-done | bytes 196640 | tf_op jit(solution)/shard_map/ppermute | solution.py:690
  39.4 3.0 %cross_sums.1 = (f32[6144,128]{1,0:T(8,128)S(1)}, f32[16,256]{1,0:T(8,128)S(1)}) custom-call(s32[576]{0:T(1024)S(1)} %get-tuple-element.19.to_ref, s32[640,128]{1,0:T(8,128)S(1)} %get-tuple-element.13.order, f32[1728,128]{1,0:T(8,128)S(1)} %get-tuple-element.11.own_ref, f32[384,128]{1,0:T(8,128)S(1)} %get-tuple-element.29.far_up, ...), custom_call_target="tpu_custom_call", output_to_operand_aliasing={{0}: (5, {})} | custom-call | flops 100000000 | bytes 4000000 | tf_op jit(solution)/shard_map/cross_sums/pallas_call | solution.py:507
  42.4 1.2 %collective-permute-done.6 = f32[16,256]{1,0:T(8,128)S(1)} collective-permute-done((f32[16,256]{1,0:T(8,128)S(1)}, f32[16,256]{1,0:T(8,128)S(1)}, u32[]{:S(2)}, u32[]{:S(2)}) %collective-permute-start.6) | collective-permute-done | bytes 16416 | tf_op jit(solution)/shard_map/ppermute | solution.py:758
  43.6 0.9 %collective-permute-start.7 = (f32[16,256]{1,0:T(8,128)S(1)}, f32[16,256]{1,0:T(8,128)S(1)}, u32[]{:S(2)}, u32[]{:S(2)}) collective-permute-start(f32[16,256]{1,0:T(8,128)S(1)} %add.30.refs_0_), channel_id=1, source_target_pairs={{0,2},{1,3},{2,0},{3,1},{4,6},{5,7},{6,4},{7,5},{8,10},{9,11},{10,... | collective-permute-start | bytes 49160 | tf_op jit(solution)/shard_map/ppermute | solution.py:761
  44.5 1.8 %shard_map.141.refs_0_ = f32[2,8,8,8,512]{4,3,2,1,0:T(8,128)} custom-call(f32[2,8,8,8,512]{4,3,2,1,0:T(8,128)S(1)} %get-tuple-element.10.start_ref, f32[6144,128]{1,0:T(8,128)S(1)} %get-tuple-element.16.rows_ref), custom_call_target="tpu_custom_call" | custom-call | flops 100000000 | bytes 9000000 | tf_op jit(solution)/shard_map/pallas_call | solution.py:568
  46.3 1.8 %shard_map.142 = f32[2,8,8,8,512]{4,3,2,1,0:T(8,128)} custom-call(f32[2,8,8,8,512]{4,3,2,1,0:T(8,128)S(1)} %get-tuple-element.10.start_ref, f32[6144,128]{1,0:T(8,128)S(1)} %get-tuple-element.16.rows_ref, f32[2,8,8,8,512]{4,3,2,1,0:T(8,128)} %shard_map.141.refs_0_), custom_call_target="tpu_custom_call", output_to_operand_aliasing={{}: (2, {})} | custom-call | flops 100000000 | bytes 9000000 | tf_op jit(solution)/shard_map/pallas_call | solution.py:568
  48.1 2.1 %correct.1 = f32[2,8,8,8,512]{4,3,2,1,0:T(8,128)} custom-call(f32[2,8,8,8,512]{4,3,2,1,0:T(8,128)S(1)} %copy-done, f32[8,8,256]{2,1,0:T(8,128)S(1)} %copy-done.5, s32[1,512]{1,0:T(1,128)S(1)} %bitcast.7, f32[16,256]{1,0:T(8,128)S(1)} %add.30.refs_0_, f32[16,256]{1,0:T(8,128)S(1)} %collective-permute-done.7.refs_1_), custom_call_target="tpu_custom_call" | custom-call | flops 100000000 | bytes 5000000 | tf_op jit(solution)/shard_map/correct/pallas_call | solution.py:653
  (32 shorter events, 0.3 us)
Async XLA Ops:
  1.4 17.2 %copy-start.3 = (bf16[256,1536]{1,0:T(8,128)(2,1)S(1)}, bf16[256,1536]{1,0:T(8,128)(2,1)}, u32[]{:S(2)}) copy-start(bf16[256,1536]{1,0:T(8,128)(2,1)} %constant.56.back_ref) | copy-start | bytes 2359300
  1.4 17.2 %copy-start.4 = (bf16[512,768]{1,0:T(8,128)(2,1)S(1)}, bf16[512,768]{1,0:T(8,128)(2,1)}, u32[]{:S(2)}) copy-start(bf16[512,768]{1,0:T(8,128)(2,1)} %constant.47.fwd_ref) | copy-start | bytes 2359300
  5.9 7.4 %copy-start.6 = (s32[5,512]{1,0:T(8,128)S(1)}, s32[5,512]{1,0:T(8,128)}, u32[]{:S(2)}) copy-start(s32[5,512]{1,0:T(8,128)} %code_ref.1) | copy-start | bytes 30724
  5.9 12.7 %copy-start.2 = (f32[2,8,8,8,512]{4,3,2,1,0:T(8,128)S(1)}, f32[2,8,8,8,512]{4,3,2,1,0:T(8,128)}, u32[]{:S(2)}) copy-start(f32[2,8,8,8,512]{4,3,2,1,0:T(8,128)} %rs_ref.1) | copy-start | bytes 6291460
  6.0 21.5 %collective-permute-start = (f32[192,128]{1,0:T(8,128)S(1)}, f32[192,128]{1,0:T(8,128)S(1)}, u32[]{:S(2)}, u32[]{:S(2)}) collective-permute-start(f32[192,128]{1,0:T(8,128)S(1)} %get-tuple-element.26), channel_id=1, source_target_pairs={{0,4},{4,0},{8,12},{12,8},{16,20},{20,16},{24,28},{28,24},{1,5},{5... | collective-permute-start | bytes 294920 | tf_op jit(solution)/shard_map/ppermute | solution.py:690
  9.0 18.5 %collective-permute-start.1 = (f32[192,128]{1,0:T(8,128)S(1)}, f32[192,128]{1,0:T(8,128)S(1)}, u32[]{:S(2)}, u32[]{:S(2)}) collective-permute-start(f32[192,128]{1,0:T(8,128)S(1)} %get-tuple-element.27), channel_id=1, source_target_pairs={{0,28},{4,8},{8,4},{12,16},{16,12},{20,24},{24,20},{28,0},{1,29},{... | collective-permute-start | bytes 294920 | tf_op jit(solution)/shard_map/ppermute | solution.py:692
  12.6 13.5 %collective-permute-start.2 = (f32[576,128]{1,0:T(8,128)S(1)}, f32[576,128]{1,0:T(8,128)S(1)}, u32[]{:S(2)}, u32[]{:S(2)}) collective-permute-start(f32[576,128]{1,0:T(8,128)S(1)} %pad_maximum_fusion), channel_id=1, source_target_pairs={{1,0},{2,1},{3,2},{0,3},{5,4},{6,5},{7,6},{4,7},{9,8},{10,9},{11,1... | collective-permute-start | bytes 884744 | tf_op jit(solution)/shard_map/ppermute | solution.py:683
  13.0 5.6 %copy-start.1 = (f32[6,8,8,8,512]{4,3,2,1,0:T(8,128)S(1)}, f32[6,8,8,8,512]{4,3,2,1,0:T(8,128)}, u32[]{:S(2)}) copy-start(f32[6,8,8,8,512]{4,3,2,1,0:T(8,128)} %g_ref.1) | copy-start | bytes 18874372
  13.1 13.2 %collective-permute-start.3 = (f32[576,128]{1,0:T(8,128)S(1)}, f32[576,128]{1,0:T(8,128)S(1)}, u32[]{:S(2)}, u32[]{:S(2)}) collective-permute-start(f32[576,128]{1,0:T(8,128)S(1)} %pad_maximum_fusion.1), channel_id=1, source_target_pairs={{3,0},{0,1},{1,2},{2,3},{7,4},{4,5},{5,6},{6,7},{11,8},{8,9},{9,10... | collective-permute-start | bytes 884744 | tf_op jit(solution)/shard_map/ppermute | solution.py:683
  13.3 5.4 %copy-start = (f32[2,8,8,8,512]{4,3,2,1,0:T(8,128)S(1)}, f32[2,8,8,8,512]{4,3,2,1,0:T(8,128)}, u32[]{:S(2)}) copy-start(f32[2,8,8,8,512]{4,3,2,1,0:T(8,128)} %p_ref.5) | copy-start | bytes 6291460
  13.3 5.4 %copy-start.9 = (s32[512]{0:T(512)S(1)}, s32[512]{0:T(512)}, u32[]{:S(2)}) copy-start(s32[512]{0:T(512)} %param.20) | copy-start | bytes 6148
  18.7 8.9 %copy-start.7 = (s32[5,1,576]{2,1,0:T(1,128)S(1)}, s32[5,1,576]{2,1,0:T(1,128)}, u32[]{:S(2)}) copy-start(s32[5,1,576]{2,1,0:T(1,128)} %slots_ref.1) | copy-start | bytes 34564
  26.3 10.5 %collective-permute-start.5 = (f32[384,128]{1,0:T(8,128)S(1)}, f32[384,128]{1,0:T(8,128)S(1)}, u32[]{:S(2)}, u32[]{:S(2)}) collective-permute-start(f32[384,128]{1,0:T(8,128)S(1)} %get-tuple-element.30), channel_id=1, source_target_pairs={{0,28},{4,8},{8,4},{12,16},{16,12},{20,24},{24,20},{28,0},{1,29},{... | collective-permute-start | bytes 589832 | tf_op jit(solution)/shard_map/ppermute | solution.py:692
  27.5 11.9 %collective-permute-start.4 = (f32[384,128]{1,0:T(8,128)S(1)}, f32[384,128]{1,0:T(8,128)S(1)}, u32[]{:S(2)}, u32[]{:S(2)}) collective-permute-start(f32[384,128]{1,0:T(8,128)S(1)} %get-tuple-element.31), channel_id=1, source_target_pairs={{0,4},{4,0},{8,12},{12,8},{16,20},{20,16},{24,28},{28,24},{1,5},{5... | collective-permute-start | bytes 589832 | tf_op jit(solution)/shard_map/ppermute | solution.py:690
  27.6 11.9 %copy-start.8 = (bf16[16,768]{1,0:T(8,128)(2,1)S(1)}, bf16[16,768]{1,0:T(8,128)(2,1)}, u32[]{:S(2)}) copy-start(bf16[16,768]{1,0:T(8,128)(2,1)} %constant.61.table_ref) | copy-start | bytes 73732
  42.4 1.2 %collective-permute-start.6 = (f32[16,256]{1,0:T(8,128)S(1)}, f32[16,256]{1,0:T(8,128)S(1)}, u32[]{:S(2)}, u32[]{:S(2)}) collective-permute-start(f32[16,256]{1,0:T(8,128)S(1)} %get-tuple-element.17), channel_id=1, source_target_pairs={{0,1},{1,0},{2,3},{3,2},{4,5},{5,4},{6,7},{7,6},{8,9},{9,8},{10,11... | collective-permute-start | bytes 49160 | tf_op jit(solution)/shard_map/ppermute | solution.py:758
  43.6 4.4 %collective-permute-start.7 = (f32[16,256]{1,0:T(8,128)S(1)}, f32[16,256]{1,0:T(8,128)S(1)}, u32[]{:S(2)}, u32[]{:S(2)}) collective-permute-start(f32[16,256]{1,0:T(8,128)S(1)} %add.30.refs_0_), channel_id=1, source_target_pairs={{0,2},{1,3},{2,0},{3,1},{4,6},{5,7},{6,4},{7,5},{8,10},{9,11},{10,... | collective-permute-start | bytes 49160 | tf_op jit(solution)/shard_map/ppermute | solution.py:761
  46.3 1.8 %copy-start.5 = (f32[8,8,256]{2,1,0:T(8,128)S(1)}, f32[8,8,256]{2,1,0:T(8,128)}, u32[]{:S(2)}) copy-start(f32[8,8,256]{2,1,0:T(8,128)} %inverse_ref.1) | copy-start | bytes 196612

commit v4 on v3

--- a/solution.py
+++ b/solution.py
@@ -96,14 +96,15 @@
     return lax.dot_general(left, right, dims, preferred_element_type=jnp.float32)
 
 
-def trace_kernel(rows_ref, p_ref, fw_ref, fm_ref, table, send_ref, nat, *, derivative, elems):
+def trace_kernel(rows_ref, *refs, derivative, elems):
+    p_refs, (fw_ref, fm_ref, table, send_ref, nat) = refs[:-5], refs[-5:]
     step = pl.program_id(0)
     steps = pl.num_programs(0)
-    fields, nodes = p_ref.shape[0], p_ref.shape[1]
+    fields, nodes = len(p_refs), p_refs[0].shape[1]
     pieces_total = fields + 1
     face_size = nodes * nodes
     last = nodes - 1
-    flat = p_ref.reshape(fields * nodes * nodes * nodes, LANES)
+    flats = [ref.reshape(nodes * nodes * nodes, LANES) for ref in p_refs]
     base = step * LANES
     low = [-derivative[0, k] for k in range(nodes)]
     high = [derivative[last, k] for k in range(nodes)]
@@ -118,12 +119,12 @@
         for axis in range(3):
             for at in range(nodes):
                 if axis == 0:
-                    terms = [p_ref[f, k, at] for k in range(nodes)]
+                    terms = [p_refs[f][0, k, at] for k in range(nodes)]
                 elif axis == 1:
-                    terms = [p_ref[f, at, k] for k in range(nodes)]
+                    terms = [p_refs[f][0, at, k] for k in range(nodes)]
                 else:
-                    first = (f * nodes + at) * nodes * nodes
-                    terms = [flat[pl.ds(first + k, nodes, stride=nodes), :] for k in range(nodes)]
+                    first = at * nodes * nodes
+                    terms = [flats[f][pl.ds(first + k, nodes, stride=nodes), :] for k in range(nodes)]
                 rows = slice(at * nodes, (at + 1) * nodes)
                 more = slice(face_size + at * nodes, face_size + (at + 1) * nodes)
                 nat[f, 2 * axis, rows] = terms[0]
@@ -162,16 +163,17 @@
         grid=(elems // LANES,),
         in_specs=[
             pl.BlockSpec(memory_space=pltpu.SMEM),
-            pl.BlockSpec((fields, nodes, nodes, nodes, LANES), lambda s: (0, 0, 0, 0, s)),
-            face_spec,
-            face_spec,
-        ],
+        ]
+        + [
+            pl.BlockSpec((1, nodes, nodes, nodes, LANES), lambda s, f=f: (f, 0, 0, 0, s)) for f in range(fields)
+        ]
+        + [face_spec, face_spec],
         out_specs=(whole, whole),
         scratch_shapes=[pltpu.VMEM((fields, 6, 2 * face_size, LANES), jnp.float32)],
         compiler_params=pltpu.CompilerParams(vmem_limit_bytes=6 * MIB),
         cost_estimate=pl.CostEstimate(flops=10**7, bytes_accessed=9 * 10**6, transcendentals=0),
         name="traces",
-    )(rows, pressure, face_weight, face_metric)
+    )(rows, *[pressure] * fields, face_weight, face_metric)
 
 
 def flux_rows(own, other, order, fields, nodes):
@@ -756,10 +758,11 @@
         )
         if sub_count == 4 and steps > 1:
             other = lax.ppermute(sums, "sub", [(at, at ^ 1) for at in range(sub_count)])
-            residual = lift(start, rows, derivative, 0, steps // 2)
+            first = max(1, steps // 4)
+            residual = lift(start, rows, derivative, 0, first)
             sums = sums + other
             other = lax.ppermute(sums, "sub", [(at, at ^ 2) for at in range(sub_count)])
-            residual = lift(start, rows, derivative, steps // 2, steps - steps // 2, (residual,))
+            residual = lift(start, rows, derivative, first, steps - first, (residual,))
             all_sums = [sums, other]
         else:
             all_sums = [sums] + [swap(sums, "sub", step) for step in range(1, sub_count)]

time: 50.4 us -> 50.7 us (level)
  no operation moved by 1% of the time
where the time goes in v4:
time: 50.7 us; the launch traced here: 50.4 us
  Pallas kernels  27.7 us (55%)
  waiting for transfers between devices  11.5 us (23%)
  starting transfers between devices  9.34 us (18%)
  other arithmetic  0.92 us (2%)
  between operations  0.88 us (2%)
    ppermute x2, waiting for transfers between devices, both_ways(): two = lax.ppermute(jnp.where(even, to_last, to_next), axis, pairs)  7.62 us
    pallas_call x1, Pallas kernels, volume(): pl.pallas_call(functools.partial(volume_kernel, derivative=derivative, ra...  7.48 us
    pallas_call x1, Pallas kernels, local_fluxes(): pl.pallas_call(functools.partial(local_kernel, fields=fields, nodes=nodes...  5.29 us
    ppermute x2, starting transfers between devices, both_ways(): two = lax.ppermute(jnp.where(even, to_last, to_next), axis, pairs)  4.79 us
    pallas_call x1, Pallas kernels, traces(): pl.pallas_call(functools.partial(trace_kernel, derivative=derivative, ele...  4.47 us
    pallas_call x2, Pallas kernels, lift(): pl.pallas_call(functools.partial(lift_kernel, derivative=derivative, elem...  3.83 us
    ppermute x2, starting transfers between devices, both_ways(): lax.ppermute(jnp.where(even, to_next, to_last), axis, [(at, at ^ 1) for a...  3.06 us
    pallas_call x1, Pallas kernels, cross_sums(): pl.pallas_call(functools.partial(cross_kernel, elems=elems, fields=fields...  2.97 us
  transfers between devices with their start and end apart: 8, of which 3 were waited for; matrix products, arithmetic and copies ran while one was open for 0% of the time, Pallas kernels for 36%

profile of v4, /device:TPU:0, one launch (start us, length us, event | category | flops | bytes accessed | tf_op | source)
XLA Modules:
  0.0 50.4 jit_solution(8639553022280209972)
XLA Ops:
  0.6 0.7 %multiply_reduce_fusion = (s32[576]{0:T(1024)S(1)}, s32[576]{0:T(1024)S(1)}) fusion(s32[5,1,576]{2,1,0:T(1,128)} %slots_ref.1), kind=kLoop, calls=%fused_computation.15 | loop fusion | flops 2304 | bytes 9216 | tf_op jit(solution)/shard_map/mul | solution.py:720
  1.4 0.0 copy-start.3
  1.4 0.0 copy-start.4
  1.4 4.5 %traces.1 = (f32[9216,128]{1,0:T(8,128)S(1)}, f32[1728,128]{1,0:T(8,128)S(1)}) custom-call(s32[576]{0:T(1024)S(1)} %get-tuple-element.18.rows_ref, f32[2,8,8,8,512]{4,3,2,1,0:T(8,128)} %p_ref.3, f32[2,8,8,8,512]{4,3,2,1,0:T(8,128)} %p_ref.3, f32[6,64,512]{2,1,0:T(8,128)} %bitcast.8, f32[6,64,512]{2,1,0:T(8,128)} %bitcast.9), custom_call_target="tpu_custom_call" | custom-call | flops 10000000 | bytes 9000000 | tf_op jit(solution)/shard_map/traces/pallas_call | solution.py:157
  5.9 0.0 copy-start.6
  5.9 0.0 copy-start.2
  5.9 0.1 fusion.4
  6.0 3.1 %collective-permute-start = (f32[192,128]{1,0:T(8,128)S(1)}, f32[192,128]{1,0:T(8,128)S(1)}, u32[]{:S(2)}, u32[]{:S(2)}) collective-permute-start(f32[192,128]{1,0:T(8,128)S(1)} %get-tuple-element.26), channel_id=1, source_target_pairs={{0,4},{4,0},{8,12},{12,8},{16,20},{20,16},{24,28},{28,24},{1,5},{5... | collective-permute-start | bytes 294920 | tf_op jit(solution)/shard_map/ppermute | solution.py:692
  9.0 3.5 %collective-permute-start.1 = (f32[192,128]{1,0:T(8,128)S(1)}, f32[192,128]{1,0:T(8,128)S(1)}, u32[]{:S(2)}, u32[]{:S(2)}) collective-permute-start(f32[192,128]{1,0:T(8,128)S(1)} %get-tuple-element.27), channel_id=1, source_target_pairs={{0,28},{4,8},{8,4},{12,16},{16,12},{20,24},{24,20},{28,0},{1,29},{... | collective-permute-start | bytes 294920 | tf_op jit(solution)/shard_map/ppermute | solution.py:694
  12.6 0.4 collective-permute-start.2
  13.0 0.2 collective-permute-start.3
  13.3 5.3 %local_fluxes.1.rows_in = f32[6144,128]{1,0:T(8,128)S(1)} custom-call(s32[1024]{0:T(1024)S(1)} %get-tuple-element.41.from_ref, s32[1024]{0:T(1024)S(1)} %get-tuple-element.40.to_ref, s32[5,512]{1,0:T(8,128)S(1)} %copy-done.6, f32[9216,128]{1,0:T(8,128)S(1)} %get-tuple-element.12.table_ref), custom_call_target="tpu_custom_call" | custom-call | flops 10000000 | bytes 12000000 | tf_op jit(solution)/shard_map/local_fluxes/pallas_call | solution.py:336
  18.6 7.5 %shard_map.140 = (f32[2,8,8,8,512]{4,3,2,1,0:T(8,128)S(1)}, f32[16,256]{1,0:T(8,128)S(1)}) custom-call(f32[2,8,8,8,512]{4,3,2,1,0:T(8,128)S(1)} %copy-done, f32[2,8,8,8,512]{4,3,2,1,0:T(8,128)S(1)} %copy-done.2, f32[6,8,8,8,512]{4,3,2,1,0:T(8,128)S(1)} %copy-done.1, bf16[512,768]{1,0:T(8,128)(2,1)S(1)} %copy-done.4, bf16[256,1536]{1,0:T(8,128)(2,1)S(1)} %copy-done.3, ...), custom_call_target="tpu_custom_call" | custom-call | flops 1000000000 | bytes 13000000 | tf_op jit(solution)/shard_map/pallas_call | solution.py:433
  26.3 1.2 %collective-permute-start.5 = (f32[384,128]{1,0:T(8,128)S(1)}, f32[384,128]{1,0:T(8,128)S(1)}, u32[]{:S(2)}, u32[]{:S(2)}) collective-permute-start(f32[384,128]{1,0:T(8,128)S(1)} %get-tuple-element.30), channel_id=1, source_target_pairs={{0,28},{4,8},{8,4},{12,16},{16,12},{20,24},{24,20},{28,0},{1,29},{... | collective-permute-start | bytes 589832 | tf_op jit(solution)/shard_map/ppermute | solution.py:694
  27.5 0.0 copy-start.8
  27.6 1.5 %center_rows.1 = (f32[6144,128]{1,0:T(8,128)S(1)}, s32[640,128]{1,0:T(8,128)S(1)}) custom-call(s32[576]{0:T(1024)S(1)} %get-tuple-element.19.to_ref, s32[5,1,576]{2,1,0:T(1,128)S(1)} %copy-done.7, f32[1728,128]{1,0:T(8,128)S(1)} %get-tuple-element.11.own_ref, f32[192,128]{1,0:T(8,128)S(1)} %get-tuple-element.37.up_ref, ...), custom_call_target="tpu_custom_call", output_to_operand_aliasing={{0}: (7, {})} | custom-call | flops 10000000 | bytes 1000000 | tf_op jit(solution)/shard_map/center_rows/pallas_call | solution.py:463
  29.1 7.6 %collective-permute-done.5 = f32[384,128]{1,0:T(8,128)S(1)} collective-permute-done((f32[384,128]{1,0:T(8,128)S(1)}, f32[384,128]{1,0:T(8,128)S(1)}, u32[]{:S(2)}, u32[]{:S(2)}) %collective-permute-start.5) | collective-permute-done | bytes 196640 | tf_op jit(solution)/shard_map/ppermute | solution.py:694
  36.7 2.6 %collective-permute-done.4 = f32[384,128]{1,0:T(8,128)S(1)} collective-permute-done((f32[384,128]{1,0:T(8,128)S(1)}, f32[384,128]{1,0:T(8,128)S(1)}, u32[]{:S(2)}, u32[]{:S(2)}) %collective-permute-start.4) | collective-permute-done | bytes 196640 | tf_op jit(solution)/shard_map/ppermute | solution.py:692
  39.4 3.0 %cross_sums.1 = (f32[6144,128]{1,0:T(8,128)S(1)}, f32[16,256]{1,0:T(8,128)S(1)}) custom-call(s32[576]{0:T(1024)S(1)} %get-tuple-element.19.to_ref, s32[640,128]{1,0:T(8,128)S(1)} %get-tuple-element.13.order, f32[1728,128]{1,0:T(8,128)S(1)} %get-tuple-element.11.own_ref, f32[384,128]{1,0:T(8,128)S(1)} %get-tuple-element.29.far_up, ...), custom_call_target="tpu_custom_call", output_to_operand_aliasing={{0}: (5, {})} | custom-call | flops 100000000 | bytes 4000000 | tf_op jit(solution)/shard_map/cross_sums/pallas_call | solution.py:509
  42.4 1.2 %collective-permute-done.6 = f32[16,256]{1,0:T(8,128)S(1)} collective-permute-done((f32[16,256]{1,0:T(8,128)S(1)}, f32[16,256]{1,0:T(8,128)S(1)}, u32[]{:S(2)}, u32[]{:S(2)}) %collective-permute-start.6) | collective-permute-done | bytes 16416 | tf_op jit(solution)/shard_map/ppermute | solution.py:760
  43.6 0.9 %collective-permute-start.7 = (f32[16,256]{1,0:T(8,128)S(1)}, f32[16,256]{1,0:T(8,128)S(1)}, u32[]{:S(2)}, u32[]{:S(2)}) collective-permute-start(f32[16,256]{1,0:T(8,128)S(1)} %add.30.refs_0_), channel_id=1, source_target_pairs={{0,2},{1,3},{2,0},{3,1},{4,6},{5,7},{6,4},{7,5},{8,10},{9,11},{10,... | collective-permute-start | bytes 49160 | tf_op jit(solution)/shard_map/ppermute | solution.py:764
  44.5 1.3 %shard_map.141.refs_0_ = f32[2,8,8,8,512]{4,3,2,1,0:T(8,128)} custom-call(f32[2,8,8,8,512]{4,3,2,1,0:T(8,128)S(1)} %get-tuple-element.10.start_ref, f32[6144,128]{1,0:T(8,128)S(1)} %get-tuple-element.16.rows_ref), custom_call_target="tpu_custom_call" | custom-call | flops 100000000 | bytes 9000000 | tf_op jit(solution)/shard_map/pallas_call | solution.py:570
  45.8 2.6 %shard_map.142 = f32[2,8,8,8,512]{4,3,2,1,0:T(8,128)} custom-call(f32[2,8,8,8,512]{4,3,2,1,0:T(8,128)S(1)} %get-tuple-element.10.start_ref, f32[6144,128]{1,0:T(8,128)S(1)} %get-tuple-element.16.rows_ref, f32[2,8,8,8,512]{4,3,2,1,0:T(8,128)} %shard_map.141.refs_0_), custom_call_target="tpu_custom_call", output_to_operand_aliasing={{}: (2, {})} | custom-call | flops 100000000 | bytes 9000000 | tf_op jit(solution)/shard_map/pallas_call | solution.py:570
  48.3 2.1 %correct.1 = f32[2,8,8,8,512]{4,3,2,1,0:T(8,128)} custom-call(f32[2,8,8,8,512]{4,3,2,1,0:T(8,128)S(1)} %copy-done, f32[8,8,256]{2,1,0:T(8,128)S(1)} %copy-done.5, s32[1,512]{1,0:T(1,128)S(1)} %bitcast.7, f32[16,256]{1,0:T(8,128)S(1)} %add.30.refs_0_, f32[16,256]{1,0:T(8,128)S(1)} %collective-permute-done.7.refs_1_), custom_call_target="tpu_custom_call" | custom-call | flops 100000000 | bytes 5000000 | tf_op jit(solution)/shard_map/correct/pallas_call | solution.py:655
  (32 shorter events, 0.3 us)
Async XLA Ops:
  1.4 17.2 %copy-start.3 = (bf16[256,1536]{1,0:T(8,128)(2,1)S(1)}, bf16[256,1536]{1,0:T(8,128)(2,1)}, u32[]{:S(2)}) copy-start(bf16[256,1536]{1,0:T(8,128)(2,1)} %constant.56.back_ref) | copy-start | bytes 2359300
  1.4 17.2 %copy-start.4 = (bf16[512,768]{1,0:T(8,128)(2,1)S(1)}, bf16[512,768]{1,0:T(8,128)(2,1)}, u32[]{:S(2)}) copy-start(bf16[512,768]{1,0:T(8,128)(2,1)} %constant.47.fwd_ref) | copy-start | bytes 2359300
  5.9 7.4 %copy-start.6 = (s32[5,512]{1,0:T(8,128)S(1)}, s32[5,512]{1,0:T(8,128)}, u32[]{:S(2)}) copy-start(s32[5,512]{1,0:T(8,128)} %code_ref.1) | copy-start | bytes 30724
  5.9 12.7 %copy-start.2 = (f32[2,8,8,8,512]{4,3,2,1,0:T(8,128)S(1)}, f32[2,8,8,8,512]{4,3,2,1,0:T(8,128)}, u32[]{:S(2)}) copy-start(f32[2,8,8,8,512]{4,3,2,1,0:T(8,128)} %rs_ref.1) | copy-start | bytes 6291460
  6.0 21.6 %collective-permute-start = (f32[192,128]{1,0:T(8,128)S(1)}, f32[192,128]{1,0:T(8,128)S(1)}, u32[]{:S(2)}, u32[]{:S(2)}) collective-permute-start(f32[192,128]{1,0:T(8,128)S(1)} %get-tuple-element.26), channel_id=1, source_target_pairs={{0,4},{4,0},{8,12},{12,8},{16,20},{20,16},{24,28},{28,24},{1,5},{5... | collective-permute-start | bytes 294920 | tf_op jit(solution)/shard_map/ppermute | solution.py:692
  9.0 18.5 %collective-permute-start.1 = (f32[192,128]{1,0:T(8,128)S(1)}, f32[192,128]{1,0:T(8,128)S(1)}, u32[]{:S(2)}, u32[]{:S(2)}) collective-permute-start(f32[192,128]{1,0:T(8,128)S(1)} %get-tuple-element.27), channel_id=1, source_target_pairs={{0,28},{4,8},{8,4},{12,16},{16,12},{20,24},{24,20},{28,0},{1,29},{... | collective-permute-start | bytes 294920 | tf_op jit(solution)/shard_map/ppermute | solution.py:694
  12.6 13.5 %collective-permute-start.2 = (f32[576,128]{1,0:T(8,128)S(1)}, f32[576,128]{1,0:T(8,128)S(1)}, u32[]{:S(2)}, u32[]{:S(2)}) collective-permute-start(f32[576,128]{1,0:T(8,128)S(1)} %pad_maximum_fusion), channel_id=1, source_target_pairs={{1,0},{2,1},{3,2},{0,3},{5,4},{6,5},{7,6},{4,7},{9,8},{10,9},{11,1... | collective-permute-start | bytes 884744 | tf_op jit(solution)/shard_map/ppermute | solution.py:685
  13.0 5.6 %copy-start.1 = (f32[6,8,8,8,512]{4,3,2,1,0:T(8,128)S(1)}, f32[6,8,8,8,512]{4,3,2,1,0:T(8,128)}, u32[]{:S(2)}) copy-start(f32[6,8,8,8,512]{4,3,2,1,0:T(8,128)} %g_ref.1) | copy-start | bytes 18874372
  13.0 13.2 %collective-permute-start.3 = (f32[576,128]{1,0:T(8,128)S(1)}, f32[576,128]{1,0:T(8,128)S(1)}, u32[]{:S(2)}, u32[]{:S(2)}) collective-permute-start(f32[576,128]{1,0:T(8,128)S(1)} %pad_maximum_fusion.1), channel_id=1, source_target_pairs={{3,0},{0,1},{1,2},{2,3},{7,4},{4,5},{5,6},{6,7},{11,8},{8,9},{9,10... | collective-permute-start | bytes 884744 | tf_op jit(solution)/shard_map/ppermute | solution.py:685
  13.3 5.4 %copy-start = (f32[2,8,8,8,512]{4,3,2,1,0:T(8,128)S(1)}, f32[2,8,8,8,512]{4,3,2,1,0:T(8,128)}, u32[]{:S(2)}) copy-start(f32[2,8,8,8,512]{4,3,2,1,0:T(8,128)} %p_ref.3) | copy-start | bytes 6291460
  13.3 5.4 %copy-start.9 = (s32[512]{0:T(512)S(1)}, s32[512]{0:T(512)}, u32[]{:S(2)}) copy-start(s32[512]{0:T(512)} %param.20) | copy-start | bytes 6148
  18.6 8.9 %copy-start.7 = (s32[5,1,576]{2,1,0:T(1,128)S(1)}, s32[5,1,576]{2,1,0:T(1,128)}, u32[]{:S(2)}) copy-start(s32[5,1,576]{2,1,0:T(1,128)} %slots_ref.1) | copy-start | bytes 34564
  26.3 10.5 %collective-permute-start.5 = (f32[384,128]{1,0:T(8,128)S(1)}, f32[384,128]{1,0:T(8,128)S(1)}, u32[]{:S(2)}, u32[]{:S(2)}) collective-permute-start(f32[384,128]{1,0:T(8,128)S(1)} %get-tuple-element.30), channel_id=1, source_target_pairs={{0,28},{4,8},{8,4},{12,16},{16,12},{20,24},{24,20},{28,0},{1,29},{... | collective-permute-start | bytes 589832 | tf_op jit(solution)/shard_map/ppermute | solution.py:694
  27.5 11.9 %collective-permute-start.4 = (f32[384,128]{1,0:T(8,128)S(1)}, f32[384,128]{1,0:T(8,128)S(1)}, u32[]{:S(2)}, u32[]{:S(2)}) collective-permute-start(f32[384,128]{1,0:T(8,128)S(1)} %get-tuple-element.31), channel_id=1, source_target_pairs={{0,4},{4,0},{8,12},{12,8},{16,20},{20,16},{24,28},{28,24},{1,5},{5... | collective-permute-start | bytes 589832 | tf_op jit(solution)/shard_map/ppermute | solution.py:692
  27.5 11.9 %copy-start.8 = (bf16[16,768]{1,0:T(8,128)(2,1)S(1)}, bf16[16,768]{1,0:T(8,128)(2,1)}, u32[]{:S(2)}) copy-start(bf16[16,768]{1,0:T(8,128)(2,1)} %constant.61.table_ref) | copy-start | bytes 73732
  42.4 1.2 %collective-permute-start.6 = (f32[16,256]{1,0:T(8,128)S(1)}, f32[16,256]{1,0:T(8,128)S(1)}, u32[]{:S(2)}, u32[]{:S(2)}) collective-permute-start(f32[16,256]{1,0:T(8,128)S(1)} %get-tuple-element.17), channel_id=1, source_target_pairs={{0,1},{1,0},{2,3},{3,2},{4,5},{5,4},{6,7},{7,6},{8,9},{9,8},{10,11... | collective-permute-start | bytes 49160 | tf_op jit(solution)/shard_map/ppermute | solution.py:760
  43.6 4.7 %collective-permute-start.7 = (f32[16,256]{1,0:T(8,128)S(1)}, f32[16,256]{1,0:T(8,128)S(1)}, u32[]{:S(2)}, u32[]{:S(2)}) collective-permute-start(f32[16,256]{1,0:T(8,128)S(1)} %add.30.refs_0_), channel_id=1, source_target_pairs={{0,2},{1,3},{2,0},{3,1},{4,6},{5,7},{6,4},{7,5},{8,10},{9,11},{10,... | collective-permute-start | bytes 49160 | tf_op jit(solution)/shard_map/ppermute | solution.py:764
  45.8 2.6 %copy-start.5 = (f32[8,8,256]{2,1,0:T(8,128)S(1)}, f32[8,8,256]{2,1,0:T(8,128)}, u32[]{:S(2)}) copy-start(f32[8,8,256]{2,1,0:T(8,128)} %inverse_ref.1) | copy-start | bytes 196612
